TPU v7x, 256 devices: a whole 4x4x8 slice. The times are simulated.
256 devices in a mesh: sub: 32 (over x, z_hi, core), coarse: 8 (over z_lo, y).
Axes of the slice: x: 4, y: 4, z: 8 (z_hi: 4, z_lo: 2; z = z_hi * 2 + z_lo), core: 2. Of those that a mesh axis runs over, the one named last changes fastest.
Arguments:
- residual_parts: bfloat16 [32, 8, 4, 256, 512], P('sub', 'coarse'), may hold values from -6 to 6
- face_slot: int32 [32, 8, 4], P('sub', 'coarse'), may hold values from 0 to 3, each once within a row
- face_order: int32 [32, 8, 4, 512], P('sub', 'coarse'), may hold values from 0 to 511, each once within a row
- face_scale: float32 [32, 8, 4], P('sub', 'coarse'), may hold values from 0 to 1, as said below
- vertex_unknowns: int32 [32, 8, 256], P('sub', 'coarse'), may hold values from 0 to 2047, all different within a row
- front_inverse: bfloat16 [32, 8, 2048, 2048], P('sub', 'coarse')
- coarse_basis: bfloat16 [32, 8, 2048, 256], P('sub', 'coarse'), may hold values from -0.125 to 0.125
- coarse_inverse: bfloat16 [32, 2048, 2048], P('sub', None, 'coarse'), as said below
- thermal_handoff: bfloat16 [32, 2048, 128], P('sub'), may hold values from -0.125 to 0.125
- chain_transfer: float32 [32, 128, 128], P('sub')
- coupling_in: bfloat16 [32, 128, 2048], P('sub', None, 'coarse'), may hold values from -0.5 to 0.5
Outputs:
- correction: bfloat16 [32, 8, 4, 256, 512], P('sub', 'coarse')
Inputs may be any that keep to these rules, and one draw needn't show every extreme that they name: `face_slot`: each row is a permutation of 0 to 3. `face_order`: each row is a permutation of 0 to 511. `vertex_unknowns`: the 256 entries of each subdomain are distinct. `face_scale`: the two weights of a shared face sum to one; a face on the outer boundary has weight one. `coarse_inverse`: each line's matrix is symmetric.
All inputs are finite; a program needn't handle non-finite values.
Results may differ from a plain program's by a relative error of at most 0.0059.
Values may be sent and summed in bfloat16 or wider, within the bound.
No kernel may reach another device: no remote copies, remote signals or barrier semaphores. Data moves between devices by JAX's collectives and lax.ppermute only.
A program may use at most 128 MiB of HBM per device.

v0:
```python
import jax
import jax.numpy as jnp
from jax import lax
from jax.sharding import PartitionSpec as P

HIGHEST = lax.Precision.HIGHEST


def with_halo(block, sides, width):
    for axis, dim in sides:
        count = lax.axis_size(axis)
        forward = [(i, i + 1) for i in range(count - 1)]
        backward = [(target, source) for source, target in forward]
        low = lax.ppermute(
            lax.slice_in_dim(block, block.shape[dim] - width, None, axis=dim), axis, forward
        )
        high = lax.ppermute(lax.slice_in_dim(block, 0, width, axis=dim), axis, backward)
        block = jnp.concatenate([low, block, high], axis=dim)
    return block


def carried_in(array, axis, combine, identity):
    peers, mine = (lax.axis_size(axis), lax.axis_index(axis))
    everything = jax.tree.map(lambda part: lax.all_gather(part, axis), array)
    start = jax.tree.map(
        lambda part, zero: jnp.broadcast_to(jnp.asarray(zero, part.dtype), part.shape),
        array,
        identity,
    )

    def step(k, before):
        reached = k < mine
        new = combine(before, jax.tree.map(lambda part: part[k], everything))
        return jax.tree.map(lambda a, b: jnp.where(reached, a, b), new, before)

    return lax.fori_loop(0, peers, step, start)


def build_tables(face_slot, face_order, table_type):
    face_count, block_size = face_order.shape
    slot_table = (
        face_slot[:, None] == lax.broadcasted_iota(jnp.int32, (face_count, face_count), 1)
    ).astype(table_type)
    order_table = (
        face_order[:, :, None]
        == lax.broadcasted_iota(jnp.int32, (face_count, block_size, block_size), 2)
    ).astype(table_type)
    return (slot_table, order_table)


def to_canonical(values, tables):
    slot_table, order_table = tables
    ordered = jnp.einsum(
        "snk,sjk->snj", values, order_table, preferred_element_type=jnp.float32, precision=HIGHEST
    ).astype(values.dtype)
    return jnp.einsum(
        "ds,snj->dnj", slot_table, ordered, preferred_element_type=jnp.float32, precision=HIGHEST
    ).astype(values.dtype)


def from_canonical(values, tables):
    slot_table, order_table = tables
    by_face = jnp.einsum(
        "ds,dnj->snj", slot_table, values, preferred_element_type=jnp.float32, precision=HIGHEST
    ).astype(values.dtype)
    return jnp.einsum(
        "snj,sjk->snk", by_face, order_table, preferred_element_type=jnp.float32, precision=HIGHEST
    ).astype(values.dtype)


def trade_faces(face_values):
    along_sub = with_halo(face_values[0:2], (("sub", 0),), 1)
    along_coarse = with_halo(face_values[2:4], (("coarse", 0),), 1)
    return jnp.stack([along_sub[0], along_sub[3], along_coarse[0], along_coarse[3]], 0)


def per_device(
    residual_parts,
    face_slot,
    face_order,
    face_scale,
    vertex_unknowns,
    front_inverse,
    coarse_basis,
    coarse_inverse,
    thermal_handoff,
    chain_transfer,
    coupling_in,
):
    own_parts = residual_parts[0, 0]
    own_slot = face_slot[0, 0]
    own_order = face_order[0, 0]
    own_scale = face_scale[0, 0][:, None, None]
    face_count, sample_count, block_size = own_parts.shape
    reduced_precision_tables = build_tables(own_slot, own_order, jnp.bfloat16)
    canon = to_canonical(own_parts, reduced_precision_tables)
    beside = trade_faces(canon)
    averaged = (own_scale * (canon.astype(jnp.float32) + beside.astype(jnp.float32))).astype(
        jnp.bfloat16
    )
    local_residual = from_canonical(averaged, reduced_precision_tables)
    own_primal = vertex_unknowns[0, 0]
    positions = lax.broadcasted_iota(jnp.int32, (own_primal.shape[0], face_count * block_size), 1)
    hits = jnp.sum((own_primal[:, None] == positions).astype(jnp.int32), axis=0)
    dual_mask = (1 - hits).astype(jnp.bfloat16).reshape(face_count, 1, block_size)
    inverse_blocks = front_inverse[0, 0].reshape(face_count, block_size, face_count, block_size)
    dual_part = (
        jnp.einsum(
            "gnj,gjfk->fnk",
            local_residual * dual_mask,
            inverse_blocks,
            preferred_element_type=jnp.float32,
        )
        * dual_mask
    )
    basis_blocks = coarse_basis[0, 0].reshape(face_count, block_size, -1)
    coarse_residual = jnp.einsum(
        "gnj,gjc->nc", local_residual, basis_blocks, preferred_element_type=jnp.float32
    ).astype(jnp.bfloat16)
    primal_count = coarse_residual.shape[1]
    line_block = coarse_inverse[0]
    line_outflow = thermal_handoff[0]
    channel_count = line_outflow.shape[1]
    line_base = lax.dot_general(
        line_block,
        lax.all_gather(coarse_residual, "coarse", axis=1, tiled=True),
        (((0,), (1,)), ((), ())),
        preferred_element_type=jnp.float32,
    )
    own_rows = lax.dynamic_slice_in_dim(
        line_outflow, lax.axis_index("coarse") * primal_count, primal_count, 0
    )
    inflow = lax.psum(
        jnp.dot(coarse_residual, own_rows, preferred_element_type=jnp.float32), "coarse"
    )
    transfer = chain_transfer[0]

    def compose(earlier, later):
        joined_map = jnp.dot(earlier[0], later[0], precision=HIGHEST)
        joined_state = jnp.dot(earlier[1], later[0], precision=HIGHEST) + later[1]
        return (joined_map, joined_state)

    identity = (jnp.eye(channel_count, dtype=jnp.float32), jnp.zeros_like(inflow))
    upstream_map, carried = carried_in((transfer, inflow), "sub", compose, identity)
    carried_term = lax.dot_general(
        coupling_in[0].astype(jnp.float32), carried, (((0,), (1,)), ((), ())), precision=HIGHEST
    )
    global_coarse_answer = (line_base + carried_term).astype(jnp.bfloat16)
    subregion_iterate = dual_part + jnp.einsum(
        "cn,gjc->gnj", global_coarse_answer, basis_blocks, preferred_element_type=jnp.float32
    )
    exact_tables = build_tables(own_slot, own_order, jnp.float32)
    weighted = (own_scale * to_canonical(subregion_iterate, exact_tables)).astype(jnp.bfloat16)
    beside_again = trade_faces(weighted)
    summed = (weighted.astype(jnp.float32) + beside_again.astype(jnp.float32)).astype(jnp.bfloat16)
    return from_canonical(summed, reduced_precision_tables)[None, None]


def solution(mesh):
    placed = (
        P("sub", "coarse", None, None, None),
        P("sub", "coarse", None),
        P("sub", "coarse", None, None),
        P("sub", "coarse", None),
        P("sub", "coarse", None),
        P("sub", "coarse", None, None),
        P("sub", "coarse", None, None),
        P("sub", None, "coarse"),
        P("sub", None, None),
        P("sub", None, None),
        P("sub", None, "coarse"),
    )
    return jax.shard_map(
        per_device,
        mesh=mesh,
        in_specs=placed,
        out_specs=P("sub", "coarse", None, None, None),
        check_vma=False,
    )
```

profile of v0, /device:TPU:26, one launch (start us, length us, event | category | flops | bytes accessed | tf_op | source)
XLA Modules:
  0.0 419.8 jit_solution(5209459540740825076)
XLA Ops:
  6.5 2.4 fusion.30
  11.1 2.3 fusion.70
  13.4 1.9 collective-permute-start
  15.4 7.6 %collective-permute-start.1 = (bf16[1,256,512]{2,0,1:T(2,128)(2,1)}, bf16[1,256,512]{2,0,1:T(2,128)(2,1)}, u32[]{:S(2)}, u32[]{:S(2)}) collective-permute-start(bf16[1,256,512]{2,0,1:T(2,128)(2,1)} %get-tuple-element.150), channel_id=1, source_target_pairs={{8,0},{16,8},{24,16},{32,24},{40,32},{48,40},{56,48},{64,56},{72,6... | collective-permute-start | bytes 786440 | tf_op jit(solution)/shard_map/ppermute | solution.py:17
  23.0 2.6 collective-permute-start.2
  25.6 3.3 collective-permute-start.3
  28.8 5.6 %collective-permute-done = bf16[1,256,512]{2,0,1:T(2,128)(2,1)} collective-permute-done((bf16[1,256,512]{2,0,1:T(2,128)(2,1)}, bf16[1,256,512]{2,0,1:T(2,128)(2,1)}, u32[]{:S(2)}, u32[]{:S(2)}) %collective-permute-start) | collective-permute-done | bytes 262176 | tf_op jit(solution)/shard_map/ppermute | solution.py:14
  35.6 6.2 %collective-permute-done.2 = bf16[1,256,512]{2,0,1:T(2,128)(2,1)} collective-permute-done((bf16[1,256,512]{2,0,1:T(2,128)(2,1)S(1)}, bf16[1,256,512]{2,0,1:T(2,128)(2,1)}, u32[]{:S(2)}, u32[]{:S(2)}) %collective-permute-start.2) | collective-permute-done | bytes 262176 | tf_op jit(solution)/shard_map/ppermute | solution.py:14
  41.8 5.4 %collective-permute-done.3 = bf16[1,256,512]{2,0,1:T(2,128)(2,1)} collective-permute-done((bf16[1,256,512]{2,0,1:T(2,128)(2,1)S(1)}, bf16[1,256,512]{2,0,1:T(2,128)(2,1)}, u32[]{:S(2)}, u32[]{:S(2)}) %collective-permute-start.3) | collective-permute-done | bytes 262176 | tf_op jit(solution)/shard_map/ppermute | solution.py:17
  47.2 4.5 %convolution_convert_fusion.1 = bf16[4,256,512]{2,0,1:T(4,128)(2,1)S(1)} fusion(bf16[4,256,512]{2,0,1:T(4,128)(2,1)S(1)} %convolution_convert_fusion.2, bf16[1,256,512]{2,0,1:T(2,128)(2,1)} %collective-permute-done.3, bf16[1,256,512]{2,0,1:T(2,128)(2,1)} %collective-permute-done.2, bf16[1,256,512]{2,0,1:T(2,128)(2,1)} %collective-permute-done.1, ...), kind=kOutput, calls=%fused_computation.36 | convolution fusion | flops 11010064 | bytes 3145760 | tf_op jit(solution)/shard_map/ds,dnj->snj/dot_general | solution.py:63
  51.7 1.4 fusion.27
  54.5 1.7 convolution_bitcast_fusion.2
  57.9 75.5 %all-reduce.2.cloned.1.call-done = f32[1,256,128]{2,1,0:T(8,128)} async-done(((f32[1,256,128]{2,1,0:T(8,128)}), f32[1,256,128]{2,1,0:T(8,128)}) %all-reduce.2.cloned.1.call-update) | async-done | bytes 131088 | tf_op jit(solution)/shard_map/psum | solution.py:133
  133.9 14.5 %reshape_squeeze.6 = bf16[4,512,4,512]{3,2,1,0:T(4,128)(2,1)} reshape(bf16[1,1,2048,2048]{3,2,1,0:T(8,128)(2,1)} %param.18) | data formatting | bytes 16777216 | tf_op jit(solution)/shard_map/reshape;squeeze | solution.py:106
  148.4 6.5 %fusion.9 = f32[256,4,512,1]{2,0,3,1:T(8,128)S(1)} fusion(bf16[4,512,4,512]{3,2,1,0:T(4,128)(2,1)} %reshape_squeeze.6, bf16[4,256,512]{2,1,0:T(8,128)(2,1)} %copy-done.2, bf16[4,512]{1,0:T(4,128)(2,1)S(1)} %convert_element_type.89), kind=kOutput, calls=%fused_computation.11 | convolution fusion | flops 2149580800 | bytes 11538432 | tf_op jit(solution)/shard_map/gnj,gjfk->fnk/dot_general | solution.py:108
  155.0 22.1 %all-gather.4.cloned.1.call-done = bf16[256,2048]{1,0:T(8,128)(2,1)} async-done(((bf16[256,256]{1,0:T(8,128)(2,1)}), bf16[256,2048]{1,0:T(8,128)(2,1)}) %all-gather.4.cloned.1.call-update) | async-done | bytes 1048592 | tf_op jit(solution)/shard_map/all_gather | solution.py:126
  177.1 2.7 fusion.48
  179.8 54.5 %all-gather.6.cloned.1.call-done = f32[32,128,128]{2,1,0:T(8,128)} async-done(((f32[1,128,128]{2,1,0:T(8,128)}), f32[32,128,128]{2,1,0:T(8,128)}) %all-gather.6.cloned.1.call-update) | async-done | bytes 2097168 | tf_op jit(solution)/shard_map/all_gather | solution.py:24
  234.3 61.3 %all-gather.8.cloned.1.call-done = f32[32,256,128]{2,1,0:T(8,128)} async-done(((f32[1,256,128]{2,1,0:T(8,128)}), f32[32,256,128]{2,1,0:T(8,128)}) %all-gather.8.cloned.1.call-update) | async-done | bytes 4194320 | tf_op jit(solution)/shard_map/all_gather | solution.py:24
  295.6 71.3 %while.14 = (s32[]{:T(128)}, f32[256,128]{0,1:T(8,128)S(1)}, s32[]{:T(128)}, f32[32,128,128]{2,1,0:T(8,128)}, f32[32,256,128]{2,1,0:T(8,128)}, /*index=5*/s32[]{:T(128)}, s32[]{:T(128)}) while((s32[]{:T(128)}, f32[256,128]{0,1:T(8,128)S(1)}, s32[]{:T(128)}, f32[32,128,128]{2,1,0:T(8,128)}, f32[32,256,128]{2,1,0:T(8,128)}, ...), condition=%wide.region_3.4_spmd.clone, body=%wide.region_2.3_spmd.clone.sunk | while | flops 50462724 | bytes 1378403 | solution.py:36
  368.7 2.8 fusion.12
  371.5 3.3 multiply_convert_fusion
  374.8 1.6 fusion.69
  376.4 2.2 collective-permute-start.4
  378.6 6.4 %collective-permute-start.5 = (bf16[1,256,512]{2,0,1:T(2,128)(2,1)S(1)}, bf16[1,256,512]{2,0,1:T(2,128)(2,1)S(1)}, u32[]{:S(2)}, u32[]{:S(2)}) collective-permute-start(bf16[1,256,512]{2,0,1:T(2,128)(2,1)S(1)} %get-tuple-element.146), channel_id=1, source_target_pairs={{8,0},{16,8},{24,16},{32,24},{40,32},{48,40},{56,48},{64,56},{72,6... | collective-permute-start | bytes 786440 | tf_op jit(solution)/shard_map/ppermute | solution.py:17
  385.0 2.1 collective-permute-start.6
  387.1 3.7 collective-permute-start.7
  390.9 5.8 %collective-permute-done.4 = bf16[1,256,512]{2,0,1:T(2,128)(2,1)S(1)} collective-permute-done((bf16[1,256,512]{2,0,1:T(2,128)(2,1)S(1)}, bf16[1,256,512]{2,0,1:T(2,128)(2,1)S(1)}, u32[]{:S(2)}, u32[]{:S(2)}) %collective-permute-start.4) | collective-permute-done | bytes 262176 | tf_op jit(solution)/shard_map/ppermute | solution.py:14
  397.1 5.4 %collective-permute-done.6 = bf16[1,256,512]{2,0,1:T(2,128)(2,1)S(1)} collective-permute-done((bf16[1,256,512]{2,0,1:T(2,128)(2,1)S(1)}, bf16[1,256,512]{2,0,1:T(2,128)(2,1)S(1)}, u32[]{:S(2)}, u32[]{:S(2)}) %collective-permute-start.6) | collective-permute-done | bytes 262176 | tf_op jit(solution)/shard_map/ppermute | solution.py:14
  402.4 5.8 %collective-permute-done.7 = bf16[1,256,512]{2,0,1:T(2,128)(2,1)S(1)} collective-permute-done((bf16[1,256,512]{2,0,1:T(2,128)(2,1)S(1)}, bf16[1,256,512]{2,0,1:T(2,128)(2,1)S(1)}, u32[]{:S(2)}, u32[]{:S(2)}) %collective-permute-start.7) | collective-permute-done | bytes 262176 | tf_op jit(solution)/shard_map/ppermute | solution.py:17
  408.2 2.9 convolution_convert_fusion
  411.1 2.2 fusion.29
  (166 shorter events, 78.6 us)
Async XLA Ops:
  6.5 46.5 %copy-start = (bf16[1,1,2048,256]{3,2,1,0:T(8,128)(2,1)S(1)}, bf16[1,1,2048,256]{3,2,1,0:T(8,128)(2,1)}, u32[]{:S(2)}) copy-start(bf16[1,1,2048,256]{3,2,1,0:T(8,128)(2,1)} %param.19) | copy-start | bytes 3145732
  6.5 126.9 %all-reduce.2.cloned.1.call-start = ((), (), s32[]{:S(2)}) async-start(), calls=%async_computation.2 | async-start | bytes 262144 | tf_op jit(solution)/shard_map/psum | solution.py:133
  6.5 3.5 copy-start.4
  11.1 36.1 %copy-start.7 = (f32[1,1,4]{2,1,0:T(1,128)S(1)}, f32[1,1,4]{2,1,0:T(1,128)}, u32[]{:S(2)}) copy-start(f32[1,1,4]{2,1,0:T(1,128)} %param.16) | copy-start | bytes 52
  13.4 21.0 %collective-permute-start = (bf16[1,256,512]{2,0,1:T(2,128)(2,1)}, bf16[1,256,512]{2,0,1:T(2,128)(2,1)}, u32[]{:S(2)}, u32[]{:S(2)}) collective-permute-start(bf16[1,256,512]{2,0,1:T(2,128)(2,1)} %get-tuple-element.147), channel_id=1, source_target_pairs={{0,8},{8,16},{16,24},{24,32},{32,40},{40,48},{48,56},{56,64},{64,7... | collective-permute-start | bytes 786440 | tf_op jit(solution)/shard_map/ppermute | solution.py:14
  15.4 20.3 %collective-permute-start.1 = (bf16[1,256,512]{2,0,1:T(2,128)(2,1)}, bf16[1,256,512]{2,0,1:T(2,128)(2,1)}, u32[]{:S(2)}, u32[]{:S(2)}) collective-permute-start(bf16[1,256,512]{2,0,1:T(2,128)(2,1)} %get-tuple-element.150), channel_id=1, source_target_pairs={{8,0},{16,8},{24,16},{32,24},{40,32},{48,40},{56,48},{64,56},{72,6... | collective-permute-start | bytes 786440 | tf_op jit(solution)/shard_map/ppermute | solution.py:17
  23.0 18.8 %collective-permute-start.2 = (bf16[1,256,512]{2,0,1:T(2,128)(2,1)S(1)}, bf16[1,256,512]{2,0,1:T(2,128)(2,1)}, u32[]{:S(2)}, u32[]{:S(2)}) collective-permute-start(bf16[1,256,512]{2,0,1:T(2,128)(2,1)S(1)} %get-tuple-element.149), channel_id=1, source_target_pairs={{0,1},{1,2},{2,3},{3,4},{4,5},{5,6},{6,7},{8,9},{9,10},{10,11},{11... | collective-permute-start | bytes 786440 | tf_op jit(solution)/shard_map/ppermute | solution.py:14
  25.6 21.6 %collective-permute-start.3 = (bf16[1,256,512]{2,0,1:T(2,128)(2,1)S(1)}, bf16[1,256,512]{2,0,1:T(2,128)(2,1)}, u32[]{:S(2)}, u32[]{:S(2)}) collective-permute-start(bf16[1,256,512]{2,0,1:T(2,128)(2,1)S(1)} %get-tuple-element.148), channel_id=1, source_target_pairs={{1,0},{2,1},{3,2},{4,3},{5,4},{6,5},{7,6},{9,8},{10,9},{11,10},{12... | collective-permute-start | bytes 786440 | tf_op jit(solution)/shard_map/ppermute | solution.py:17
  47.2 4.5 %copy-start.3 = (s32[1,1,4,512]{3,2,1,0:T(4,128)S(1)}, s32[1,1,4,512]{3,2,1,0:T(4,128)}, u32[]{:S(2)}) copy-start(s32[1,1,4,512]{3,2,1,0:T(4,128)} %param.15) | copy-start | bytes 24580
  53.1 1.0 copy-start.2
  53.1 80.5 %copy-start.6 = (s32[1,1,256]{2,1,0:T(1,128)S(1)}, s32[1,1,256]{2,1,0:T(1,128)}, u32[]{:S(2)}) copy-start(s32[1,1,256]{2,1,0:T(1,128)} %param.17) | copy-start | bytes 3076
  54.5 1.8 copy-start.1
  56.2 120.8 %all-gather.4.cloned.1.call-start = ((), (), s32[]{:S(2)}) async-start(), calls=%async_computation | async-start | bytes 1179648 | tf_op jit(solution)/shard_map/all_gather | solution.py:126
  57.0 177.3 %all-gather.6.cloned.1.call-start = ((), (), s32[]{:S(2)}) async-start(), calls=%async_computation.1 | async-start | bytes 2162688 | tf_op jit(solution)/shard_map/all_gather | solution.py:24
  57.7 237.9 %all-gather.8.cloned.1.call-start = ((), (), s32[]{:S(2)}) async-start(), calls=%async_computation.3 | async-start | bytes 4325376 | tf_op jit(solution)/shard_map/all_gather | solution.py:24
  368.7 2.8 copy-start.5
  368.7 2.8 copy-start.8
  376.4 20.3 %collective-permute-start.4 = (bf16[1,256,512]{2,0,1:T(2,128)(2,1)S(1)}, bf16[1,256,512]{2,0,1:T(2,128)(2,1)S(1)}, u32[]{:S(2)}, u32[]{:S(2)}) collective-permute-start(bf16[1,256,512]{2,0,1:T(2,128)(2,1)S(1)} %get-tuple-element.143), channel_id=1, source_target_pairs={{0,8},{8,16},{16,24},{24,32},{32,40},{40,48},{48,56},{56,64},{64,7... | collective-permute-start | bytes 786440 | tf_op jit(solution)/shard_map/ppermute | solution.py:14
  378.6 18.5 %collective-permute-start.5 = (bf16[1,256,512]{2,0,1:T(2,128)(2,1)S(1)}, bf16[1,256,512]{2,0,1:T(2,128)(2,1)S(1)}, u32[]{:S(2)}, u32[]{:S(2)}) collective-permute-start(bf16[1,256,512]{2,0,1:T(2,128)(2,1)S(1)} %get-tuple-element.146), channel_id=1, source_target_pairs={{8,0},{16,8},{24,16},{32,24},{40,32},{48,40},{56,48},{64,56},{72,6... | collective-permute-start | bytes 786440 | tf_op jit(solution)/shard_map/ppermute | solution.py:17
  385.0 17.5 %collective-permute-start.6 = (bf16[1,256,512]{2,0,1:T(2,128)(2,1)S(1)}, bf16[1,256,512]{2,0,1:T(2,128)(2,1)S(1)}, u32[]{:S(2)}, u32[]{:S(2)}) collective-permute-start(bf16[1,256,512]{2,0,1:T(2,128)(2,1)S(1)} %get-tuple-element.145), channel_id=1, source_target_pairs={{0,1},{1,2},{2,3},{3,4},{4,5},{5,6},{6,7},{8,9},{9,10},{10,11},{11... | collective-permute-start | bytes 786440 | tf_op jit(solution)/shard_map/ppermute | solution.py:14
  387.1 21.1 %collective-permute-start.7 = (bf16[1,256,512]{2,0,1:T(2,128)(2,1)S(1)}, bf16[1,256,512]{2,0,1:T(2,128)(2,1)S(1)}, u32[]{:S(2)}, u32[]{:S(2)}) collective-permute-start(bf16[1,256,512]{2,0,1:T(2,128)(2,1)S(1)} %get-tuple-element.144), channel_id=1, source_target_pairs={{1,0},{2,1},{3,2},{4,3},{5,4},{6,5},{7,6},{9,8},{10,9},{11,10},{12... | collective-permute-start | bytes 786440 | tf_op jit(solution)/shard_map/ppermute | solution.py:17
Sparse Core Ops, SparseCore 0:
  56.3 77.0 all-reduce.1
  135.3 41.7 all-gather.3
  180.0 54.2 all-gather.5
  237.0 58.5 all-gather.7
where the time goes:
time: 423 us; the launch traced here: 420 us
  waiting for transfers between devices  251 us (59%)
  matrix products  70.6 us (17%)
  local copies, waits for them, and re-layouts  53.2 us (13%)
  starting transfers between devices  30.1 us (7%)
  between operations  13.4 us (3%)
    all_gather x2, waiting for transfers between devices, carried_in(): everything = jax.tree.map(lambda part: lax.all_gather(part, axis), array)  116 us
    psum x1, waiting for transfers between devices, per_device(): lax.psum(jnp.dot(coarse_residual, own_rows, preferred_element_type=jnp.fl...  75.5 us
    dot_general x32, matrix products, compose(): joined_state = jnp.dot(earlier[1], later[0], precision=HIGHEST) + later[1]  37 us
    dynamic_slice x64, local copies, waits for them, and re-layouts, step(): new = combine(before, jax.tree.map(lambda part: part[k], everything))  32.4 us
    ppermute x4, waiting for transfers between devices, with_halo(): lax.ppermute(lax.slice_in_dim(block, block.shape[dim] - width, None, axis...  23 us
    all_gather x1, waiting for transfers between devices, per_device(): lax.all_gather(coarse_residual, 'coarse', axis=1, tiled=True)  22.1 us
    ppermute x4, starting transfers between devices, with_halo(): lax.ppermute(lax.slice_in_dim(block, 0, width, axis=dim), axis, backward)  21 us
    another operation x1, local copies, waits for them, and re-layouts, per_device(): front_inverse[0, 0].reshape(face_count, block_size, face_count, block_size)  14.5 us
  transfers between devices with their start and end apart: 12, of which 12 were waited for; matrix products, arithmetic and copies ran while one was open for 6% of the time, Pallas kernels for 0%

commit v1 on v0

v1 whole, which is shorter than its diff:
```python
import jax
import jax.numpy as jnp
from jax import lax
from jax.experimental import pallas as pl
from jax.experimental.pallas import tpu as pltpu
from jax.sharding import PartitionSpec as P

BF16 = jnp.bfloat16
F32 = jnp.float32


def params(megabytes):
    return pltpu.CompilerParams(vmem_limit_bytes=megabytes << 20)


def cost(flops, bytes_accessed):
    return pl.CostEstimate(flops=flops, bytes_accessed=bytes_accessed, transcendentals=0)


def resident(shape):
    return pl.BlockSpec(shape, lambda *_: (0,) * len(shape))


IN_VMEM = pl.BlockSpec(memory_space=pltpu.VMEM)


def in_hbm(value):
    return pltpu.with_memory_space_constraint(value, pltpu.HBM)


def times(a, b):
    return jnp.dot(a, b, preferred_element_type=F32)


def times_columns(a, b):
    return lax.dot_general(a, b, (((0,), (0,)), ((), ())), preferred_element_type=F32)


def split(value):
    high = value.astype(BF16)
    return high, (value - high.astype(F32)).astype(BF16)


def sorting_table(order, face):
    size = order.shape[1]
    local = lax.broadcasted_iota(jnp.int32, (size, size), 0)
    return jnp.where(local == order[pl.ds(face, 1), :], 1.0, 0.0)


def canon_kernel(slot, parts, order, *outs):
    d = pl.program_id(0)
    table = sorting_table(order, slot[d]).astype(BF16)
    value = times(parts[0], table).astype(BF16)
    for i, out in enumerate(outs):

        @pl.when(d == i)
        def _():
            out[...] = value


def to_canonical(slot, parts, order):
    faces, samples, size = parts.shape
    return pl.pallas_call(
        canon_kernel,
        out_shape=[jax.ShapeDtypeStruct((samples, size), BF16)] * faces,
        grid_spec=pltpu.PrefetchScalarGridSpec(
            num_scalar_prefetch=1,
            grid=(faces,),
            in_specs=[
                pl.BlockSpec((1, samples, size), lambda d, slot: (slot[d], 0, 0)),
                resident((faces, size)),
            ],
            out_specs=[IN_VMEM] * faces,
        ),
        compiler_params=params(8),
        cost_estimate=cost(2 * faces * samples * size * size, 4 * faces * samples * size),
        name="canon",
    )(slot, in_hbm(parts), in_hbm(order))


def tables_kernel(slot, order, basis, sort, restore, ordered, ordered_columns):
    d = pl.program_id(0)
    table = sorting_table(order, slot[d])
    sort[0] = table.astype(BF16)
    restore[0] = table.T.astype(BF16)
    ordered[0] = times(restore[0], basis[0]).astype(BF16)
    ordered_columns[0] = times_columns(basis[0], sort[0]).astype(BF16)


def tables(slot, order, basis):
    faces, size, primal = basis.shape

    def by_direction(*shape):
        return pl.BlockSpec((1,) + shape, lambda d, slot: (d, 0, 0))

    return pl.pallas_call(
        tables_kernel,
        out_shape=[
            pltpu.HBM((faces, size, size), BF16),
            pltpu.HBM((faces, size, size), BF16),
            jax.ShapeDtypeStruct((faces, size, primal), BF16),
            pltpu.HBM((faces, primal, size), BF16),
        ],
        grid_spec=pltpu.PrefetchScalarGridSpec(
            num_scalar_prefetch=1,
            grid=(faces,),
            in_specs=[
                resident((faces, size)),
                pl.BlockSpec((1, size, primal), lambda d, slot: (slot[d], 0, 0)),
            ],
            out_specs=[
                by_direction(size, size),
                by_direction(size, size),
                by_direction(size, primal),
                by_direction(primal, size),
            ],
        ),
        compiler_params=params(12),
        cost_estimate=cost(
            4 * faces * size * size * primal, 4 * faces * size * size + 6 * faces * size * primal
        ),
        name="tables",
    )(slot, in_hbm(order), in_hbm(basis))


def has_neighbour(d):
    axis = "sub" if d < 2 else "coarse"
    place = lax.axis_index(axis)
    return place > 0 if d % 2 == 0 else place < lax.axis_size(axis) - 1


def sum_across(own, beside, d):
    own, beside = own[...].astype(F32), beside[...].astype(F32)
    return own + jnp.where(has_neighbour(d), beside, 0.0)


def residual_kernel(scale, *refs):
    d = pl.program_id(0)
    faces = scale.shape[0]
    canon, beside = refs[:faces], refs[faces : 2 * faces]
    ordered, handoff, averaged, coarse, heat, total = refs[2 * faces :]
    for i in range(faces):

        @pl.when(d == i)
        def _():
            value = (scale[i] * sum_across(canon[i], beside[i], i)).astype(BF16)
            averaged[0] = value
            term = times(value, ordered[i])
            total[...] = term if i == 0 else total[...] + term

    @pl.when(d == faces - 1)
    def _():
        rounded = total[...].astype(BF16)
        coarse[...] = rounded
        primal = rounded.shape[1]
        start = pl.multiple_of(lax.axis_index("coarse") * primal, primal)
        heat[...] = times(rounded, handoff[pl.ds(start, primal), :])


def residuals(scale, canon, beside, ordered, handoff):
    faces, size, primal = ordered.shape
    samples = canon[0].shape[0]
    channels = handoff.shape[1]
    return pl.pallas_call(
        residual_kernel,
        out_shape=[
            pltpu.HBM((faces, samples, size), BF16),
            jax.ShapeDtypeStruct((samples, primal), BF16),
            jax.ShapeDtypeStruct((samples, channels), F32),
        ],
        grid=(faces,),
        in_specs=[pl.BlockSpec(memory_space=pltpu.SMEM)] + [IN_VMEM] * (2 * faces + 2),
        out_specs=[pl.BlockSpec((1, samples, size), lambda d: (d, 0, 0)), IN_VMEM, IN_VMEM],
        scratch_shapes=[pltpu.VMEM((samples, primal), F32)],
        compiler_params=params(8),
        cost_estimate=cost(
            2 * faces * samples * size * primal, 6 * faces * samples * size + 2 * faces * size * primal
        ),
        name="residuals",
    )(scale, *canon, *beside, ordered, handoff)


def share_kernel(inflow, out):
    total = inflow[0]
    for q in range(1, inflow.shape[0]):
        total = total + inflow[q]
    out[...] = jnp.broadcast_to(total[None], out.shape)


def shared_sum(inflow, lines):
    members, share, channels = inflow.shape
    return pl.pallas_call(
        share_kernel,
        out_shape=jax.ShapeDtypeStruct((lines, share, channels), F32),
        compiler_params=params(8),
        cost_estimate=cost(members * share * channels, 4 * (lines + members) * share * channels),
        name="shared_sum",
    )(inflow)


def dual_kernel(slot, scale, averaged, restore, sort, mask, inverse, out, masked):
    i = pl.program_id(0)
    faces, _, size = masked.shape

    @pl.when(i < faces)
    def _():
        local = times(averaged[0], restore[0])
        masked[slot[i]] = (local * mask[slot[i]]).astype(BF16)

    @pl.when(i >= faces)
    def _():
        d = i - faces
        total = None
        for g in range(faces):
            term = times(masked[g], inverse[g * size : (g + 1) * size, :])
            total = term if total is None else total + term
        high, low = split(total * (mask[slot[d]] * scale[d]))
        out[0] = times(high, sort[0]) + times(low, sort[0])


def dual(slot, scale, averaged, sort, restore, mask, inverse):
    faces, samples, size = averaged.shape

    def first(i):
        return jnp.minimum(i, faces - 1)

    def second(i):
        return jnp.maximum(i - faces, 0)

    return pl.pallas_call(
        dual_kernel,
        out_shape=pltpu.HBM(averaged.shape, F32),
        grid_spec=pltpu.PrefetchScalarGridSpec(
            num_scalar_prefetch=1,
            grid=(2 * faces,),
            in_specs=[
                pl.BlockSpec(memory_space=pltpu.SMEM),
                pl.BlockSpec((1, samples, size), lambda i, slot: (first(i), 0, 0)),
                pl.BlockSpec((1, size, size), lambda i, slot: (first(i), 0, 0)),
                pl.BlockSpec((1, size, size), lambda i, slot: (second(i), 0, 0)),
                resident(mask.shape),
                pl.BlockSpec((faces * size, size), lambda i, slot: (0, slot[second(i)])),
            ],
            out_specs=pl.BlockSpec((1, samples, size), lambda i, slot: (second(i), 0, 0)),
            scratch_shapes=[pltpu.VMEM((faces, samples, size), BF16)],
        ),
        compiler_params=params(16),
        cost_estimate=cost(
            2 * samples * faces * size * (faces + 3) * size,
            2 * faces * size * (faces + 2) * size + 6 * faces * samples * size,
        ),
        name="dual",
    )(slot, scale, in_hbm(averaged), in_hbm(restore), in_hbm(sort), mask, in_hbm(inverse))


def chain_kernel(inflow, transfer, out, state):
    i = pl.program_id(0)
    lines = inflow.shape[0]

    @pl.when(i == 0)
    def _():
        state[...] = jnp.zeros_like(state)

    def step(k, value):
        high, low = split(value)
        map_high, map_low = split(transfer[k])
        value = times(high, map_high) + (times(low, map_high) + times(high, map_low))
        return value + inflow[k]

    ahead = jnp.clip(lax.axis_index("sub") - i * lines, 0, lines)
    state[...] = lax.fori_loop(0, ahead, step, state[...])

    @pl.when(i == pl.num_programs(0) - 1)
    def _():
        out[...] = jnp.broadcast_to(state[...][None], out.shape)


def chain(inflow, transfer, members):
    lines, samples, channels = inflow.shape
    steps = 4
    return pl.pallas_call(
        chain_kernel,
        out_shape=jax.ShapeDtypeStruct((members, samples, channels), F32),
        grid=(steps,),
        in_specs=[
            pl.BlockSpec((lines // steps, samples, channels), lambda i: (i, 0, 0)),
            pl.BlockSpec((lines // steps, channels, channels), lambda i: (i, 0, 0)),
        ],
        out_specs=IN_VMEM,
        scratch_shapes=[pltpu.VMEM((samples, channels), F32)],
        compiler_params=params(8),
        cost_estimate=cost(
            6 * lines * samples * channels * channels, 4 * lines * channels * (samples + channels)
        ),
        name="chain",
    )(inflow, in_hbm(transfer))


def line_kernel(gathered, inverse, out):
    members, _, primal = gathered.shape
    member = lax.axis_index("coarse")
    total = None
    for i, bits in enumerate(GATHER_BITS):
        start = pl.multiple_of(jnp.bitwise_xor(member, bits) * primal, primal)
        term = times(gathered[i], inverse[pl.ds(start, primal), :])
        total = term if total is None else total + term
    out[...] = total


def line_base(gathered, inverse):
    members, samples, primal = gathered.shape
    return pl.pallas_call(
        line_kernel,
        out_shape=jax.ShapeDtypeStruct((samples, primal), F32),
        grid=(1,),
        in_specs=[resident(gathered.shape), resident(inverse.shape)],
        out_specs=IN_VMEM,
        compiler_params=params(12),
        cost_estimate=cost(
            2 * members * samples * primal * primal, 2 * members * primal * (samples + primal)
        ),
        name="line_base",
    )(gathered, in_hbm(inverse))


def extend_kernel(scale, base, carried, coupling, ordered_columns, dual_part, *rest):
    outs, answer = rest[:-1], rest[-1]
    d = pl.program_id(0)

    @pl.when(d == 0)
    def _():
        high, low = split(carried[...])
        term = times(high, coupling[...]) + times(low, coupling[...])
        answer[...] = (base[...] + term).astype(BF16)

    value = dual_part[0] + scale[d] * times(answer[...], ordered_columns[0])
    value = value.astype(BF16)
    for i, out in enumerate(outs):

        @pl.when(d == i)
        def _():
            out[...] = value


def extend(scale, base, carried, coupling, ordered_columns, dual_part):
    faces, samples, size = dual_part.shape
    primal = base.shape[1]
    channels = carried.shape[1]
    return pl.pallas_call(
        extend_kernel,
        out_shape=[jax.ShapeDtypeStruct((samples, size), BF16)] * faces,
        grid=(faces,),
        in_specs=[
            pl.BlockSpec(memory_space=pltpu.SMEM),
            IN_VMEM,
            IN_VMEM,
            resident((channels, primal)),
            pl.BlockSpec((1, primal, size), lambda d: (d, 0, 0)),
            pl.BlockSpec((1, samples, size), lambda d: (d, 0, 0)),
        ],
        out_specs=[IN_VMEM] * faces,
        scratch_shapes=[pltpu.VMEM((samples, primal), BF16)],
        compiler_params=params(8),
        cost_estimate=cost(
            2 * faces * samples * size * primal, 6 * faces * samples * size + 2 * faces * size * primal
        ),
        name="extend",
    )(scale, base, carried, in_hbm(coupling), in_hbm(ordered_columns), in_hbm(dual_part))


def finish_kernel(slot, *refs):
    d = pl.program_id(0)
    restore, out = refs[-2:]
    faces = (len(refs) - 2) // 2
    for i in range(faces):

        @pl.when(d == i)
        def _():
            value = sum_across(refs[i], refs[faces + i], i).astype(BF16)
            out[0] = times(value, restore[i]).astype(BF16)


def finish(slot, weighted, beside, restore):
    faces, size, _ = restore.shape
    samples = weighted[0].shape[0]
    return pl.pallas_call(
        finish_kernel,
        out_shape=jax.ShapeDtypeStruct((faces, samples, size), BF16),
        grid_spec=pltpu.PrefetchScalarGridSpec(
            num_scalar_prefetch=1,
            grid=(faces,),
            in_specs=[IN_VMEM] * (2 * faces + 1),
            out_specs=pl.BlockSpec((1, samples, size), lambda d, s: (s[d], 0, 0)),
        ),
        compiler_params=params(8),
        cost_estimate=cost(
            2 * faces * samples * size * size, 6 * faces * samples * size + 2 * faces * size * size
        ),
        name="finish",
    )(slot, *weighted, *beside, restore)


GATHER_STAGES = (2, 1, 4)
GATHER_BITS = (0, 2, 1, 3, 4, 6, 5, 7)


def gather_stage(value, bit):
    pairs = [(i, i ^ bit) for i in range(lax.axis_size("coarse"))]
    return lax.ppermute(value, "coarse", pairs)


def neighbours(faces):
    lower, upper, left, right = faces

    def shifted(value, axis, step):
        count = lax.axis_size(axis)
        pairs = [(i, (i + step) % count) for i in range(count)]
        return lax.ppermute(value, axis, pairs)

    return (
        shifted(upper, "sub", 1),
        shifted(lower, "sub", -1),
        shifted(right, "coarse", 1),
        shifted(left, "coarse", -1),
    )


def per_device(
    residual_parts,
    face_slot,
    face_order,
    face_scale,
    vertex_unknowns,
    front_inverse,
    coarse_basis,
    coarse_inverse,
    thermal_handoff,
    chain_transfer,
    coupling_in,
):
    parts = residual_parts[0, 0]
    slot = face_slot[0, 0]
    order = face_order[0, 0]
    scale = face_scale[0, 0]
    faces, samples, size = parts.shape
    basis = coarse_basis[0, 0].reshape(faces, size, -1)
    lines, members = lax.axis_size("sub"), lax.axis_size("coarse")
    share = samples // members

    transfers = lax.all_gather(chain_transfer[0], "sub")

    canon = to_canonical(slot, parts, order)
    beside = neighbours(canon)
    basis, canon = lax.optimization_barrier((basis, canon))
    sort, restore, ordered, ordered_columns = tables(slot, order, basis)
    averaged, coarse_residual, heat = residuals(
        scale, canon, beside, ordered, thermal_handoff[0]
    )

    channels = heat.shape[1]
    gathered = coarse_residual[None]
    received = gather_stage(gathered, GATHER_STAGES[0])
    inflow = lax.all_to_all(heat.reshape(members, share, channels), "coarse", 0, 0)
    inflow = shared_sum(inflow, lines)
    averaged, received, inflow = lax.optimization_barrier((averaged, received, inflow))
    inflow = lax.all_to_all(inflow, "sub", 0, 0)
    gathered = jnp.concatenate([gathered, received])
    received = gather_stage(gathered, GATHER_STAGES[1])

    positions = lax.broadcasted_iota(jnp.int32, (vertex_unknowns.shape[2], faces * size), 1)
    hits = jnp.sum((vertex_unknowns[0, 0][:, None] == positions).astype(F32), axis=0)
    mask = (1.0 - hits).reshape(faces, 1, size)
    dual_part = dual(slot, scale, averaged, sort, restore, mask, front_inverse[0, 0])

    inflow, received, dual_part = lax.optimization_barrier((inflow, received, dual_part))
    gathered = jnp.concatenate([gathered, received])
    gathered = jnp.concatenate([gathered, gather_stage(gathered, GATHER_STAGES[2])])
    carried = chain(inflow, transfers, members)
    carried = lax.all_to_all(carried, "coarse", 0, 0).reshape(samples, channels)
    base = line_base(gathered, coarse_inverse[0])

    weighted = extend(scale, base, carried, coupling_in[0], ordered_columns, dual_part)
    beside = neighbours(weighted)
    return finish(slot, weighted, beside, restore)[None, None]


def solution(mesh):
    placed = (
        P("sub", "coarse", None, None, None),
        P("sub", "coarse", None),
        P("sub", "coarse", None, None),
        P("sub", "coarse", None),
        P("sub", "coarse", None),
        P("sub", "coarse", None, None),
        P("sub", "coarse", None, None),
        P("sub", None, "coarse"),
        P("sub", None, None),
        P("sub", None, None),
        P("sub", None, "coarse"),
    )
    return jax.shard_map(
        per_device,
        mesh=mesh,
        in_specs=placed,
        out_specs=P("sub", "coarse", None, None, None),
        check_vma=False,
    )
```

time: 423 us -> 126 us (0.30)
  the two profiles are of different devices: /device:TPU:26 before, /device:TPU:2 now
where the time goes in v1:
time: 126 us; the launch traced here: 125 us
  starting transfers between devices  40.9 us (32%)
  Pallas kernels  36.6 us (29%)
  waiting for transfers between devices  32.2 us (26%)
  between operations  13.5 us (11%)
  local copies, waits for them, and re-layouts  1.33 us (1%)
    ppermute x8, starting transfers between devices, shifted(): return lax.ppermute(value, axis, pairs)  16.9 us
    ppermute x8, waiting for transfers between devices, shifted(): return lax.ppermute(value, axis, pairs)  16.7 us
    pallas_call x1, Pallas kernels, dual(): pl.pallas_call(dual_kernel, out_shape=pltpu.HBM(averaged.shape, F32), gri...  11.7 us
    all_to_all x1, starting transfers between devices, per_device(): inflow = lax.all_to_all(inflow, 'sub', 0, 0)  9.63 us
    ppermute x3, starting transfers between devices, gather_stage(): return lax.ppermute(value, 'coarse', pairs)  5.55 us
    all_to_all x1, waiting for transfers between devices, per_device(): inflow = lax.all_to_all(inflow, 'sub', 0, 0)  5.49 us
    all_to_all x1, starting transfers between devices, per_device(): carried = lax.all_to_all(carried, 'coarse', 0, 0).reshape(samples, channels)  5.3 us
    pallas_call x1, Pallas kernels, tables(): pl.pallas_call(tables_kernel, out_shape=[pltpu.HBM((faces, size, size), B...  5.27 us
  transfers between devices with their start and end apart: 15, of which 8 were waited for; matrix products, arithmetic and copies ran while one was open for 0% of the time, Pallas kernels for 24%

profile of v1, /device:TPU:2, one launch (start us, length us, event | category | flops | bytes accessed | tf_op | source)
XLA Modules:
  0.0 125.1 jit_solution(14183146741890651911)
XLA Ops:
  6.5 0.7 all-gather.2.cloned.1.call-update
  7.3 0.6 copy-done.3
  7.9 3.5 %canon.1 = (bf16[256,512]{1,0:T(8,128)(2,1)S(1)}, bf16[256,512]{1,0:T(8,128)(2,1)S(1)}, bf16[256,512]{1,0:T(8,128)(2,1)S(1)}, bf16[256,512]{1,0:T(8,128)(2,1)S(1)}) custom-call(s32[4]{0:T(128)S(1)} %bitcast.25, bf16[4,256,512]{2,1,0:T(8,128)(2,1)} %bitcast.33, s32[4,512]{1,0:T(4,128)} %bitcast.35), custom_call_target="tpu_custom_call" | custom-call | flops 536870912 | bytes 2097152 | tf_op jit(solution)/shard_map/canon/pallas_call | solution.py:63
  11.6 5.8 %collective-permute-start.1 = (bf16[256,512]{1,0:T(8,128)(2,1)S(1)}, bf16[256,512]{1,0:T(8,128)(2,1)S(1)}, u32[]{:S(2)}, u32[]{:S(2)}) collective-permute-start(bf16[256,512]{1,0:T(8,128)(2,1)S(1)} %get-tuple-element.35.refs_0_), channel_id=1, source_target_pairs={{0,248},{8,0},{16,8},{24,16},{32,24},{40,32},{48,40},{56,48},{64,5... | collective-permute-start | bytes 786440 | tf_op jit(solution)/shard_map/ppermute | solution.py:418
  17.4 1.6 %collective-permute-start.2 = (bf16[256,512]{1,0:T(8,128)(2,1)S(1)}, bf16[256,512]{1,0:T(8,128)(2,1)S(1)}, u32[]{:S(2)}, u32[]{:S(2)}) collective-permute-start(bf16[256,512]{1,0:T(8,128)(2,1)S(1)} %get-tuple-element.38.refs_3_), channel_id=1, source_target_pairs={{0,1},{1,2},{2,3},{3,4},{4,5},{5,6},{6,7},{7,0},{8,9},{9,10},{10,1... | collective-permute-start | bytes 786440 | tf_op jit(solution)/shard_map/ppermute | solution.py:418
  18.9 2.6 %collective-permute-start.3 = (bf16[256,512]{1,0:T(8,128)(2,1)S(1)}, bf16[256,512]{1,0:T(8,128)(2,1)S(1)}, u32[]{:S(2)}, u32[]{:S(2)}) collective-permute-start(bf16[256,512]{1,0:T(8,128)(2,1)S(1)} %get-tuple-element.37.refs_2_), channel_id=1, source_target_pairs={{0,7},{1,0},{2,1},{3,2},{4,3},{5,4},{6,5},{7,6},{8,15},{9,8},{10,9... | collective-permute-start | bytes 786440 | tf_op jit(solution)/shard_map/ppermute | solution.py:418
  21.5 0.7 copy-done.4
  22.2 5.3 %tables.1 = (bf16[4,512,512]{2,1,0:T(8,128)(2,1)}, bf16[4,512,512]{2,1,0:T(8,128)(2,1)}, bf16[4,512,256]{2,1,0:T(8,128)(2,1)S(1)}, bf16[4,256,512]{2,1,0:T(8,128)(2,1)}) custom-call(s32[4]{0:T(128)S(1)} %bitcast.26, s32[4,512]{1,0:T(4,128)} %bitcast.36, bf16[4,512,256]{2,1,0:T(8,128)(2,1)} %bitcast.34), custom_call_target="tpu_custom_call" | custom-call | flops 1073741824 | bytes 7340032 | tf_op jit(solution)/shard_map/tables/pallas_call | solution.py:96
  27.4 4.7 %collective-permute-done.2.refs_6_ = bf16[256,512]{1,0:T(8,128)(2,1)S(1)} collective-permute-done((bf16[256,512]{1,0:T(8,128)(2,1)S(1)}, bf16[256,512]{1,0:T(8,128)(2,1)S(1)}, u32[]{:S(2)}, u32[]{:S(2)}) %collective-permute-start.2) | collective-permute-done | bytes 262176 | tf_op jit(solution)/shard_map/ppermute | solution.py:418
  32.1 3.1 %residuals.1 = (bf16[4,256,512]{2,1,0:T(8,128)(2,1)}, bf16[256,256]{1,0:T(8,128)(2,1)S(1)}, f32[256,128]{1,0:T(8,128)}) custom-call(f32[4]{0:T(128)S(1)} %bitcast.22, bf16[256,512]{1,0:T(8,128)(2,1)S(1)} %get-tuple-element.35.refs_0_, bf16[256,512]{1,0:T(8,128)(2,1)S(1)} %get-tuple-element.36.refs_1_, bf16[256,512]{1,0:T(8,128)(2,1)S(1)} %get-tuple-element.37.refs_2_, ...), custom_call_target="tpu_custom_call" | custom-call | flops 268435456 | bytes 4194304 | tf_op jit(solution)/shard_map/residuals/pallas_call | solution.py:164
  35.2 3.5 %all-to-all-start = ((f32[8,32,128]{2,1,0:T(8,128)}), f32[8,32,128]{2,1,0:T(8,128)S(1)}, u32[]{:S(2)}, u32[]{:S(2)}) async-start(f32[8,32,128]{2,1,0:T(8,128)} %bitcast.7), calls=%async_computation | async-start | bytes 262144 | tf_op jit(solution)/shard_map/all_to_all | solution.py:463
  38.7 3.4 %collective-permute-start.4 = (bf16[1,256,256]{2,1,0:T(8,128)(2,1)S(1)}, bf16[1,256,256]{2,1,0:T(8,128)(2,1)S(1)}, u32[]{:S(2)}, u32[]{:S(2)}) collective-permute-start(bf16[1,256,256]{2,1,0:T(8,128)(2,1)S(1)} %bitcast.15), channel_id=1, source_target_pairs={{0,2},{1,3},{2,0},{3,1},{4,6},{5,7},{6,4},{7,5},{8,10},{9,11},{10,... | collective-permute-start | bytes 393224 | tf_op jit(solution)/shard_map/ppermute | solution.py:409
  42.2 3.3 %all-to-all-done.inflow = f32[8,32,128]{2,1,0:T(8,128)S(1)} async-done(((f32[8,32,128]{2,1,0:T(8,128)}), f32[8,32,128]{2,1,0:T(8,128)S(1)}, u32[]{:S(2)}, u32[]{:S(2)}) %all-to-all-start) | async-done | bytes 131104 | tf_op jit(solution)/shard_map/all_to_all | solution.py:463
  45.4 0.9 shared_sum.1
  46.3 9.6 %all-to-all-start.1 = ((f32[32,32,128]{2,1,0:T(8,128)}), f32[32,32,128]{2,1,0:T(8,128)S(1)}, u32[]{:S(2)}, u32[]{:S(2)}) async-start(f32[32,32,128]{2,1,0:T(8,128)} %shared_sum.1), calls=%async_computation.1 | async-start | bytes 1048576 | tf_op jit(solution)/shard_map/all_to_all | solution.py:466
  56.0 0.3 convert_reduce_fusion
  56.3 0.9 collective-permute-start.5
  57.2 11.7 %dual.1.dual_part = f32[4,256,512]{2,1,0:T(8,128)} custom-call(s32[4]{0:T(128)S(1)} %bitcast.27, f32[4]{0:T(128)S(1)} %bitcast.23, bf16[4,256,512]{2,1,0:T(8,128)(2,1)} %get-tuple-element.46.averaged, bf16[4,512,512]{2,1,0:T(8,128)(2,1)} %get-tuple-element.47.restore.refs_8_, bf16[4,512,512]{2,1,0:T(8,128)(2,1)} %get-tuple-element.48.sort, ...), custom_call_target="tpu_custom_call" | custom-call | flops 3758096384 | bytes 15728640 | tf_op jit(solution)/shard_map/dual/pallas_call | solution.py:230
  68.9 5.5 %all-to-all-done.1.inflow = f32[32,32,128]{2,1,0:T(8,128)S(1)} async-done(((f32[32,32,128]{2,1,0:T(8,128)}), f32[32,32,128]{2,1,0:T(8,128)S(1)}, u32[]{:S(2)}, u32[]{:S(2)}) %all-to-all-start.1) | async-done | bytes 524320 | tf_op jit(solution)/shard_map/all_to_all | solution.py:466
  74.5 1.2 collective-permute-start.6
  75.7 4.2 %chain.1 = f32[8,32,128]{2,1,0:T(8,128)} custom-call(f32[32,32,128]{2,1,0:T(8,128)S(1)} %all-to-all-done.1.inflow, f32[32,128,128]{2,1,0:T(8,128)} %all-gather.2.cloned.1.call-done.transfer), custom_call_target="tpu_custom_call" | custom-call | flops 100663296 | bytes 2621440 | tf_op jit(solution)/shard_map/chain/pallas_call | solution.py:281
  79.8 5.3 %all-to-all-start.2 = ((f32[8,32,128]{2,1,0:T(8,128)}), f32[8,32,128]{2,1,0:T(8,128)S(1)}, u32[]{:S(2)}, u32[]{:S(2)}) async-start(f32[8,32,128]{2,1,0:T(8,128)} %chain.1), calls=%async_computation.2 | async-start | bytes 262144 | tf_op jit(solution)/shard_map/all_to_all | solution.py:479
  85.1 3.8 %collective-permute-done.6 = bf16[4,256,256]{2,1,0:T(8,128)(2,1)S(1)} collective-permute-done((bf16[4,256,256]{2,1,0:T(8,128)(2,1)S(1)}, bf16[4,256,256]{2,1,0:T(8,128)(2,1)S(1)}, u32[]{:S(2)}, u32[]{:S(2)}) %collective-permute-start.6) | collective-permute-done | bytes 524320 | tf_op jit(solution)/shard_map/ppermute | solution.py:409
  89.1 1.7 %line_base.1.base = f32[256,256]{1,0:T(8,128)S(1)} custom-call(bf16[8,256,256]{2,1,0:T(8,128)(2,1)S(1)} %pad_maximum_fusion.gathered, bf16[2048,256]{1,0:T(8,128)(2,1)} %bitcast.30), custom_call_target="tpu_custom_call" | custom-call | flops 268435456 | bytes 2097152 | tf_op jit(solution)/shard_map/line_base/pallas_call | solution.py:312
  90.8 2.2 %all-to-all-done.2 = f32[8,32,128]{2,1,0:T(8,128)S(1)} async-done(((f32[8,32,128]{2,1,0:T(8,128)}), f32[8,32,128]{2,1,0:T(8,128)S(1)}, u32[]{:S(2)}, u32[]{:S(2)}) %all-to-all-start.2) | async-done | bytes 131104 | tf_op jit(solution)/shard_map/all_to_all | solution.py:479
  93.0 3.4 %extend.1 = (bf16[256,512]{1,0:T(8,128)(2,1)S(1)}, bf16[256,512]{1,0:T(8,128)(2,1)S(1)}, bf16[256,512]{1,0:T(8,128)(2,1)S(1)}, bf16[256,512]{1,0:T(8,128)(2,1)S(1)}) custom-call(f32[4]{0:T(128)S(1)} %bitcast.24, f32[256,256]{1,0:T(8,128)S(1)} %line_base.1.base, f32[256,128]{1,0:T(8,128)S(1)} %bitcast.20, bf16[128,256]{1,0:T(8,128)(2,1)} %bitcast.31, ...), custom_call_target="tpu_custom_call" | custom-call | flops 268435456 | bytes 4194304 | tf_op jit(solution)/shard_map/extend/pallas_call | solution.py:349
  96.4 2.2 %collective-permute-start.10 = (bf16[256,512]{1,0:T(8,128)(2,1)S(1)}, bf16[256,512]{1,0:T(8,128)(2,1)S(1)}, u32[]{:S(2)}, u32[]{:S(2)}) collective-permute-start(bf16[256,512]{1,0:T(8,128)(2,1)S(1)} %get-tuple-element.55.refs_2_), channel_id=1, source_target_pairs={{0,7},{1,0},{2,1},{3,2},{4,3},{5,4},{6,5},{7,6},{8,15},{9,8},{10,9... | collective-permute-start | bytes 786440 | tf_op jit(solution)/shard_map/ppermute | solution.py:418
  98.6 4.8 %collective-permute-start.8 = (bf16[256,512]{1,0:T(8,128)(2,1)S(1)}, bf16[256,512]{1,0:T(8,128)(2,1)S(1)}, u32[]{:S(2)}, u32[]{:S(2)}) collective-permute-start(bf16[256,512]{1,0:T(8,128)(2,1)S(1)} %get-tuple-element.53.refs_0_), channel_id=1, source_target_pairs={{0,248},{8,0},{16,8},{24,16},{32,24},{40,32},{48,40},{56,48},{64,5... | collective-permute-start | bytes 786440 | tf_op jit(solution)/shard_map/ppermute | solution.py:418
  103.3 4.8 %collective-permute-done.10.refs_7_ = bf16[256,512]{1,0:T(8,128)(2,1)S(1)} collective-permute-done((bf16[256,512]{1,0:T(8,128)(2,1)S(1)}, bf16[256,512]{1,0:T(8,128)(2,1)S(1)}, u32[]{:S(2)}, u32[]{:S(2)}) %collective-permute-start.10) | collective-permute-done | bytes 262176 | tf_op jit(solution)/shard_map/ppermute | solution.py:418
  108.1 5.7 %collective-permute-done.7.refs_4_ = bf16[256,512]{1,0:T(8,128)(2,1)S(1)} collective-permute-done((bf16[256,512]{1,0:T(8,128)(2,1)S(1)}, bf16[256,512]{1,0:T(8,128)(2,1)S(1)}, u32[]{:S(2)}, u32[]{:S(2)}) %collective-permute-start.7) | collective-permute-done | bytes 262176 | tf_op jit(solution)/shard_map/ppermute | solution.py:418
  113.9 1.5 %collective-permute-done.9.refs_6_ = bf16[256,512]{1,0:T(8,128)(2,1)S(1)} collective-permute-done((bf16[256,512]{1,0:T(8,128)(2,1)S(1)}, bf16[256,512]{1,0:T(8,128)(2,1)S(1)}, u32[]{:S(2)}, u32[]{:S(2)}) %collective-permute-start.9) | collective-permute-done | bytes 262176 | tf_op jit(solution)/shard_map/ppermute | solution.py:418
  115.3 3.0 %finish.1 = bf16[4,256,512]{2,1,0:T(8,128)(2,1)} custom-call(s32[4]{0:T(128)S(1)} %bitcast.28, bf16[256,512]{1,0:T(8,128)(2,1)S(1)} %get-tuple-element.53.refs_0_, bf16[256,512]{1,0:T(8,128)(2,1)S(1)} %get-tuple-element.54.refs_1_, bf16[256,512]{1,0:T(8,128)(2,1)S(1)} %get-tuple-element.55.refs_2_, bf16[256,512]{1,0:T(8,128)(2,1)S(1)} %get-tuple-element.56.refs_3_, ...), custom_call_target="tpu_custom_call" | custom-call | flops 536870912 | bytes 5242880 | tf_op jit(solution)/shard_map/finish/pallas_call | solution.py:386
  (27 shorter events, 0.3 us)
Async XLA Ops:
  6.5 69.2 %all-gather.2.cloned.1.call-start = ((), (), s32[]{:S(2)}) async-start(), calls=%async_computation.3 | async-start | bytes 2162688 | tf_op jit(solution)/shard_map/all_gather | solution.py:450
  7.3 0.7 copy-start.3
  11.5 20.7 %copy-start.1 = (bf16[1,2048,128]{2,1,0:T(8,128)(2,1)S(1)}, bf16[1,2048,128]{2,1,0:T(8,128)(2,1)}, u32[]{:S(2)}) copy-start(bf16[1,2048,128]{2,1,0:T(8,128)(2,1)} %param.19) | copy-start | bytes 1572868
  11.5 20.6 %copy-start.2 = (f32[1,1,4]{2,1,0:T(1,128)S(1)}, f32[1,1,4]{2,1,0:T(1,128)}, u32[]{:S(2)}) copy-start(f32[1,1,4]{2,1,0:T(1,128)} %param.14) | copy-start | bytes 52
  11.5 15.9 %collective-permute-start = (bf16[256,512]{1,0:T(8,128)(2,1)S(1)}, bf16[256,512]{1,0:T(8,128)(2,1)S(1)}, u32[]{:S(2)}, u32[]{:S(2)}) collective-permute-start(bf16[256,512]{1,0:T(8,128)(2,1)S(1)} %get-tuple-element.36.refs_1_), channel_id=1, source_target_pairs={{0,8},{8,16},{16,24},{24,32},{32,40},{40,48},{48,56},{56,64},{64,7... | collective-permute-start | bytes 786440 | tf_op jit(solution)/shard_map/ppermute | solution.py:418
  11.6 15.9 %collective-permute-start.1 = (bf16[256,512]{1,0:T(8,128)(2,1)S(1)}, bf16[256,512]{1,0:T(8,128)(2,1)S(1)}, u32[]{:S(2)}, u32[]{:S(2)}) collective-permute-start(bf16[256,512]{1,0:T(8,128)(2,1)S(1)} %get-tuple-element.35.refs_0_), channel_id=1, source_target_pairs={{0,248},{8,0},{16,8},{24,16},{32,24},{40,32},{48,40},{56,48},{64,5... | collective-permute-start | bytes 786440 | tf_op jit(solution)/shard_map/ppermute | solution.py:418
  17.4 14.7 %collective-permute-start.2 = (bf16[256,512]{1,0:T(8,128)(2,1)S(1)}, bf16[256,512]{1,0:T(8,128)(2,1)S(1)}, u32[]{:S(2)}, u32[]{:S(2)}) collective-permute-start(bf16[256,512]{1,0:T(8,128)(2,1)S(1)} %get-tuple-element.38.refs_3_), channel_id=1, source_target_pairs={{0,1},{1,2},{2,3},{3,4},{4,5},{5,6},{6,7},{7,0},{8,9},{9,10},{10,1... | collective-permute-start | bytes 786440 | tf_op jit(solution)/shard_map/ppermute | solution.py:418
  18.9 13.2 %collective-permute-start.3 = (bf16[256,512]{1,0:T(8,128)(2,1)S(1)}, bf16[256,512]{1,0:T(8,128)(2,1)S(1)}, u32[]{:S(2)}, u32[]{:S(2)}) collective-permute-start(bf16[256,512]{1,0:T(8,128)(2,1)S(1)} %get-tuple-element.37.refs_2_), channel_id=1, source_target_pairs={{0,7},{1,0},{2,1},{3,2},{4,3},{5,4},{6,5},{7,6},{8,15},{9,8},{10,9... | collective-permute-start | bytes 786440 | tf_op jit(solution)/shard_map/ppermute | solution.py:418
  21.5 0.7 copy-start.4
  32.1 23.8 %copy-start.6 = (s32[1,1,256]{2,1,0:T(1,128)S(1)}, s32[1,1,256]{2,1,0:T(1,128)}, u32[]{:S(2)}) copy-start(s32[1,1,256]{2,1,0:T(1,128)} %param.15) | copy-start | bytes 3076
  35.2 22.0 %copy-start.5 = (s32[1,1,4]{2,1,0:T(1,128)S(1)}, s32[1,1,4]{2,1,0:T(1,128)}, u32[]{:S(2)}) copy-start(s32[1,1,4]{2,1,0:T(1,128)} %param.12) | copy-start | bytes 52
  35.2 10.2 %all-to-all-start = ((f32[8,32,128]{2,1,0:T(8,128)}), f32[8,32,128]{2,1,0:T(8,128)S(1)}, u32[]{:S(2)}, u32[]{:S(2)}) async-start(f32[8,32,128]{2,1,0:T(8,128)} %bitcast.7), calls=%async_computation | async-start | bytes 262144 | tf_op jit(solution)/shard_map/all_to_all | solution.py:463
  38.7 7.6 %collective-permute-start.4 = (bf16[1,256,256]{2,1,0:T(8,128)(2,1)S(1)}, bf16[1,256,256]{2,1,0:T(8,128)(2,1)S(1)}, u32[]{:S(2)}, u32[]{:S(2)}) collective-permute-start(bf16[1,256,256]{2,1,0:T(8,128)(2,1)S(1)} %bitcast.15), channel_id=1, source_target_pairs={{0,2},{1,3},{2,0},{3,1},{4,6},{5,7},{6,4},{7,5},{8,10},{9,11},{10,... | collective-permute-start | bytes 393224 | tf_op jit(solution)/shard_map/ppermute | solution.py:409
  46.3 28.1 %all-to-all-start.1 = ((f32[32,32,128]{2,1,0:T(8,128)}), f32[32,32,128]{2,1,0:T(8,128)S(1)}, u32[]{:S(2)}, u32[]{:S(2)}) async-start(f32[32,32,128]{2,1,0:T(8,128)} %shared_sum.1), calls=%async_computation.1 | async-start | bytes 1048576 | tf_op jit(solution)/shard_map/all_to_all | solution.py:466
  56.3 12.6 %collective-permute-start.5 = (bf16[2,256,256]{2,1,0:T(8,128)(2,1)S(1)}, bf16[2,256,256]{2,1,0:T(8,128)(2,1)S(1)}, u32[]{:S(2)}, u32[]{:S(2)}) collective-permute-start(bf16[2,256,256]{2,1,0:T(8,128)(2,1)S(1)} %pad_maximum_fusion.2), channel_id=1, source_target_pairs={{0,1},{1,0},{2,3},{3,2},{4,5},{5,4},{6,7},{7,6},{8,9},{9,8},{10,11... | collective-permute-start | bytes 786440 | tf_op jit(solution)/shard_map/ppermute | solution.py:409
  74.5 14.5 %collective-permute-start.6 = (bf16[4,256,256]{2,1,0:T(8,128)(2,1)S(1)}, bf16[4,256,256]{2,1,0:T(8,128)(2,1)S(1)}, u32[]{:S(2)}, u32[]{:S(2)}) collective-permute-start(bf16[4,256,256]{2,1,0:T(8,128)(2,1)S(1)} %pad_maximum_fusion.1), channel_id=1, source_target_pairs={{0,4},{1,5},{2,6},{3,7},{4,0},{5,1},{6,2},{7,3},{8,12},{9,13},{10,... | collective-permute-start | bytes 1572872 | tf_op jit(solution)/shard_map/ppermute | solution.py:409
  79.8 13.2 %all-to-all-start.2 = ((f32[8,32,128]{2,1,0:T(8,128)}), f32[8,32,128]{2,1,0:T(8,128)S(1)}, u32[]{:S(2)}, u32[]{:S(2)}) async-start(f32[8,32,128]{2,1,0:T(8,128)} %chain.1), calls=%async_computation.2 | async-start | bytes 262144 | tf_op jit(solution)/shard_map/all_to_all | solution.py:479
  90.8 24.6 %copy-start = (bf16[4,512,512]{2,1,0:T(8,128)(2,1)S(1)}, bf16[4,512,512]{2,1,0:T(8,128)(2,1)}, u32[]{:S(2)}) copy-start(bf16[4,512,512]{2,1,0:T(8,128)(2,1)} %get-tuple-element.47.restore.refs_8_) | copy-start | bytes 6291460
  96.4 11.7 %collective-permute-start.10 = (bf16[256,512]{1,0:T(8,128)(2,1)S(1)}, bf16[256,512]{1,0:T(8,128)(2,1)S(1)}, u32[]{:S(2)}, u32[]{:S(2)}) collective-permute-start(bf16[256,512]{1,0:T(8,128)(2,1)S(1)} %get-tuple-element.55.refs_2_), channel_id=1, source_target_pairs={{0,7},{1,0},{2,1},{3,2},{4,3},{5,4},{6,5},{7,6},{8,15},{9,8},{10,9... | collective-permute-start | bytes 786440 | tf_op jit(solution)/shard_map/ppermute | solution.py:418
  98.6 15.3 %collective-permute-start.7 = (bf16[256,512]{1,0:T(8,128)(2,1)S(1)}, bf16[256,512]{1,0:T(8,128)(2,1)S(1)}, u32[]{:S(2)}, u32[]{:S(2)}) collective-permute-start(bf16[256,512]{1,0:T(8,128)(2,1)S(1)} %get-tuple-element.54.refs_1_), channel_id=1, source_target_pairs={{0,8},{8,16},{16,24},{24,32},{32,40},{40,48},{48,56},{56,64},{64,7... | collective-permute-start | bytes 786440 | tf_op jit(solution)/shard_map/ppermute | solution.py:418
  98.6 15.3 %collective-permute-start.8 = (bf16[256,512]{1,0:T(8,128)(2,1)S(1)}, bf16[256,512]{1,0:T(8,128)(2,1)S(1)}, u32[]{:S(2)}, u32[]{:S(2)}) collective-permute-start(bf16[256,512]{1,0:T(8,128)(2,1)S(1)} %get-tuple-element.53.refs_0_), channel_id=1, source_target_pairs={{0,248},{8,0},{16,8},{24,16},{32,24},{40,32},{48,40},{56,48},{64,5... | collective-permute-start | bytes 786440 | tf_op jit(solution)/shard_map/ppermute | solution.py:418
  103.3 12.0 %collective-permute-start.9 = (bf16[256,512]{1,0:T(8,128)(2,1)S(1)}, bf16[256,512]{1,0:T(8,128)(2,1)S(1)}, u32[]{:S(2)}, u32[]{:S(2)}) collective-permute-start(bf16[256,512]{1,0:T(8,128)(2,1)S(1)} %get-tuple-element.56.refs_3_), channel_id=1, source_target_pairs={{0,1},{1,2},{2,3},{3,4},{4,5},{5,6},{6,7},{7,0},{8,9},{9,10},{10,1... | collective-permute-start | bytes 786440 | tf_op jit(solution)/shard_map/ppermute | solution.py:418
Sparse Core Ops, SparseCore 0:
  9.9 61.1 all-gather.1

commit v2 on v1

--- a/solution.py
+++ b/solution.py
@@ -1,3 +1,5 @@
+import functools
+
 import jax
 import jax.numpy as jnp
 from jax import lax
@@ -135,26 +137,20 @@
 
 
 def residual_kernel(scale, *refs):
-    d = pl.program_id(0)
     faces = scale.shape[0]
     canon, beside = refs[:faces], refs[faces : 2 * faces]
-    ordered, handoff, averaged, coarse, heat, total = refs[2 * faces :]
-    for i in range(faces):
-
-        @pl.when(d == i)
-        def _():
-            value = (scale[i] * sum_across(canon[i], beside[i], i)).astype(BF16)
-            averaged[0] = value
-            term = times(value, ordered[i])
-            total[...] = term if i == 0 else total[...] + term
-
-    @pl.when(d == faces - 1)
-    def _():
-        rounded = total[...].astype(BF16)
-        coarse[...] = rounded
-        primal = rounded.shape[1]
-        start = pl.multiple_of(lax.axis_index("coarse") * primal, primal)
-        heat[...] = times(rounded, handoff[pl.ds(start, primal), :])
+    ordered, handoff, averaged, coarse, heat = refs[2 * faces :]
+    total = None
+    for d in range(faces):
+        value = (scale[d] * sum_across(canon[d], beside[d], d)).astype(BF16)
+        averaged[d] = value
+        term = times(value, ordered[d])
+        total = term if total is None else total + term
+    rounded = total.astype(BF16)
+    coarse[...] = rounded
+    primal = rounded.shape[1]
+    start = pl.multiple_of(lax.axis_index("coarse") * primal, primal)
+    heat[...] = times(rounded, handoff[pl.ds(start, primal), :])
 
 
 def residuals(scale, canon, beside, ordered, handoff):
@@ -168,10 +164,9 @@
             jax.ShapeDtypeStruct((samples, primal), BF16),
             jax.ShapeDtypeStruct((samples, channels), F32),
         ],
-        grid=(faces,),
+        grid=(1,),
         in_specs=[pl.BlockSpec(memory_space=pltpu.SMEM)] + [IN_VMEM] * (2 * faces + 2),
-        out_specs=[pl.BlockSpec((1, samples, size), lambda d: (d, 0, 0)), IN_VMEM, IN_VMEM],
-        scratch_shapes=[pltpu.VMEM((samples, primal), F32)],
+        out_specs=[resident((faces, samples, size)), IN_VMEM, IN_VMEM],
         compiler_params=params(8),
         cost_estimate=cost(
             2 * faces * samples * size * primal, 6 * faces * samples * size + 2 * faces * size * primal
@@ -187,113 +182,195 @@
     out[...] = jnp.broadcast_to(total[None], out.shape)
 
 
-def shared_sum(inflow, lines):
+def shared_sum(inflow, copies):
     members, share, channels = inflow.shape
     return pl.pallas_call(
         share_kernel,
-        out_shape=jax.ShapeDtypeStruct((lines, share, channels), F32),
-        compiler_params=params(8),
-        cost_estimate=cost(members * share * channels, 4 * (lines + members) * share * channels),
+        out_shape=jax.ShapeDtypeStruct((copies, share, channels), F32),
+        compiler_params=params(8),
+        cost_estimate=cost(members * share * channels, 4 * (copies + members) * share * channels),
         name="shared_sum",
     )(inflow)
 
 
-def dual_kernel(slot, scale, averaged, restore, sort, mask, inverse, out, masked):
-    i = pl.program_id(0)
-    faces, _, size = masked.shape
-
-    @pl.when(i < faces)
-    def _():
-        local = times(averaged[0], restore[0])
-        masked[slot[i]] = (local * mask[slot[i]]).astype(BF16)
-
-    @pl.when(i >= faces)
-    def _():
-        d = i - faces
-        total = None
-        for g in range(faces):
-            term = times(masked[g], inverse[g * size : (g + 1) * size, :])
-            total = term if total is None else total + term
-        high, low = split(total * (mask[slot[d]] * scale[d]))
-        out[0] = times(high, sort[0]) + times(low, sort[0])
-
-
-def dual(slot, scale, averaged, sort, restore, mask, inverse):
+def local_kernel(slot, averaged, restore, mask, out):
+    for d in range(averaged.shape[0]):
+        s = slot[d]
+        out[s] = (times(averaged[d], restore[d]) * mask[s]).astype(BF16)
+
+
+def masked_local(slot, averaged, restore, mask):
     faces, samples, size = averaged.shape
-
-    def first(i):
-        return jnp.minimum(i, faces - 1)
-
-    def second(i):
-        return jnp.maximum(i - faces, 0)
-
-    return pl.pallas_call(
-        dual_kernel,
-        out_shape=pltpu.HBM(averaged.shape, F32),
+    return pl.pallas_call(
+        local_kernel,
+        out_shape=pltpu.HBM(averaged.shape, BF16),
         grid_spec=pltpu.PrefetchScalarGridSpec(
             num_scalar_prefetch=1,
-            grid=(2 * faces,),
+            grid=(1,),
+            in_specs=[resident(averaged.shape), resident(restore.shape), resident(mask.shape)],
+            out_specs=resident(averaged.shape),
+        ),
+        compiler_params=params(12),
+        cost_estimate=cost(
+            2 * faces * samples * size * size, 4 * faces * samples * size + 2 * faces * size * size
+        ),
+        name="masked_local",
+    )(slot, in_hbm(averaged), in_hbm(restore), mask)
+
+
+def dual_kernel(first, slot, scale, masked, sort, mask, inverse, out):
+    d = first + pl.program_id(0)
+    faces, _, size = masked.shape
+    total = None
+    for g in range(faces):
+        term = times(masked[g], inverse[g * size : (g + 1) * size, :])
+        total = term if total is None else total + term
+    high, low = split(total * (mask[slot[d]] * scale[d]))
+    out[0] = times(high, sort[0]) + times(low, sort[0])
+
+
+def dual(first, count, slot, scale, masked, sort, mask, inverse):
+    faces, samples, size = masked.shape
+    return pl.pallas_call(
+        functools.partial(dual_kernel, first),
+        out_shape=pltpu.HBM((count, samples, size), F32),
+        grid_spec=pltpu.PrefetchScalarGridSpec(
+            num_scalar_prefetch=1,
+            grid=(count,),
             in_specs=[
                 pl.BlockSpec(memory_space=pltpu.SMEM),
-                pl.BlockSpec((1, samples, size), lambda i, slot: (first(i), 0, 0)),
-                pl.BlockSpec((1, size, size), lambda i, slot: (first(i), 0, 0)),
-                pl.BlockSpec((1, size, size), lambda i, slot: (second(i), 0, 0)),
+                resident(masked.shape),
+                pl.BlockSpec((1, size, size), lambda i, slot: (first + i, 0, 0)),
                 resident(mask.shape),
-                pl.BlockSpec((faces * size, size), lambda i, slot: (0, slot[second(i)])),
+                pl.BlockSpec((faces * size, size), lambda i, slot: (0, slot[first + i])),
             ],
-            out_specs=pl.BlockSpec((1, samples, size), lambda i, slot: (second(i), 0, 0)),
-            scratch_shapes=[pltpu.VMEM((faces, samples, size), BF16)],
+            out_specs=pl.BlockSpec((1, samples, size), lambda i, slot: (i, 0, 0)),
         ),
         compiler_params=params(16),
         cost_estimate=cost(
-            2 * samples * faces * size * (faces + 3) * size,
-            2 * faces * size * (faces + 2) * size + 6 * faces * samples * size,
-        ),
-        name="dual",
-    )(slot, scale, in_hbm(averaged), in_hbm(restore), in_hbm(sort), mask, in_hbm(inverse))
-
-
-def chain_kernel(inflow, transfer, out, state):
-    i = pl.program_id(0)
-    lines = inflow.shape[0]
-
-    @pl.when(i == 0)
-    def _():
-        state[...] = jnp.zeros_like(state)
-
+            2 * count * samples * size * (faces + 2) * size,
+            2 * count * size * (faces + 1) * size + 6 * faces * samples * size,
+        ),
+        name=f"dual{first}",
+    )(slot, scale, in_hbm(masked), in_hbm(sort), mask, in_hbm(inverse))
+
+
+DOUBLING = (4, 2, 1)
+DOUBLED_BITS = (0, 4, 2, 6, 1, 5, 3, 7)
+TINY = 1e-30
+
+
+def triple(value, high, low):
+    value_high, value_low = split(value)
+    return times(value_high, high) + (times(value_low, high) + times(value_high, low))
+
+
+def maps_kernel(transfer, maps, product):
+    group, channels, _ = transfer.shape
+    own = lax.rem(lax.axis_index("sub"), group)
+    total = None
+    for k in range(group):
+        bits = jnp.bitwise_xor(own, k)
+        place = (bits & 1) * 4 + (bits & 2) + lax.shift_right_logical(bits, 2)
+        value = transfer[place]
+        high, low = split(value)
+        maps[2 * k] = high
+        maps[2 * k + 1] = low
+        largest = jnp.max(jnp.abs(value), axis=1, keepdims=True)
+        largest = jnp.maximum(jnp.max(largest, axis=0, keepdims=True), TINY)
+        product[0, pl.ds(channels + k, 1), :] = jnp.broadcast_to(largest, (1, channels))
+        scaled = value / largest
+        total = scaled if total is None else triple(total, *split(scaled))
+    product[0, pl.ds(0, channels), :] = total
+
+
+def group_maps(transfer):
+    group, channels, _ = transfer.shape
+    return pl.pallas_call(
+        maps_kernel,
+        out_shape=[
+            pltpu.HBM((2 * group, channels, channels), BF16),
+            jax.ShapeDtypeStruct((1, channels + group, channels), F32),
+        ],
+        grid=(1,),
+        in_specs=[resident(transfer.shape)],
+        out_specs=[
+            resident((2 * group, channels, channels)),
+            resident((1, channels + group, channels)),
+        ],
+        compiler_params=params(8),
+        cost_estimate=cost(6 * group * channels**3, 8 * group * channels * channels),
+        name="group_maps",
+    )(transfer)
+
+
+def run_lines(state, inflow, maps, count):
     def step(k, value):
-        high, low = split(value)
-        map_high, map_low = split(transfer[k])
-        value = times(high, map_high) + (times(low, map_high) + times(high, map_low))
-        return value + inflow[k]
-
-    ahead = jnp.clip(lax.axis_index("sub") - i * lines, 0, lines)
-    state[...] = lax.fori_loop(0, ahead, step, state[...])
-
-    @pl.when(i == pl.num_programs(0) - 1)
-    def _():
-        out[...] = jnp.broadcast_to(state[...][None], out.shape)
-
-
-def chain(inflow, transfer, members):
+        return triple(value, maps[2 * k], maps[2 * k + 1]) + inflow[k]
+
+    return lax.fori_loop(0, count, step, state)
+
+
+def outflow_kernel(inflow, maps, out):
     lines, samples, channels = inflow.shape
-    steps = 4
-    return pl.pallas_call(
-        chain_kernel,
-        out_shape=jax.ShapeDtypeStruct((members, samples, channels), F32),
-        grid=(steps,),
+    state = jnp.zeros((samples, channels), F32)
+    for k in range(lines):
+        state = triple(state, maps[2 * k], maps[2 * k + 1]) + inflow[k] if k else inflow[0]
+    out[...] = jnp.broadcast_to(state[None], out.shape)
+
+
+def group_outflow(inflow, maps, copies):
+    lines, samples, channels = inflow.shape
+    return pl.pallas_call(
+        outflow_kernel,
+        out_shape=jax.ShapeDtypeStruct((copies, samples, channels), F32),
+        grid=(1,),
+        in_specs=[resident(inflow.shape), resident(maps.shape)],
+        out_specs=IN_VMEM,
+        compiler_params=params(8),
+        cost_estimate=cost(
+            6 * lines * samples * channels * channels, 4 * lines * channels * (samples + channels)
+        ),
+        name="group_outflow",
+    )(inflow, in_hbm(maps))
+
+
+def carried_kernel(outflow, products, inflow, maps, out):
+    lines, samples, channels = inflow.shape
+    line = lax.axis_index("sub")
+    group = lax.div(line, lines)
+
+    def enter(a, value):
+        place = jnp.bitwise_xor(group, a)
+        value = triple(value, *split(products[place, pl.ds(0, channels), :]))
+        for k in range(lines):
+            value = value * products[place, pl.ds(channels + k, 1), :]
+        return value + outflow[a]
+
+    state = lax.fori_loop(0, group, enter, jnp.zeros((samples, channels), F32))
+    state = run_lines(state, inflow, maps, lax.rem(line, lines))
+    out[...] = jnp.broadcast_to(state[None], out.shape)
+
+
+def carried_states(outflow, products, inflow, maps, copies):
+    lines, samples, channels = inflow.shape
+    return pl.pallas_call(
+        carried_kernel,
+        out_shape=jax.ShapeDtypeStruct((copies, samples, channels), F32),
+        grid=(1,),
         in_specs=[
-            pl.BlockSpec((lines // steps, samples, channels), lambda i: (i, 0, 0)),
-            pl.BlockSpec((lines // steps, channels, channels), lambda i: (i, 0, 0)),
+            resident(outflow.shape),
+            resident(products.shape),
+            resident(inflow.shape),
+            resident(maps.shape),
         ],
         out_specs=IN_VMEM,
-        scratch_shapes=[pltpu.VMEM((samples, channels), F32)],
-        compiler_params=params(8),
-        cost_estimate=cost(
-            6 * lines * samples * channels * channels, 4 * lines * channels * (samples + channels)
-        ),
-        name="chain",
-    )(inflow, in_hbm(transfer))
+        compiler_params=params(8),
+        cost_estimate=cost(
+            6 * lines * samples * channels * channels, 8 * lines * channels * (samples + channels)
+        ),
+        name="carried_states",
+    )(outflow, products, inflow, in_hbm(maps))
 
 
 def line_kernel(gathered, inverse, out):
@@ -323,7 +400,7 @@
     )(gathered, in_hbm(inverse))
 
 
-def extend_kernel(scale, base, carried, coupling, ordered_columns, dual_part, *rest):
+def extend_kernel(scale, base, carried, coupling, ordered_columns, dual0, dual1, *rest):
     outs, answer = rest[:-1], rest[-1]
     d = pl.program_id(0)
 
@@ -333,17 +410,18 @@
         term = times(high, coupling[...]) + times(low, coupling[...])
         answer[...] = (base[...] + term).astype(BF16)
 
-    value = dual_part[0] + scale[d] * times(answer[...], ordered_columns[0])
-    value = value.astype(BF16)
+    value = scale[d] * times(answer[...], ordered_columns[0])
+    half = len(outs) // 2
     for i, out in enumerate(outs):
 
         @pl.when(d == i)
         def _():
-            out[...] = value
-
-
-def extend(scale, base, carried, coupling, ordered_columns, dual_part):
-    faces, samples, size = dual_part.shape
+            out[...] = ((dual0 if i < half else dual1)[0] + value).astype(BF16)
+
+
+def extend(scale, base, carried, coupling, ordered_columns, dual0, dual1):
+    half, samples, size = dual0.shape
+    faces = 2 * half
     primal = base.shape[1]
     channels = carried.shape[1]
     return pl.pallas_call(
@@ -356,7 +434,8 @@
             IN_VMEM,
             resident((channels, primal)),
             pl.BlockSpec((1, primal, size), lambda d: (d, 0, 0)),
-            pl.BlockSpec((1, samples, size), lambda d: (d, 0, 0)),
+            pl.BlockSpec((1, samples, size), lambda d: (jnp.minimum(d, half - 1), 0, 0)),
+            pl.BlockSpec((1, samples, size), lambda d: (jnp.maximum(d - half, 0), 0, 0)),
         ],
         out_specs=[IN_VMEM] * faces,
         scratch_shapes=[pltpu.VMEM((samples, primal), BF16)],
@@ -365,7 +444,7 @@
             2 * faces * samples * size * primal, 6 * faces * samples * size + 2 * faces * size * primal
         ),
         name="extend",
-    )(scale, base, carried, in_hbm(coupling), in_hbm(ordered_columns), in_hbm(dual_part))
+    )(scale, base, carried, in_hbm(coupling), in_hbm(ordered_columns), in_hbm(dual0), in_hbm(dual1))
 
 
 def finish_kernel(slot, *refs):
@@ -400,13 +479,17 @@
     )(slot, *weighted, *beside, restore)
 
 
+GROUP = 8
 GATHER_STAGES = (2, 1, 4)
 GATHER_BITS = (0, 2, 1, 3, 4, 6, 5, 7)
 
 
-def gather_stage(value, bit):
-    pairs = [(i, i ^ bit) for i in range(lax.axis_size("coarse"))]
-    return lax.ppermute(value, "coarse", pairs)
+def exchange(value, axis, bit):
+    return lax.ppermute(value, axis, [(i, i ^ bit) for i in range(lax.axis_size(axis))])
+
+
+def doubled(value, axis, bit):
+    return jnp.concatenate([value, exchange(value, axis, bit)])
 
 
 def neighbours(faces):
@@ -447,7 +530,12 @@
     lines, members = lax.axis_size("sub"), lax.axis_size("coarse")
     share = samples // members
 
-    transfers = lax.all_gather(chain_transfer[0], "sub")
+    groups = lines // GROUP
+    inside = [[a * GROUP + b for b in range(GROUP)] for a in range(groups)]
+    between = [[a * GROUP + b for a in range(groups)] for b in range(GROUP)]
+    transfer = chain_transfer
+    for bit in DOUBLING:
+        transfer = doubled(transfer, "sub", bit)
 
     canon = to_canonical(slot, parts, order)
     beside = neighbours(canon)
@@ -456,30 +544,44 @@
     averaged, coarse_residual, heat = residuals(
         scale, canon, beside, ordered, thermal_handoff[0]
     )
-
-    channels = heat.shape[1]
-    gathered = coarse_residual[None]
-    received = gather_stage(gathered, GATHER_STAGES[0])
-    inflow = lax.all_to_all(heat.reshape(members, share, channels), "coarse", 0, 0)
-    inflow = shared_sum(inflow, lines)
-    averaged, received, inflow = lax.optimization_barrier((averaged, received, inflow))
-    inflow = lax.all_to_all(inflow, "sub", 0, 0)
-    gathered = jnp.concatenate([gathered, received])
-    received = gather_stage(gathered, GATHER_STAGES[1])
-
     positions = lax.broadcasted_iota(jnp.int32, (vertex_unknowns.shape[2], faces * size), 1)
     hits = jnp.sum((vertex_unknowns[0, 0][:, None] == positions).astype(F32), axis=0)
     mask = (1.0 - hits).reshape(faces, 1, size)
-    dual_part = dual(slot, scale, averaged, sort, restore, mask, front_inverse[0, 0])
-
-    inflow, received, dual_part = lax.optimization_barrier((inflow, received, dual_part))
+
+    channels = heat.shape[1]
+    gathered = coarse_residual[None]
+    received = exchange(gathered, "coarse", GATHER_STAGES[0])
+    inflow = lax.all_to_all(heat.reshape(members, share, channels), "coarse", 0, 0)
+    masked = masked_local(slot, averaged, restore, mask)
+    inflow, masked = lax.optimization_barrier((inflow, masked))
+    inflow = shared_sum(inflow, GROUP)
+    masked, inflow = lax.optimization_barrier((masked, inflow))
+
+    inflow = lax.all_to_all(inflow, "sub", 0, 0, axis_index_groups=inside)
+    half = faces // 2
+    dual0 = dual(0, half, slot, scale, masked, sort, mask, front_inverse[0, 0])
+    transfer, received, dual0 = lax.optimization_barrier((transfer, received, dual0))
+    maps, product = group_maps(transfer)
+    others = exchange(product, "sub", GROUP)
     gathered = jnp.concatenate([gathered, received])
-    gathered = jnp.concatenate([gathered, gather_stage(gathered, GATHER_STAGES[2])])
-    carried = chain(inflow, transfers, members)
+    received = exchange(gathered, "coarse", GATHER_STAGES[1])
+    inflow, maps, masked = lax.optimization_barrier((inflow, maps, masked))
+
+    outflow = group_outflow(inflow, maps, groups)
+    masked, others, outflow = lax.optimization_barrier((masked, others, outflow))
+    outflow = lax.all_to_all(outflow, "sub", 0, 0, axis_index_groups=between)
+    product = jnp.concatenate([product, others])
+    others = exchange(product, "sub", 2 * GROUP)
+    dual1 = dual(half, half, slot, scale, masked, sort, mask, front_inverse[0, 0])
+    outflow, others, received, dual1 = lax.optimization_barrier((outflow, others, received, dual1))
+    product = jnp.concatenate([product, others])
+    gathered = jnp.concatenate([gathered, received])
+    gathered = doubled(gathered, "coarse", GATHER_STAGES[2])
+    carried = carried_states(outflow, product, inflow, maps, members)
     carried = lax.all_to_all(carried, "coarse", 0, 0).reshape(samples, channels)
     base = line_base(gathered, coarse_inverse[0])
 
-    weighted = extend(scale, base, carried, coupling_in[0], ordered_columns, dual_part)
+    weighted = extend(scale, base, carried, coupling_in[0], ordered_columns, dual0, dual1)
     beside = neighbours(weighted)
     return finish(slot, weighted, beside, restore)[None, None]
 

time: 126 us -> 121 us (0.960)
  between operations: 13.5 us -> 0.21 us
  starting transfers between devices: 40.9 us -> 51 us
  waiting for transfers between devices: 32.2 us -> 24.8 us
  Pallas kernels: 36.6 us -> 41.8 us
    ppermute x3 -> x8, waiting for transfers between devices: 3.85 us -> 13.7 us  [exchange(): lax.ppermute(value, axis, [(i, i ^ bit) for i in range(lax.axis_size(axis...]
    ppermute x3 -> x8, starting transfers between devices: 5.55 us -> 14.5 us  [exchange(): lax.ppermute(value, axis, [(i, i ^ bit) for i in range(lax.axis_size(axis...]
    ppermute x8, waiting for transfers between devices: 16.7 us -> 9.79 us  [shifted(): return lax.ppermute(value, axis, pairs)]
    pallas_call x3 -> x7, Pallas kernels: 16.7 us -> 22.4 us  [the longest x2 11.3 us: dual(): pl.pallas_call(functools.partial(dual_kernel, first), out_shape=pltpu.HBM...]
    all_to_all x1 -> x2, waiting for transfers between devices: 5.49 us -> 1.34 us  [the longest x1 1.33 us: per_device(): inflow = lax.all_to_all(inflow, 'sub', 0, 0, axis_index_groups=inside)]
    all_to_all x1, waiting for transfers between devices: 3.3 us -> 0.01 us  [per_device(): lax.all_to_all(heat.reshape(members, share, channels), 'coarse', 0, 0)]
    all_to_all x1, starting transfers between devices: 3.5 us -> 5.8 us  [per_device(): lax.all_to_all(heat.reshape(members, share, channels), 'coarse', 0, 0)]
    all_to_all x1, waiting for transfers between devices: 2.22 us -> 0.03 us  [per_device(): carried = lax.all_to_all(carried, 'coarse', 0, 0).reshape(samples, channels)]
  transfers between devices with their start and end apart: 15 -> 20, of which waited for: 8 -> 6; matrix products, arithmetic and copies ran while one was open for 0% -> 0% of each run, Pallas kernels for 24% -> 26%
where the time goes in v2:
time: 121 us; the launch traced here: 120 us
  starting transfers between devices  51 us (42%)
  Pallas kernels  41.8 us (35%)
  waiting for transfers between devices  24.8 us (20%)
  local copies, waits for them, and re-layouts  1.33 us (1%)
    ppermute x8, starting transfers between devices, shifted(): return lax.ppermute(value, axis, pairs)  19 us
    ppermute x8, starting transfers between devices, exchange(): lax.ppermute(value, axis, [(i, i ^ bit) for i in range(lax.axis_size(axis...  14.5 us
    ppermute x8, waiting for transfers between devices, exchange(): lax.ppermute(value, axis, [(i, i ^ bit) for i in range(lax.axis_size(axis...  13.7 us
    pallas_call x2, Pallas kernels, dual(): pl.pallas_call(functools.partial(dual_kernel, first), out_shape=pltpu.HBM...  11.3 us
    ppermute x8, waiting for transfers between devices, shifted(): return lax.ppermute(value, axis, pairs)  9.79 us
    all_to_all x1, starting transfers between devices, per_device(): lax.all_to_all(heat.reshape(members, share, channels), 'coarse', 0, 0)  5.8 us
    pallas_call x1, Pallas kernels, tables(): pl.pallas_call(tables_kernel, out_shape=[pltpu.HBM((faces, size, size), B...  5.27 us
    all_to_all x1, starting transfers between devices, per_device(): outflow = lax.all_to_all(outflow, 'sub', 0, 0, axis_index_groups=between)  4.68 us
  transfers between devices with their start and end apart: 20, of which 6 were waited for; matrix products, arithmetic and copies ran while one was open for 0% of the time, Pallas kernels for 26%

profile of v2, /device:TPU:2, one launch (start us, length us, event | category | flops | bytes accessed | tf_op | source)
XLA Modules:
  0.0 119.8 jit_solution(17253803541688237324)
XLA Ops:
  0.7 3.5 %canon.1 = (bf16[256,512]{1,0:T(8,128)(2,1)S(1)}, bf16[256,512]{1,0:T(8,128)(2,1)S(1)}, bf16[256,512]{1,0:T(8,128)(2,1)S(1)}, bf16[256,512]{1,0:T(8,128)(2,1)S(1)}) custom-call(s32[4]{0:T(128)S(1)} %bitcast.24, bf16[4,256,512]{2,1,0:T(8,128)(2,1)} %bitcast.39, s32[4,512]{1,0:T(4,128)} %bitcast.41), custom_call_target="tpu_custom_call" | custom-call | flops 536870912 | bytes 2097152 | tf_op jit(solution)/shard_map/canon/pallas_call | solution.py:65
  4.3 5.8 %collective-permute-start.1 = (bf16[256,512]{1,0:T(8,128)(2,1)S(1)}, bf16[256,512]{1,0:T(8,128)(2,1)S(1)}, u32[]{:S(2)}, u32[]{:S(2)}) collective-permute-start(bf16[256,512]{1,0:T(8,128)(2,1)S(1)} %get-tuple-element.48.refs_0_), channel_id=1, source_target_pairs={{0,248},{8,0},{16,8},{24,16},{32,24},{40,32},{48,40},{56,48},{64,5... | collective-permute-start | bytes 786440 | tf_op jit(solution)/shard_map/ppermute | solution.py:501
  10.1 1.6 %collective-permute-start.2 = (bf16[256,512]{1,0:T(8,128)(2,1)S(1)}, bf16[256,512]{1,0:T(8,128)(2,1)S(1)}, u32[]{:S(2)}, u32[]{:S(2)}) collective-permute-start(bf16[256,512]{1,0:T(8,128)(2,1)S(1)} %get-tuple-element.51.refs_3_), channel_id=1, source_target_pairs={{0,1},{1,2},{2,3},{3,4},{4,5},{5,6},{6,7},{7,0},{8,9},{9,10},{10,1... | collective-permute-start | bytes 786440 | tf_op jit(solution)/shard_map/ppermute | solution.py:501
  11.7 2.6 %collective-permute-start.3 = (bf16[256,512]{1,0:T(8,128)(2,1)S(1)}, bf16[256,512]{1,0:T(8,128)(2,1)S(1)}, u32[]{:S(2)}, u32[]{:S(2)}) collective-permute-start(bf16[256,512]{1,0:T(8,128)(2,1)S(1)} %get-tuple-element.50.refs_2_), channel_id=1, source_target_pairs={{0,7},{1,0},{2,1},{3,2},{4,3},{5,4},{6,5},{7,6},{8,15},{9,8},{10,9... | collective-permute-start | bytes 786440 | tf_op jit(solution)/shard_map/ppermute | solution.py:501
  14.2 5.2 %collective-permute-start.4 = (f32[1,128,128]{2,1,0:T(8,128)}, f32[1,128,128]{2,1,0:T(8,128)S(1)}, u32[]{:S(2)}, u32[]{:S(2)}) collective-permute-start(f32[1,128,128]{2,1,0:T(8,128)} %param.20), channel_id=1, source_target_pairs={{0,32},{8,40},{16,48},{24,56},{32,0},{40,8},{48,16},{56,24},{64,96... | collective-permute-start | bytes 196616 | tf_op jit(solution)/shard_map/ppermute | solution.py:488
  20.1 5.3 %tables.1 = (bf16[4,512,512]{2,1,0:T(8,128)(2,1)}, bf16[4,512,512]{2,1,0:T(8,128)(2,1)}, bf16[4,512,256]{2,1,0:T(8,128)(2,1)S(1)}, bf16[4,256,512]{2,1,0:T(8,128)(2,1)}) custom-call(s32[4]{0:T(128)S(1)} %bitcast.25, s32[4,512]{1,0:T(4,128)} %bitcast.42, bf16[4,512,256]{2,1,0:T(8,128)(2,1)} %bitcast.40), custom_call_target="tpu_custom_call" | custom-call | flops 1073741824 | bytes 7340032 | tf_op jit(solution)/shard_map/tables/pallas_call | solution.py:98
  25.4 1.5 %collective-permute-done.4 = f32[1,128,128]{2,1,0:T(8,128)S(1)} collective-permute-done((f32[1,128,128]{2,1,0:T(8,128)}, f32[1,128,128]{2,1,0:T(8,128)S(1)}, u32[]{:S(2)}, u32[]{:S(2)}) %collective-permute-start.4) | collective-permute-done | bytes 65568 | tf_op jit(solution)/shard_map/ppermute | solution.py:488
  28.4 5.0 %collective-permute-done.5 = f32[2,128,128]{2,1,0:T(8,128)S(1)} collective-permute-done((f32[2,128,128]{2,1,0:T(8,128)S(1)}, f32[2,128,128]{2,1,0:T(8,128)S(1)}, u32[]{:S(2)}, u32[]{:S(2)}) %collective-permute-start.5) | collective-permute-done | bytes 131104 | tf_op jit(solution)/shard_map/ppermute | solution.py:488
  33.6 2.1 %residuals.1 = (bf16[4,256,512]{2,1,0:T(8,128)(2,1)}, bf16[256,256]{1,0:T(8,128)(2,1)S(1)}, f32[256,128]{1,0:T(8,128)}) custom-call(f32[4]{0:T(128)S(1)} %bitcast.30, bf16[256,512]{1,0:T(8,128)(2,1)S(1)} %get-tuple-element.48.refs_0_, bf16[256,512]{1,0:T(8,128)(2,1)S(1)} %get-tuple-element.49.refs_1_, bf16[256,512]{1,0:T(8,128)(2,1)S(1)} %get-tuple-element.50.refs_2_, ...), custom_call_target="tpu_custom_call" | custom-call | flops 268435456 | bytes 4194304 | tf_op jit(solution)/shard_map/residuals/pallas_call | solution.py:160
  35.7 5.8 %all-to-all-start = ((f32[8,32,128]{2,1,0:T(8,128)}), f32[8,32,128]{2,1,0:T(8,128)S(1)}, u32[]{:S(2)}, u32[]{:S(2)}) async-start(f32[8,32,128]{2,1,0:T(8,128)} %bitcast.7), calls=%async_computation | async-start | bytes 262144 | tf_op jit(solution)/shard_map/all_to_all | solution.py:554
  41.5 3.5 %collective-permute-start.7 = (bf16[1,256,256]{2,1,0:T(8,128)(2,1)S(1)}, bf16[1,256,256]{2,1,0:T(8,128)(2,1)S(1)}, u32[]{:S(2)}, u32[]{:S(2)}) collective-permute-start(bf16[1,256,256]{2,1,0:T(8,128)(2,1)S(1)} %bitcast.15), channel_id=1, source_target_pairs={{0,2},{1,3},{2,0},{3,1},{4,6},{5,7},{6,4},{7,5},{8,10},{9,11},{10,... | collective-permute-start | bytes 393224 | tf_op jit(solution)/shard_map/ppermute | solution.py:488
  45.0 4.2 %masked_local.1.masked = bf16[4,256,512]{2,1,0:T(8,128)(2,1)} custom-call(s32[4]{0:T(128)S(1)} %bitcast.26, bf16[4,256,512]{2,1,0:T(8,128)(2,1)} %get-tuple-element.56.averaged, bf16[4,512,512]{2,1,0:T(8,128)(2,1)} %get-tuple-element.57.restore.refs_8_, f32[4,1,512]{2,1,0:T(1,128)S(1)} %bitcast.21), custom_call_target="tpu_custom_call" | custom-call | flops 536870912 | bytes 4194304 | tf_op jit(solution)/shard_map/masked_local/pallas_call | solution.py:204
  49.9 3.6 %all-to-all-start.1 = ((f32[8,32,128]{2,1,0:T(8,128)}), f32[8,32,128]{2,1,0:T(8,128)S(1)}, u32[]{:S(2)}, u32[]{:S(2)}) async-start(f32[8,32,128]{2,1,0:T(8,128)} %shared_sum.1), calls=%async_computation.1 | async-start | bytes 262144 | tf_op jit(solution)/shard_map/all_to_all | solution.py:560
  53.6 5.8 %dual0.1 = f32[2,256,512]{2,1,0:T(8,128)} custom-call(s32[4]{0:T(128)S(1)} %bitcast.27, f32[4]{0:T(128)S(1)} %bitcast.31, bf16[4,256,512]{2,1,0:T(8,128)(2,1)} %masked_local.1.masked, bf16[4,512,512]{2,1,0:T(8,128)(2,1)} %get-tuple-element.61.sort, f32[4,1,512]{2,1,0:T(1,128)S(1)} %bitcast.22, bf16[2048,2048]{1,0:T(8,128)(2,1)} %bitcast.34), custom_call_target="tpu_custom_call" | custom-call | flops 1610612736 | bytes 8388608 | tf_op jit(solution)/shard_map/dual0/pallas_call | solution.py:234
  59.3 1.6 %group_maps.1 = (bf16[16,128,128]{2,1,0:T(8,128)(2,1)}, f32[1,136,128]{2,1,0:T(8,128)S(1)}) custom-call(f32[8,128,128]{2,1,0:T(8,128)S(1)} %pad_maximum_fusion.1.transfer), custom_call_target="tpu_custom_call" | custom-call | flops 100663296 | bytes 1048576 | tf_op jit(solution)/shard_map/group_maps/pallas_call | solution.py:289
  62.2 1.3 %all-to-all-done.1.inflow = f32[8,32,128]{2,1,0:T(8,128)S(1)} async-done(((f32[8,32,128]{2,1,0:T(8,128)}), f32[8,32,128]{2,1,0:T(8,128)S(1)}, u32[]{:S(2)}, u32[]{:S(2)}) %all-to-all-start.1) | async-done | bytes 131104 | tf_op jit(solution)/shard_map/all_to_all | solution.py:560
  63.5 2.7 %group_outflow.1 = f32[4,32,128]{2,1,0:T(8,128)} custom-call(f32[8,32,128]{2,1,0:T(8,128)S(1)} %all-to-all-done.1.inflow, bf16[16,128,128]{2,1,0:T(8,128)(2,1)} %get-tuple-element.69.maps), custom_call_target="tpu_custom_call" | custom-call | flops 25165824 | bytes 655360 | tf_op jit(solution)/shard_map/group_outflow/pallas_call | solution.py:324
  66.3 2.2 %collective-permute-start.9 = (f32[2,136,128]{2,1,0:T(8,128)S(1)}, f32[2,136,128]{2,1,0:T(8,128)S(1)}, u32[]{:S(2)}, u32[]{:S(2)}) collective-permute-start(f32[2,136,128]{2,1,0:T(8,128)S(1)} %pad_maximum_fusion.6), channel_id=1, source_target_pairs={{0,128},{8,136},{16,144},{24,152},{32,160},{40,168},{48,176},{56,1... | collective-permute-start | bytes 417800 | tf_op jit(solution)/shard_map/ppermute | solution.py:488
  68.5 4.7 %all-to-all-start.2 = ((f32[4,32,128]{2,1,0:T(8,128)}), f32[4,32,128]{2,1,0:T(8,128)S(1)}, u32[]{:S(2)}, u32[]{:S(2)}) async-start(f32[4,32,128]{2,1,0:T(8,128)} %group_outflow.1), calls=%async_computation.2 | async-start | bytes 131072 | tf_op jit(solution)/shard_map/all_to_all | solution.py:572
  73.2 5.6 %dual2.1.dual1 = f32[2,256,512]{2,1,0:T(8,128)} custom-call(s32[4]{0:T(128)S(1)} %bitcast.28, f32[4]{0:T(128)S(1)} %bitcast.32, bf16[4,256,512]{2,1,0:T(8,128)(2,1)} %masked_local.1.masked, bf16[4,512,512]{2,1,0:T(8,128)(2,1)} %get-tuple-element.61.sort, f32[4,1,512]{2,1,0:T(1,128)S(1)} %bitcast.23, bf16[2048,2048]{1,0:T(8,128)(2,1)} %bitcast.35), custom_call_target="tpu_custom_call" | custom-call | flops 1610612736 | bytes 8388608 | tf_op jit(solution)/shard_map/dual2/pallas_call | solution.py:234
  78.8 1.1 collective-permute-start.11
  80.0 1.9 %carried_states.1 = f32[8,32,128]{2,1,0:T(8,128)} custom-call(f32[4,32,128]{2,1,0:T(8,128)S(1)} %all-to-all-done.2.outflow, f32[4,136,128]{2,1,0:T(8,128)S(1)} %pad_maximum_fusion.3.products, f32[8,32,128]{2,1,0:T(8,128)S(1)} %all-to-all-done.1.inflow, bf16[16,128,128]{2,1,0:T(8,128)(2,1)} %get-tuple-element.69.maps), custom_call_target="tpu_custom_call" | custom-call | flops 25165824 | bytes 1310720 | tf_op jit(solution)/shard_map/carried_states/pallas_call | solution.py:357
  81.9 3.4 %all-to-all-start.3 = ((f32[8,32,128]{2,1,0:T(8,128)}), f32[8,32,128]{2,1,0:T(8,128)S(1)}, u32[]{:S(2)}, u32[]{:S(2)}) async-start(f32[8,32,128]{2,1,0:T(8,128)} %carried_states.1), calls=%async_computation.3 | async-start | bytes 262144 | tf_op jit(solution)/shard_map/all_to_all | solution.py:581
  85.2 7.1 %collective-permute-done.11 = bf16[4,256,256]{2,1,0:T(8,128)(2,1)S(1)} collective-permute-done((bf16[4,256,256]{2,1,0:T(8,128)(2,1)S(1)}, bf16[4,256,256]{2,1,0:T(8,128)(2,1)S(1)}, u32[]{:S(2)}, u32[]{:S(2)}) %collective-permute-start.11) | collective-permute-done | bytes 524320 | tf_op jit(solution)/shard_map/ppermute | solution.py:488
  92.5 1.7 %line_base.1.base = f32[256,256]{1,0:T(8,128)S(1)} custom-call(bf16[8,256,256]{2,1,0:T(8,128)(2,1)S(1)} %pad_maximum_fusion.gathered, bf16[2048,256]{1,0:T(8,128)(2,1)} %bitcast.36), custom_call_target="tpu_custom_call" | custom-call | flops 268435456 | bytes 2097152 | tf_op jit(solution)/shard_map/line_base/pallas_call | solution.py:389
  94.2 3.9 %extend.1 = (bf16[256,512]{1,0:T(8,128)(2,1)S(1)}, bf16[256,512]{1,0:T(8,128)(2,1)S(1)}, bf16[256,512]{1,0:T(8,128)(2,1)S(1)}, bf16[256,512]{1,0:T(8,128)(2,1)S(1)}) custom-call(f32[4]{0:T(128)S(1)} %bitcast.33, f32[256,256]{1,0:T(8,128)S(1)} %line_base.1.base, f32[256,128]{1,0:T(8,128)S(1)} %bitcast.20, bf16[128,256]{1,0:T(8,128)(2,1)} %bitcast.37, ...), custom_call_target="tpu_custom_call" | custom-call | flops 268435456 | bytes 4194304 | tf_op jit(solution)/shard_map/extend/pallas_call | solution.py:427
  98.1 4.7 %collective-permute-start.13 = (bf16[256,512]{1,0:T(8,128)(2,1)S(1)}, bf16[256,512]{1,0:T(8,128)(2,1)S(1)}, u32[]{:S(2)}, u32[]{:S(2)}) collective-permute-start(bf16[256,512]{1,0:T(8,128)(2,1)S(1)} %get-tuple-element.79.refs_0_), channel_id=1, source_target_pairs={{0,248},{8,0},{16,8},{24,16},{32,24},{40,32},{48,40},{56,48},{64,5... | collective-permute-start | bytes 786440 | tf_op jit(solution)/shard_map/ppermute | solution.py:501
  102.9 1.4 %collective-permute-start.14 = (bf16[256,512]{1,0:T(8,128)(2,1)S(1)}, bf16[256,512]{1,0:T(8,128)(2,1)S(1)}, u32[]{:S(2)}, u32[]{:S(2)}) collective-permute-start(bf16[256,512]{1,0:T(8,128)(2,1)S(1)} %get-tuple-element.82.refs_3_), channel_id=1, source_target_pairs={{0,1},{1,2},{2,3},{3,4},{4,5},{5,6},{6,7},{7,0},{8,9},{9,10},{10,1... | collective-permute-start | bytes 786440 | tf_op jit(solution)/shard_map/ppermute | solution.py:501
  104.3 2.7 %collective-permute-start.15 = (bf16[256,512]{1,0:T(8,128)(2,1)S(1)}, bf16[256,512]{1,0:T(8,128)(2,1)S(1)}, u32[]{:S(2)}, u32[]{:S(2)}) collective-permute-start(bf16[256,512]{1,0:T(8,128)(2,1)S(1)} %get-tuple-element.81.refs_2_), channel_id=1, source_target_pairs={{0,7},{1,0},{2,1},{3,2},{4,3},{5,4},{6,5},{7,6},{8,15},{9,8},{10,9... | collective-permute-start | bytes 786440 | tf_op jit(solution)/shard_map/ppermute | solution.py:501
  107.0 1.6 %collective-permute-done.13.refs_5_ = bf16[256,512]{1,0:T(8,128)(2,1)S(1)} collective-permute-done((bf16[256,512]{1,0:T(8,128)(2,1)S(1)}, bf16[256,512]{1,0:T(8,128)(2,1)S(1)}, u32[]{:S(2)}, u32[]{:S(2)}) %collective-permute-start.13) | collective-permute-done | bytes 262176 | tf_op jit(solution)/shard_map/ppermute | solution.py:501
  108.6 8.2 %collective-permute-done.14.refs_6_ = bf16[256,512]{1,0:T(8,128)(2,1)S(1)} collective-permute-done((bf16[256,512]{1,0:T(8,128)(2,1)S(1)}, bf16[256,512]{1,0:T(8,128)(2,1)S(1)}, u32[]{:S(2)}, u32[]{:S(2)}) %collective-permute-start.14) | collective-permute-done | bytes 262176 | tf_op jit(solution)/shard_map/ppermute | solution.py:501
  116.8 3.0 %finish.1 = bf16[4,256,512]{2,1,0:T(8,128)(2,1)} custom-call(s32[4]{0:T(128)S(1)} %bitcast.29, bf16[256,512]{1,0:T(8,128)(2,1)S(1)} %get-tuple-element.79.refs_0_, bf16[256,512]{1,0:T(8,128)(2,1)S(1)} %get-tuple-element.80.refs_1_, bf16[256,512]{1,0:T(8,128)(2,1)S(1)} %get-tuple-element.81.refs_2_, bf16[256,512]{1,0:T(8,128)(2,1)S(1)} %get-tuple-element.82.refs_3_, ...), custom_call_target="tpu_custom_call" | custom-call | flops 536870912 | bytes 5242880 | tf_op jit(solution)/shard_map/finish/pallas_call | solution.py:465
  (47 shorter events, 5.3 us)
Async XLA Ops:
  0.0 0.7 copy-start.2
  0.7 26.3 %copy-start.6 = (f32[1,128,128]{2,1,0:T(8,128)S(1)}, f32[1,128,128]{2,1,0:T(8,128)}, u32[]{:S(2)}) copy-start(f32[1,128,128]{2,1,0:T(8,128)} %param.20) | copy-start | bytes 196612
  4.2 29.4 %collective-permute-start = (bf16[256,512]{1,0:T(8,128)(2,1)S(1)}, bf16[256,512]{1,0:T(8,128)(2,1)S(1)}, u32[]{:S(2)}, u32[]{:S(2)}) collective-permute-start(bf16[256,512]{1,0:T(8,128)(2,1)S(1)} %get-tuple-element.49.refs_1_), channel_id=1, source_target_pairs={{0,8},{8,16},{16,24},{24,32},{32,40},{40,48},{48,56},{56,64},{64,7... | collective-permute-start | bytes 786440 | tf_op jit(solution)/shard_map/ppermute | solution.py:501
  4.3 29.3 %collective-permute-start.1 = (bf16[256,512]{1,0:T(8,128)(2,1)S(1)}, bf16[256,512]{1,0:T(8,128)(2,1)S(1)}, u32[]{:S(2)}, u32[]{:S(2)}) collective-permute-start(bf16[256,512]{1,0:T(8,128)(2,1)S(1)} %get-tuple-element.48.refs_0_), channel_id=1, source_target_pairs={{0,248},{8,0},{16,8},{24,16},{32,24},{40,32},{48,40},{56,48},{64,5... | collective-permute-start | bytes 786440 | tf_op jit(solution)/shard_map/ppermute | solution.py:501
  10.1 23.5 %collective-permute-start.2 = (bf16[256,512]{1,0:T(8,128)(2,1)S(1)}, bf16[256,512]{1,0:T(8,128)(2,1)S(1)}, u32[]{:S(2)}, u32[]{:S(2)}) collective-permute-start(bf16[256,512]{1,0:T(8,128)(2,1)S(1)} %get-tuple-element.51.refs_3_), channel_id=1, source_target_pairs={{0,1},{1,2},{2,3},{3,4},{4,5},{5,6},{6,7},{7,0},{8,9},{9,10},{10,1... | collective-permute-start | bytes 786440 | tf_op jit(solution)/shard_map/ppermute | solution.py:501
  11.7 21.9 %collective-permute-start.3 = (bf16[256,512]{1,0:T(8,128)(2,1)S(1)}, bf16[256,512]{1,0:T(8,128)(2,1)S(1)}, u32[]{:S(2)}, u32[]{:S(2)}) collective-permute-start(bf16[256,512]{1,0:T(8,128)(2,1)S(1)} %get-tuple-element.50.refs_2_), channel_id=1, source_target_pairs={{0,7},{1,0},{2,1},{3,2},{4,3},{5,4},{6,5},{7,6},{8,15},{9,8},{10,9... | collective-permute-start | bytes 786440 | tf_op jit(solution)/shard_map/ppermute | solution.py:501
  14.2 12.7 %collective-permute-start.4 = (f32[1,128,128]{2,1,0:T(8,128)}, f32[1,128,128]{2,1,0:T(8,128)S(1)}, u32[]{:S(2)}, u32[]{:S(2)}) collective-permute-start(f32[1,128,128]{2,1,0:T(8,128)} %param.20), channel_id=1, source_target_pairs={{0,32},{8,40},{16,48},{24,56},{32,0},{40,8},{48,16},{56,24},{64,96... | collective-permute-start | bytes 196616 | tf_op jit(solution)/shard_map/ppermute | solution.py:488
  19.5 0.7 copy-start.3
  20.1 7.9 %copy-start.7 = (s32[1,1,256]{2,1,0:T(1,128)S(1)}, s32[1,1,256]{2,1,0:T(1,128)}, u32[]{:S(2)}) copy-start(s32[1,1,256]{2,1,0:T(1,128)} %param.15) | copy-start | bytes 3076
  20.1 13.5 %copy-start.1 = (bf16[1,2048,128]{2,1,0:T(8,128)(2,1)S(1)}, bf16[1,2048,128]{2,1,0:T(8,128)(2,1)}, u32[]{:S(2)}) copy-start(bf16[1,2048,128]{2,1,0:T(8,128)(2,1)} %param.19) | copy-start | bytes 1572868
  20.1 13.5 %copy-start.5 = (f32[1,1,4]{2,1,0:T(1,128)S(1)}, f32[1,1,4]{2,1,0:T(1,128)}, u32[]{:S(2)}) copy-start(f32[1,1,4]{2,1,0:T(1,128)} %param.14) | copy-start | bytes 52
  27.0 6.5 %collective-permute-start.5 = (f32[2,128,128]{2,1,0:T(8,128)S(1)}, f32[2,128,128]{2,1,0:T(8,128)S(1)}, u32[]{:S(2)}, u32[]{:S(2)}) collective-permute-start(f32[2,128,128]{2,1,0:T(8,128)S(1)} %pad_maximum_fusion.7), channel_id=1, source_target_pairs={{0,16},{8,24},{16,0},{24,8},{32,48},{40,56},{48,32},{56,40},{64,80... | collective-permute-start | bytes 393224 | tf_op jit(solution)/shard_map/ppermute | solution.py:488
  33.4 11.6 %copy-start.4 = (s32[1,1,4]{2,1,0:T(1,128)S(1)}, s32[1,1,4]{2,1,0:T(1,128)}, u32[]{:S(2)}) copy-start(s32[1,1,4]{2,1,0:T(1,128)} %param.12) | copy-start | bytes 52
  33.5 15.7 %collective-permute-start.6 = (f32[4,128,128]{2,1,0:T(8,128)S(1)}, f32[4,128,128]{2,1,0:T(8,128)S(1)}, u32[]{:S(2)}, u32[]{:S(2)}) collective-permute-start(f32[4,128,128]{2,1,0:T(8,128)S(1)} %pad_maximum_fusion.4), channel_id=1, source_target_pairs={{0,8},{8,0},{16,24},{24,16},{32,40},{40,32},{48,56},{56,48},{64,72... | collective-permute-start | bytes 786440 | tf_op jit(solution)/shard_map/ppermute | solution.py:488
  35.7 13.5 %all-to-all-start = ((f32[8,32,128]{2,1,0:T(8,128)}), f32[8,32,128]{2,1,0:T(8,128)S(1)}, u32[]{:S(2)}, u32[]{:S(2)}) async-start(f32[8,32,128]{2,1,0:T(8,128)} %bitcast.7), calls=%async_computation | async-start | bytes 262144 | tf_op jit(solution)/shard_map/all_to_all | solution.py:554
  41.5 17.8 %collective-permute-start.7 = (bf16[1,256,256]{2,1,0:T(8,128)(2,1)S(1)}, bf16[1,256,256]{2,1,0:T(8,128)(2,1)S(1)}, u32[]{:S(2)}, u32[]{:S(2)}) collective-permute-start(bf16[1,256,256]{2,1,0:T(8,128)(2,1)S(1)} %bitcast.15), channel_id=1, source_target_pairs={{0,2},{1,3},{2,0},{3,1},{4,6},{5,7},{6,4},{7,5},{8,10},{9,11},{10,... | collective-permute-start | bytes 393224 | tf_op jit(solution)/shard_map/ppermute | solution.py:488
  49.9 13.6 %all-to-all-start.1 = ((f32[8,32,128]{2,1,0:T(8,128)}), f32[8,32,128]{2,1,0:T(8,128)S(1)}, u32[]{:S(2)}, u32[]{:S(2)}) async-start(f32[8,32,128]{2,1,0:T(8,128)} %shared_sum.1), calls=%async_computation.1 | async-start | bytes 262144 | tf_op jit(solution)/shard_map/all_to_all | solution.py:560
  61.0 5.3 %collective-permute-start.8 = (f32[1,136,128]{2,1,0:T(8,128)S(1)}, f32[1,136,128]{2,1,0:T(8,128)S(1)}, u32[]{:S(2)}, u32[]{:S(2)}) collective-permute-start(f32[1,136,128]{2,1,0:T(8,128)S(1)} %get-tuple-element.67), channel_id=1, source_target_pairs={{0,64},{8,72},{16,80},{24,88},{32,96},{40,104},{48,112},{56,120},{... | collective-permute-start | bytes 208904 | tf_op jit(solution)/shard_map/ppermute | solution.py:488
  61.5 17.2 %collective-permute-start.10 = (bf16[2,256,256]{2,1,0:T(8,128)(2,1)S(1)}, bf16[2,256,256]{2,1,0:T(8,128)(2,1)S(1)}, u32[]{:S(2)}, u32[]{:S(2)}) collective-permute-start(bf16[2,256,256]{2,1,0:T(8,128)(2,1)S(1)} %pad_maximum_fusion.5), channel_id=1, source_target_pairs={{0,1},{1,0},{2,3},{3,2},{4,5},{5,4},{6,7},{7,6},{8,9},{9,8},{10,11... | collective-permute-start | bytes 786440 | tf_op jit(solution)/shard_map/ppermute | solution.py:488
  66.3 12.5 %collective-permute-start.9 = (f32[2,136,128]{2,1,0:T(8,128)S(1)}, f32[2,136,128]{2,1,0:T(8,128)S(1)}, u32[]{:S(2)}, u32[]{:S(2)}) collective-permute-start(f32[2,136,128]{2,1,0:T(8,128)S(1)} %pad_maximum_fusion.6), channel_id=1, source_target_pairs={{0,128},{8,136},{16,144},{24,152},{32,160},{40,168},{48,176},{56,1... | collective-permute-start | bytes 417800 | tf_op jit(solution)/shard_map/ppermute | solution.py:488
  68.5 10.3 %all-to-all-start.2 = ((f32[4,32,128]{2,1,0:T(8,128)}), f32[4,32,128]{2,1,0:T(8,128)S(1)}, u32[]{:S(2)}, u32[]{:S(2)}) async-start(f32[4,32,128]{2,1,0:T(8,128)} %group_outflow.1), calls=%async_computation.2 | async-start | bytes 131072 | tf_op jit(solution)/shard_map/all_to_all | solution.py:572
  78.8 13.5 %collective-permute-start.11 = (bf16[4,256,256]{2,1,0:T(8,128)(2,1)S(1)}, bf16[4,256,256]{2,1,0:T(8,128)(2,1)S(1)}, u32[]{:S(2)}, u32[]{:S(2)}) collective-permute-start(bf16[4,256,256]{2,1,0:T(8,128)(2,1)S(1)} %pad_maximum_fusion.2), channel_id=1, source_target_pairs={{0,4},{1,5},{2,6},{3,7},{4,0},{5,1},{6,2},{7,3},{8,12},{9,13},{10,... | collective-permute-start | bytes 1572872 | tf_op jit(solution)/shard_map/ppermute | solution.py:488
  81.9 12.3 %all-to-all-start.3 = ((f32[8,32,128]{2,1,0:T(8,128)}), f32[8,32,128]{2,1,0:T(8,128)S(1)}, u32[]{:S(2)}, u32[]{:S(2)}) async-start(f32[8,32,128]{2,1,0:T(8,128)} %carried_states.1), calls=%async_computation.3 | async-start | bytes 262144 | tf_op jit(solution)/shard_map/all_to_all | solution.py:581
  94.1 22.7 %copy-start = (bf16[4,512,512]{2,1,0:T(8,128)(2,1)S(1)}, bf16[4,512,512]{2,1,0:T(8,128)(2,1)}, u32[]{:S(2)}) copy-start(bf16[4,512,512]{2,1,0:T(8,128)(2,1)} %get-tuple-element.57.restore.refs_8_) | copy-start | bytes 6291460
  98.0 9.0 %collective-permute-start.12 = (bf16[256,512]{1,0:T(8,128)(2,1)S(1)}, bf16[256,512]{1,0:T(8,128)(2,1)S(1)}, u32[]{:S(2)}, u32[]{:S(2)}) collective-permute-start(bf16[256,512]{1,0:T(8,128)(2,1)S(1)} %get-tuple-element.80.refs_1_), channel_id=1, source_target_pairs={{0,8},{8,16},{16,24},{24,32},{32,40},{40,48},{48,56},{56,64},{64,7... | collective-permute-start | bytes 786440 | tf_op jit(solution)/shard_map/ppermute | solution.py:501
  98.1 10.5 %collective-permute-start.13 = (bf16[256,512]{1,0:T(8,128)(2,1)S(1)}, bf16[256,512]{1,0:T(8,128)(2,1)S(1)}, u32[]{:S(2)}, u32[]{:S(2)}) collective-permute-start(bf16[256,512]{1,0:T(8,128)(2,1)S(1)} %get-tuple-element.79.refs_0_), channel_id=1, source_target_pairs={{0,248},{8,0},{16,8},{24,16},{32,24},{40,32},{48,40},{56,48},{64,5... | collective-permute-start | bytes 786440 | tf_op jit(solution)/shard_map/ppermute | solution.py:501
  102.9 13.9 %collective-permute-start.14 = (bf16[256,512]{1,0:T(8,128)(2,1)S(1)}, bf16[256,512]{1,0:T(8,128)(2,1)S(1)}, u32[]{:S(2)}, u32[]{:S(2)}) collective-permute-start(bf16[256,512]{1,0:T(8,128)(2,1)S(1)} %get-tuple-element.82.refs_3_), channel_id=1, source_target_pairs={{0,1},{1,2},{2,3},{3,4},{4,5},{5,6},{6,7},{7,0},{8,9},{9,10},{10,1... | collective-permute-start | bytes 786440 | tf_op jit(solution)/shard_map/ppermute | solution.py:501
  104.3 12.5 %collective-permute-start.15 = (bf16[256,512]{1,0:T(8,128)(2,1)S(1)}, bf16[256,512]{1,0:T(8,128)(2,1)S(1)}, u32[]{:S(2)}, u32[]{:S(2)}) collective-permute-start(bf16[256,512]{1,0:T(8,128)(2,1)S(1)} %get-tuple-element.81.refs_2_), channel_id=1, source_target_pairs={{0,7},{1,0},{2,1},{3,2},{4,3},{5,4},{6,5},{7,6},{8,15},{9,8},{10,9... | collective-permute-start | bytes 786440 | tf_op jit(solution)/shard_map/ppermute | solution.py:501

commit v3 on v2

--- a/solution.py
+++ b/solution.py
@@ -316,14 +316,14 @@
     state = jnp.zeros((samples, channels), F32)
     for k in range(lines):
         state = triple(state, maps[2 * k], maps[2 * k + 1]) + inflow[k] if k else inflow[0]
-    out[...] = jnp.broadcast_to(state[None], out.shape)
-
-
-def group_outflow(inflow, maps, copies):
+    out[...] = state
+
+
+def group_outflow(inflow, maps):
     lines, samples, channels = inflow.shape
     return pl.pallas_call(
         outflow_kernel,
-        out_shape=jax.ShapeDtypeStruct((copies, samples, channels), F32),
+        out_shape=jax.ShapeDtypeStruct((samples, channels), F32),
         grid=(1,),
         in_specs=[resident(inflow.shape), resident(maps.shape)],
         out_specs=IN_VMEM,
@@ -335,42 +335,41 @@
     )(inflow, in_hbm(maps))
 
 
-def carried_kernel(outflow, products, inflow, maps, out):
+def carried_kernel(products, inflow, maps, *refs):
+    outflows, out = refs[:-1], refs[-1]
     lines, samples, channels = inflow.shape
     line = lax.axis_index("sub")
     group = lax.div(line, lines)
-
-    def enter(a, value):
-        place = jnp.bitwise_xor(group, a)
-        value = triple(value, *split(products[place, pl.ds(0, channels), :]))
+    state = jnp.zeros((samples, channels), F32)
+    for step, outflow in zip(range(len(outflows), 0, -1), outflows):
+        place = jnp.bitwise_xor(group, jnp.maximum(group - step, 0))
+        value = triple(state, *split(products[place, pl.ds(0, channels), :]))
         for k in range(lines):
             value = value * products[place, pl.ds(channels + k, 1), :]
-        return value + outflow[a]
-
-    state = lax.fori_loop(0, group, enter, jnp.zeros((samples, channels), F32))
+        state = jnp.where(group >= step, value + outflow[...], state)
     state = run_lines(state, inflow, maps, lax.rem(line, lines))
     out[...] = jnp.broadcast_to(state[None], out.shape)
 
 
-def carried_states(outflow, products, inflow, maps, copies):
+def carried_states(outflows, products, inflow, maps, copies):
     lines, samples, channels = inflow.shape
     return pl.pallas_call(
         carried_kernel,
         out_shape=jax.ShapeDtypeStruct((copies, samples, channels), F32),
         grid=(1,),
         in_specs=[
-            resident(outflow.shape),
             resident(products.shape),
             resident(inflow.shape),
             resident(maps.shape),
-        ],
+        ]
+        + [resident((samples, channels))] * len(outflows),
         out_specs=IN_VMEM,
         compiler_params=params(8),
         cost_estimate=cost(
             6 * lines * samples * channels * channels, 8 * lines * channels * (samples + channels)
         ),
         name="carried_states",
-    )(outflow, products, inflow, in_hbm(maps))
+    )(products, inflow, in_hbm(maps), *outflows)
 
 
 def line_kernel(gathered, inverse, out):
@@ -400,46 +399,35 @@
     )(gathered, in_hbm(inverse))
 
 
-def extend_kernel(scale, base, carried, coupling, ordered_columns, dual0, dual1, *rest):
-    outs, answer = rest[:-1], rest[-1]
-    d = pl.program_id(0)
-
-    @pl.when(d == 0)
-    def _():
-        high, low = split(carried[...])
-        term = times(high, coupling[...]) + times(low, coupling[...])
-        answer[...] = (base[...] + term).astype(BF16)
-
-    value = scale[d] * times(answer[...], ordered_columns[0])
+def extend_kernel(scale, base, carried, coupling, ordered_columns, dual0, dual1, *outs):
+    high, low = split(carried[...])
+    term = times(high, coupling[...]) + times(low, coupling[...])
+    answer = (base[...] + term).astype(BF16)
     half = len(outs) // 2
-    for i, out in enumerate(outs):
-
-        @pl.when(d == i)
-        def _():
-            out[...] = ((dual0 if i < half else dual1)[0] + value).astype(BF16)
+    for d, out in enumerate(outs):
+        value = dual0[d] if d < half else dual1[d - half]
+        out[...] = (value + scale[d] * times(answer, ordered_columns[d])).astype(BF16)
 
 
 def extend(scale, base, carried, coupling, ordered_columns, dual0, dual1):
     half, samples, size = dual0.shape
     faces = 2 * half
     primal = base.shape[1]
-    channels = carried.shape[1]
     return pl.pallas_call(
         extend_kernel,
         out_shape=[jax.ShapeDtypeStruct((samples, size), BF16)] * faces,
-        grid=(faces,),
+        grid=(1,),
         in_specs=[
             pl.BlockSpec(memory_space=pltpu.SMEM),
             IN_VMEM,
             IN_VMEM,
-            resident((channels, primal)),
-            pl.BlockSpec((1, primal, size), lambda d: (d, 0, 0)),
-            pl.BlockSpec((1, samples, size), lambda d: (jnp.minimum(d, half - 1), 0, 0)),
-            pl.BlockSpec((1, samples, size), lambda d: (jnp.maximum(d - half, 0), 0, 0)),
+            resident(coupling.shape),
+            resident(ordered_columns.shape),
+            resident(dual0.shape),
+            resident(dual1.shape),
         ],
         out_specs=[IN_VMEM] * faces,
-        scratch_shapes=[pltpu.VMEM((samples, primal), BF16)],
-        compiler_params=params(8),
+        compiler_params=params(12),
         cost_estimate=cost(
             2 * faces * samples * size * primal, 6 * faces * samples * size + 2 * faces * size * primal
         ),
@@ -492,14 +480,13 @@
     return jnp.concatenate([value, exchange(value, axis, bit)])
 
 
+def shifted(value, axis, step):
+    count = lax.axis_size(axis)
+    return lax.ppermute(value, axis, [(i, (i + step) % count) for i in range(count)])
+
+
 def neighbours(faces):
     lower, upper, left, right = faces
-
-    def shifted(value, axis, step):
-        count = lax.axis_size(axis)
-        pairs = [(i, (i + step) % count) for i in range(count)]
-        return lax.ppermute(value, axis, pairs)
-
     return (
         shifted(upper, "sub", 1),
         shifted(lower, "sub", -1),
@@ -532,18 +519,20 @@
 
     groups = lines // GROUP
     inside = [[a * GROUP + b for b in range(GROUP)] for a in range(groups)]
-    between = [[a * GROUP + b for a in range(groups)] for b in range(GROUP)]
-    transfer = chain_transfer
-    for bit in DOUBLING:
-        transfer = doubled(transfer, "sub", bit)
+    copied = exchange(chain_transfer, "sub", DOUBLING[0])
 
     canon = to_canonical(slot, parts, order)
+    copied, canon = lax.optimization_barrier((copied, canon))
+    transfer = jnp.concatenate([chain_transfer, copied])
+    copied = exchange(transfer, "sub", DOUBLING[1])
     beside = neighbours(canon)
     basis, canon = lax.optimization_barrier((basis, canon))
     sort, restore, ordered, ordered_columns = tables(slot, order, basis)
     averaged, coarse_residual, heat = residuals(
         scale, canon, beside, ordered, thermal_handoff[0]
     )
+    copied, heat = lax.optimization_barrier((copied, heat))
+    transfer = doubled(jnp.concatenate([transfer, copied]), "sub", DOUBLING[2])
     positions = lax.broadcasted_iota(jnp.int32, (vertex_unknowns.shape[2], faces * size), 1)
     hits = jnp.sum((vertex_unknowns[0, 0][:, None] == positions).astype(F32), axis=0)
     mask = (1.0 - hits).reshape(faces, 1, size)
@@ -555,29 +544,31 @@
     masked = masked_local(slot, averaged, restore, mask)
     inflow, masked = lax.optimization_barrier((inflow, masked))
     inflow = shared_sum(inflow, GROUP)
-    masked, inflow = lax.optimization_barrier((masked, inflow))
+    masked, transfer, received, inflow = lax.optimization_barrier((masked, transfer, received, inflow))
 
     inflow = lax.all_to_all(inflow, "sub", 0, 0, axis_index_groups=inside)
     half = faces // 2
     dual0 = dual(0, half, slot, scale, masked, sort, mask, front_inverse[0, 0])
-    transfer, received, dual0 = lax.optimization_barrier((transfer, received, dual0))
+    transfer, dual0 = lax.optimization_barrier((transfer, dual0))
     maps, product = group_maps(transfer)
     others = exchange(product, "sub", GROUP)
     gathered = jnp.concatenate([gathered, received])
     received = exchange(gathered, "coarse", GATHER_STAGES[1])
     inflow, maps, masked = lax.optimization_barrier((inflow, maps, masked))
 
-    outflow = group_outflow(inflow, maps, groups)
-    masked, others, outflow = lax.optimization_barrier((masked, others, outflow))
-    outflow = lax.all_to_all(outflow, "sub", 0, 0, axis_index_groups=between)
+    outflow = group_outflow(inflow, maps)
+    masked, others, received, outflow = lax.optimization_barrier((masked, others, received, outflow))
+    outflows = [shifted(outflow, "sub", GROUP * step) for step in range(groups - 1, 0, -1)]
     product = jnp.concatenate([product, others])
     others = exchange(product, "sub", 2 * GROUP)
+    gathered = jnp.concatenate([gathered, received])
+    masked, gathered = lax.optimization_barrier((masked, gathered))
     dual1 = dual(half, half, slot, scale, masked, sort, mask, front_inverse[0, 0])
-    outflow, others, received, dual1 = lax.optimization_barrier((outflow, others, received, dual1))
+    received = exchange(gathered, "coarse", GATHER_STAGES[2])
+    outflows, others, dual1 = lax.optimization_barrier((outflows, others, dual1))
     product = jnp.concatenate([product, others])
     gathered = jnp.concatenate([gathered, received])
-    gathered = doubled(gathered, "coarse", GATHER_STAGES[2])
-    carried = carried_states(outflow, product, inflow, maps, members)
+    carried = carried_states(outflows, product, inflow, maps, members)
     carried = lax.all_to_all(carried, "coarse", 0, 0).reshape(samples, channels)
     base = line_base(gathered, coarse_inverse[0])
 

time: 121 us -> 117 us (0.967)
  waiting for transfers between devices: 24.8 us -> 22.2 us
  Pallas kernels: 41.8 us -> 40.1 us
    ppermute x8, waiting for transfers between devices: 13.7 us -> 0.44 us  [exchange(): lax.ppermute(value, axis, [(i, i ^ bit) for i in range(lax.axis_size(axis...]
    ppermute x8 -> x11, waiting for transfers between devices: 9.79 us -> 15 us  [shifted(): lax.ppermute(value, axis, [(i, (i + step) % count) for i in range(count)])]
    all_to_all x1, waiting for transfers between devices: 0.03 us -> 4.79 us  [per_device(): carried = lax.all_to_all(carried, 'coarse', 0, 0).reshape(samples, channels)]
    all_to_all x1 -> x0, starting transfers between devices: 4.68 us -> none  [per_device(): outflow = lax.all_to_all(outflow, 'sub', 0, 0, axis_index_groups=between)]
    ppermute x8 -> x11, starting transfers between devices: 19 us -> 22.7 us  [shifted(): lax.ppermute(value, axis, [(i, (i + step) % count) for i in range(count)])]
    all_to_all x1, starting transfers between devices: 3.63 us -> 6.18 us  [per_device(): inflow = lax.all_to_all(inflow, 'sub', 0, 0, axis_index_groups=inside)]
    all_to_all x1, starting transfers between devices: 5.8 us -> 4.03 us  [per_device(): lax.all_to_all(heat.reshape(members, share, channels), 'coarse', 0, 0)]
    pallas_call x1, Pallas kernels: 3.87 us -> 2.56 us  [extend(): pl.pallas_call(extend_kernel, out_shape=[jax.ShapeDtypeStruct((samples, s...]
  transfers between devices with their start and end apart: 20 -> 22, of which waited for: 6 -> 8; matrix products, arithmetic and copies ran while one was open for 0% -> 1% of each run, Pallas kernels for 26% -> 30%
where the time goes in v3:
time: 117 us; the launch traced here: 116 us
  starting transfers between devices  51.8 us (44%)
  Pallas kernels  40.1 us (34%)
  waiting for transfers between devices  22.2 us (19%)
  other arithmetic  1.42 us (1%)
    ppermute x11, starting transfers between devices, shifted(): lax.ppermute(value, axis, [(i, (i + step) % count) for i in range(count)])  22.7 us
    ppermute x8, starting transfers between devices, exchange(): lax.ppermute(value, axis, [(i, i ^ bit) for i in range(lax.axis_size(axis...  15 us
    ppermute x11, waiting for transfers between devices, shifted(): lax.ppermute(value, axis, [(i, (i + step) % count) for i in range(count)])  15 us
    pallas_call x2, Pallas kernels, dual(): pl.pallas_call(functools.partial(dual_kernel, first), out_shape=pltpu.HBM...  11.3 us
    all_to_all x1, starting transfers between devices, per_device(): inflow = lax.all_to_all(inflow, 'sub', 0, 0, axis_index_groups=inside)  6.18 us
    pallas_call x1, Pallas kernels, tables(): pl.pallas_call(tables_kernel, out_shape=[pltpu.HBM((faces, size, size), B...  5.27 us
    all_to_all x1, waiting for transfers between devices, per_device(): carried = lax.all_to_all(carried, 'coarse', 0, 0).reshape(samples, channels)  4.79 us
    pallas_call x1, Pallas kernels, masked_local(): pl.pallas_call(local_kernel, out_shape=pltpu.HBM(averaged.shape, BF16), g...  4.21 us
  transfers between devices with their start and end apart: 22, of which 8 were waited for; matrix products, arithmetic and copies ran while one was open for 1% of the time, Pallas kernels for 30%

profile of v3, /device:TPU:2, one launch (start us, length us, event | category | flops | bytes accessed | tf_op | source)
XLA Modules:
  0.0 116.4 jit_solution(5693627715115403773)
XLA Ops:
  0.0 7.2 %collective-permute-start = (f32[1,128,128]{2,1,0:T(8,128)}, f32[1,128,128]{2,1,0:T(8,128)S(1)}, u32[]{:S(2)}, u32[]{:S(2)}) collective-permute-start(f32[1,128,128]{2,1,0:T(8,128)} %param.20), channel_id=1, source_target_pairs={{0,32},{8,40},{16,48},{24,56},{32,0},{40,8},{48,16},{56,24},{64,96... | collective-permute-start | bytes 196616 | tf_op jit(solution)/shard_map/ppermute | solution.py:476
  7.8 3.5 %canon.1 = (bf16[256,512]{1,0:T(8,128)(2,1)S(1)}, bf16[256,512]{1,0:T(8,128)(2,1)S(1)}, bf16[256,512]{1,0:T(8,128)(2,1)S(1)}, bf16[256,512]{1,0:T(8,128)(2,1)S(1)}) custom-call(s32[4]{0:T(128)S(1)} %bitcast.23, bf16[4,256,512]{2,1,0:T(8,128)(2,1)} %bitcast.38, s32[4,512]{1,0:T(4,128)} %bitcast.40), custom_call_target="tpu_custom_call" | custom-call | flops 536870912 | bytes 2097152 | tf_op jit(solution)/shard_map/canon/pallas_call | solution.py:65
  11.5 4.7 %collective-permute-start.3 = (bf16[256,512]{1,0:T(8,128)(2,1)S(1)}, bf16[256,512]{1,0:T(8,128)(2,1)S(1)}, u32[]{:S(2)}, u32[]{:S(2)}) collective-permute-start(bf16[256,512]{1,0:T(8,128)(2,1)S(1)} %get-tuple-element.65.refs_0_), channel_id=1, source_target_pairs={{0,248},{8,0},{16,8},{24,16},{32,24},{40,32},{48,40},{56,48},{64,5... | collective-permute-start | bytes 786440 | tf_op jit(solution)/shard_map/ppermute | solution.py:485
  16.3 1.6 %collective-permute-start.4 = (bf16[256,512]{1,0:T(8,128)(2,1)S(1)}, bf16[256,512]{1,0:T(8,128)(2,1)S(1)}, u32[]{:S(2)}, u32[]{:S(2)}) collective-permute-start(bf16[256,512]{1,0:T(8,128)(2,1)S(1)} %get-tuple-element.68.refs_3_), channel_id=1, source_target_pairs={{0,1},{1,2},{2,3},{3,4},{4,5},{5,6},{6,7},{7,0},{8,9},{9,10},{10,1... | collective-permute-start | bytes 786440 | tf_op jit(solution)/shard_map/ppermute | solution.py:485
  17.8 2.6 %collective-permute-start.5 = (bf16[256,512]{1,0:T(8,128)(2,1)S(1)}, bf16[256,512]{1,0:T(8,128)(2,1)S(1)}, u32[]{:S(2)}, u32[]{:S(2)}) collective-permute-start(bf16[256,512]{1,0:T(8,128)(2,1)S(1)} %get-tuple-element.67.refs_2_), channel_id=1, source_target_pairs={{0,7},{1,0},{2,1},{3,2},{4,3},{5,4},{6,5},{7,6},{8,15},{9,8},{10,9... | collective-permute-start | bytes 786440 | tf_op jit(solution)/shard_map/ppermute | solution.py:485
  21.7 5.3 %tables.1 = (bf16[4,512,512]{2,1,0:T(8,128)(2,1)}, bf16[4,512,512]{2,1,0:T(8,128)(2,1)}, bf16[4,512,256]{2,1,0:T(8,128)(2,1)S(1)}, bf16[4,256,512]{2,1,0:T(8,128)(2,1)}) custom-call(s32[4]{0:T(128)S(1)} %bitcast.24, s32[4,512]{1,0:T(4,128)} %bitcast.41, bf16[4,512,256]{2,1,0:T(8,128)(2,1)} %bitcast.39), custom_call_target="tpu_custom_call" | custom-call | flops 1073741824 | bytes 7340032 | tf_op jit(solution)/shard_map/tables/pallas_call | solution.py:98
  27.0 5.0 %collective-permute-done.4.refs_6_ = bf16[256,512]{1,0:T(8,128)(2,1)S(1)} collective-permute-done((bf16[256,512]{1,0:T(8,128)(2,1)S(1)}, bf16[256,512]{1,0:T(8,128)(2,1)S(1)}, u32[]{:S(2)}, u32[]{:S(2)}) %collective-permute-start.4) | collective-permute-done | bytes 262176 | tf_op jit(solution)/shard_map/ppermute | solution.py:485
  32.0 2.0 %residuals.1 = (bf16[4,256,512]{2,1,0:T(8,128)(2,1)}, bf16[256,256]{1,0:T(8,128)(2,1)S(1)}, f32[256,128]{1,0:T(8,128)}) custom-call(f32[4]{0:T(128)S(1)} %bitcast.29, bf16[256,512]{1,0:T(8,128)(2,1)S(1)} %get-tuple-element.65.refs_0_, bf16[256,512]{1,0:T(8,128)(2,1)S(1)} %get-tuple-element.66.refs_1_, bf16[256,512]{1,0:T(8,128)(2,1)S(1)} %get-tuple-element.67.refs_2_, ...), custom_call_target="tpu_custom_call" | custom-call | flops 268435456 | bytes 4194304 | tf_op jit(solution)/shard_map/residuals/pallas_call | solution.py:160
  34.1 4.0 %all-to-all-start = ((f32[8,32,128]{2,1,0:T(8,128)}), f32[8,32,128]{2,1,0:T(8,128)S(1)}, u32[]{:S(2)}, u32[]{:S(2)}) async-start(f32[8,32,128]{2,1,0:T(8,128)} %bitcast.6), calls=%async_computation | async-start | bytes 262144 | tf_op jit(solution)/shard_map/all_to_all | solution.py:543
  38.2 3.5 %collective-permute-start.7 = (bf16[1,256,256]{2,1,0:T(8,128)(2,1)S(1)}, bf16[1,256,256]{2,1,0:T(8,128)(2,1)S(1)}, u32[]{:S(2)}, u32[]{:S(2)}) collective-permute-start(bf16[1,256,256]{2,1,0:T(8,128)(2,1)S(1)} %bitcast.16), channel_id=1, source_target_pairs={{0,2},{1,3},{2,0},{3,1},{4,6},{5,7},{6,4},{7,5},{8,10},{9,11},{10,... | collective-permute-start | bytes 393224 | tf_op jit(solution)/shard_map/ppermute | solution.py:476
  41.7 4.2 %masked_local.1.masked = bf16[4,256,512]{2,1,0:T(8,128)(2,1)} custom-call(s32[4]{0:T(128)S(1)} %bitcast.25, bf16[4,256,512]{2,1,0:T(8,128)(2,1)} %get-tuple-element.73.averaged, bf16[4,512,512]{2,1,0:T(8,128)(2,1)} %get-tuple-element.74.restore.refs_8_, f32[4,1,512]{2,1,0:T(1,128)S(1)} %bitcast.20), custom_call_target="tpu_custom_call" | custom-call | flops 536870912 | bytes 4194304 | tf_op jit(solution)/shard_map/masked_local/pallas_call | solution.py:204
  46.9 1.1 collective-permute-start.9
  48.0 6.2 %all-to-all-start.1 = ((f32[8,32,128]{2,1,0:T(8,128)}), f32[8,32,128]{2,1,0:T(8,128)S(1)}, u32[]{:S(2)}, u32[]{:S(2)}) async-start(f32[8,32,128]{2,1,0:T(8,128)} %shared_sum.1), calls=%async_computation.1 | async-start | bytes 262144 | tf_op jit(solution)/shard_map/all_to_all | solution.py:549
  54.1 5.7 %dual0.1 = f32[2,256,512]{2,1,0:T(8,128)} custom-call(s32[4]{0:T(128)S(1)} %bitcast.26, f32[4]{0:T(128)S(1)} %bitcast.30, bf16[4,256,512]{2,1,0:T(8,128)(2,1)} %masked_local.1.masked, bf16[4,512,512]{2,1,0:T(8,128)(2,1)} %get-tuple-element.82.sort, f32[4,1,512]{2,1,0:T(1,128)S(1)} %bitcast.21, bf16[2048,2048]{1,0:T(8,128)(2,1)} %bitcast.33), custom_call_target="tpu_custom_call" | custom-call | flops 1610612736 | bytes 8388608 | tf_op jit(solution)/shard_map/dual0/pallas_call | solution.py:234
  59.9 1.6 %group_maps.1 = (bf16[16,128,128]{2,1,0:T(8,128)(2,1)}, f32[1,136,128]{2,1,0:T(8,128)S(1)}) custom-call(f32[8,128,128]{2,1,0:T(8,128)S(1)} %pad_maximum_fusion.1.transfer), custom_call_target="tpu_custom_call" | custom-call | flops 100663296 | bytes 1048576 | tf_op jit(solution)/shard_map/group_maps/pallas_call | solution.py:289
  61.9 1.9 %all-to-all-done.1.inflow = f32[8,32,128]{2,1,0:T(8,128)S(1)} async-done(((f32[8,32,128]{2,1,0:T(8,128)}), f32[8,32,128]{2,1,0:T(8,128)S(1)}, u32[]{:S(2)}, u32[]{:S(2)}) %all-to-all-start.1) | async-done | bytes 131104 | tf_op jit(solution)/shard_map/all_to_all | solution.py:549
  63.8 2.1 %group_outflow.1 = f32[32,128]{1,0:T(8,128)S(1)} custom-call(f32[8,32,128]{2,1,0:T(8,128)S(1)} %all-to-all-done.1.inflow, bf16[16,128,128]{2,1,0:T(8,128)(2,1)} %get-tuple-element.89.maps), custom_call_target="tpu_custom_call" | custom-call | flops 25165824 | bytes 655360 | tf_op jit(solution)/shard_map/group_outflow/pallas_call | solution.py:324
  66.2 1.2 %collective-permute-start.10 = (bf16[4,256,256]{2,1,0:T(8,128)(2,1)S(1)}, bf16[4,256,256]{2,1,0:T(8,128)(2,1)S(1)}, u32[]{:S(2)}, u32[]{:S(2)}) collective-permute-start(bf16[4,256,256]{2,1,0:T(8,128)(2,1)S(1)} %pad_maximum_fusion.2), channel_id=1, source_target_pairs={{0,4},{1,5},{2,6},{3,7},{4,0},{5,1},{6,2},{7,3},{8,12},{9,13},{10,... | collective-permute-start | bytes 1572872 | tf_op jit(solution)/shard_map/ppermute | solution.py:476
  67.8 2.5 %collective-permute-start.12 = (f32[32,128]{1,0:T(8,128)S(1)}, f32[32,128]{1,0:T(8,128)S(1)}, u32[]{:S(2)}, u32[]{:S(2)}) collective-permute-start(f32[32,128]{1,0:T(8,128)S(1)} %group_outflow.1), channel_id=1, source_target_pairs={{0,128},{8,136},{16,144},{24,152},{32,160},{40,168},{48,176},{56,1... | collective-permute-start | bytes 49160 | tf_op jit(solution)/shard_map/ppermute | solution.py:485
  70.3 1.8 %collective-permute-start.13 = (f32[32,128]{1,0:T(8,128)S(1)}, f32[32,128]{1,0:T(8,128)S(1)}, u32[]{:S(2)}, u32[]{:S(2)}) collective-permute-start(f32[32,128]{1,0:T(8,128)S(1)} %group_outflow.1), channel_id=1, source_target_pairs={{0,64},{8,72},{16,80},{24,88},{32,96},{40,104},{48,112},{56,120},{... | collective-permute-start | bytes 49160 | tf_op jit(solution)/shard_map/ppermute | solution.py:485
  72.2 1.5 %collective-permute-start.14 = (f32[2,136,128]{2,1,0:T(8,128)S(1)}, f32[2,136,128]{2,1,0:T(8,128)S(1)}, u32[]{:S(2)}, u32[]{:S(2)}) collective-permute-start(f32[2,136,128]{2,1,0:T(8,128)S(1)} %pad_maximum_fusion.6), channel_id=1, source_target_pairs={{0,128},{8,136},{16,144},{24,152},{32,160},{40,168},{48,176},{56,1... | collective-permute-start | bytes 417800 | tf_op jit(solution)/shard_map/ppermute | solution.py:476
  73.6 5.6 %dual2.1.dual1 = f32[2,256,512]{2,1,0:T(8,128)} custom-call(s32[4]{0:T(128)S(1)} %bitcast.27, f32[4]{0:T(128)S(1)} %bitcast.31, bf16[4,256,512]{2,1,0:T(8,128)(2,1)} %masked_local.1.masked, bf16[4,512,512]{2,1,0:T(8,128)(2,1)} %get-tuple-element.82.sort, f32[4,1,512]{2,1,0:T(1,128)S(1)} %bitcast.22, bf16[2048,2048]{1,0:T(8,128)(2,1)} %bitcast.34), custom_call_target="tpu_custom_call" | custom-call | flops 1610612736 | bytes 8388608 | tf_op jit(solution)/shard_map/dual2/pallas_call | solution.py:234
  79.2 2.2 %carried_states.1 = f32[8,32,128]{2,1,0:T(8,128)} custom-call(f32[4,136,128]{2,1,0:T(8,128)S(1)} %pad_maximum_fusion.3.products, f32[8,32,128]{2,1,0:T(8,128)S(1)} %all-to-all-done.1.inflow, bf16[16,128,128]{2,1,0:T(8,128)(2,1)} %get-tuple-element.89.maps, f32[32,128]{1,0:T(8,128)S(1)} %collective-permute-done.11.refs_0_, ...), custom_call_target="tpu_custom_call" | custom-call | flops 25165824 | bytes 1310720 | tf_op jit(solution)/shard_map/carried_states/pallas_call | solution.py:356
  81.4 3.8 %all-to-all-start.2 = ((f32[8,32,128]{2,1,0:T(8,128)}), f32[8,32,128]{2,1,0:T(8,128)S(1)}, u32[]{:S(2)}, u32[]{:S(2)}) async-start(f32[8,32,128]{2,1,0:T(8,128)} %carried_states.1), calls=%async_computation.2 | async-start | bytes 262144 | tf_op jit(solution)/shard_map/all_to_all | solution.py:572
  85.4 1.7 %line_base.1.base = f32[256,256]{1,0:T(8,128)S(1)} custom-call(bf16[8,256,256]{2,1,0:T(8,128)(2,1)S(1)} %pad_maximum_fusion.gathered, bf16[2048,256]{1,0:T(8,128)(2,1)} %bitcast.35), custom_call_target="tpu_custom_call" | custom-call | flops 268435456 | bytes 2097152 | tf_op jit(solution)/shard_map/line_base/pallas_call | solution.py:388
  87.0 4.8 %all-to-all-done.2 = f32[8,32,128]{2,1,0:T(8,128)S(1)} async-done(((f32[8,32,128]{2,1,0:T(8,128)}), f32[8,32,128]{2,1,0:T(8,128)S(1)}, u32[]{:S(2)}, u32[]{:S(2)}) %all-to-all-start.2) | async-done | bytes 131104 | tf_op jit(solution)/shard_map/all_to_all | solution.py:572
  91.8 2.6 %extend.1 = (bf16[256,512]{1,0:T(8,128)(2,1)S(1)}, bf16[256,512]{1,0:T(8,128)(2,1)S(1)}, bf16[256,512]{1,0:T(8,128)(2,1)S(1)}, bf16[256,512]{1,0:T(8,128)(2,1)S(1)}) custom-call(f32[4]{0:T(128)S(1)} %bitcast.32, f32[256,256]{1,0:T(8,128)S(1)} %line_base.1.base, f32[256,128]{1,0:T(8,128)S(1)} %bitcast.19, bf16[128,256]{1,0:T(8,128)(2,1)} %bitcast.36, ...), custom_call_target="tpu_custom_call" | custom-call | flops 268435456 | bytes 4194304 | tf_op jit(solution)/shard_map/extend/pallas_call | solution.py:416
  94.5 4.7 %collective-permute-start.16 = (bf16[256,512]{1,0:T(8,128)(2,1)S(1)}, bf16[256,512]{1,0:T(8,128)(2,1)S(1)}, u32[]{:S(2)}, u32[]{:S(2)}) collective-permute-start(bf16[256,512]{1,0:T(8,128)(2,1)S(1)} %get-tuple-element.103.refs_0_), channel_id=1, source_target_pairs={{0,248},{8,0},{16,8},{24,16},{32,24},{40,32},{48,40},{56,48},{64,5... | collective-permute-start | bytes 786440 | tf_op jit(solution)/shard_map/ppermute | solution.py:485
  99.7 3.6 %collective-permute-start.18 = (bf16[256,512]{1,0:T(8,128)(2,1)S(1)}, bf16[256,512]{1,0:T(8,128)(2,1)S(1)}, u32[]{:S(2)}, u32[]{:S(2)}) collective-permute-start(bf16[256,512]{1,0:T(8,128)(2,1)S(1)} %get-tuple-element.105.refs_2_), channel_id=1, source_target_pairs={{0,7},{1,0},{2,1},{3,2},{4,3},{5,4},{6,5},{7,6},{8,15},{9,8},{10,9... | collective-permute-start | bytes 786440 | tf_op jit(solution)/shard_map/ppermute | solution.py:485
  104.2 0.9 collective-permute-done.16.refs_5_
  105.2 8.2 %collective-permute-done.17.refs_6_ = bf16[256,512]{1,0:T(8,128)(2,1)S(1)} collective-permute-done((bf16[256,512]{1,0:T(8,128)(2,1)S(1)}, bf16[256,512]{1,0:T(8,128)(2,1)S(1)}, u32[]{:S(2)}, u32[]{:S(2)}) %collective-permute-start.17) | collective-permute-done | bytes 262176 | tf_op jit(solution)/shard_map/ppermute | solution.py:485
  113.4 3.0 %finish.1 = bf16[4,256,512]{2,1,0:T(8,128)(2,1)} custom-call(s32[4]{0:T(128)S(1)} %bitcast.28, bf16[256,512]{1,0:T(8,128)(2,1)S(1)} %get-tuple-element.103.refs_0_, bf16[256,512]{1,0:T(8,128)(2,1)S(1)} %get-tuple-element.104.refs_1_, bf16[256,512]{1,0:T(8,128)(2,1)S(1)} %get-tuple-element.105.refs_2_, bf16[256,512]{1,0:T(8,128)(2,1)S(1)} %get-tuple-element.106.refs_3_, ...), custom_call_target="tpu_custom_call" | custom-call | flops 536870912 | bytes 5242880 | tf_op jit(solution)/shard_map/finish/pallas_call | solution.py:453
  (49 shorter events, 5.8 us)
Async XLA Ops:
  0.0 21.7 %copy-start.3 = (s32[1,1,4]{2,1,0:T(1,128)S(1)}, s32[1,1,4]{2,1,0:T(1,128)}, u32[]{:S(2)}) copy-start(s32[1,1,4]{2,1,0:T(1,128)} %param.12) | copy-start | bytes 52
  0.0 21.4 %copy-start.6 = (s32[1,1,256]{2,1,0:T(1,128)S(1)}, s32[1,1,256]{2,1,0:T(1,128)}, u32[]{:S(2)}) copy-start(s32[1,1,256]{2,1,0:T(1,128)} %param.15) | copy-start | bytes 3076
  0.0 11.4 %collective-permute-start = (f32[1,128,128]{2,1,0:T(8,128)}, f32[1,128,128]{2,1,0:T(8,128)S(1)}, u32[]{:S(2)}, u32[]{:S(2)}) collective-permute-start(f32[1,128,128]{2,1,0:T(8,128)} %param.20), channel_id=1, source_target_pairs={{0,32},{8,40},{16,48},{24,56},{32,0},{40,8},{48,16},{56,24},{64,96... | collective-permute-start | bytes 196616 | tf_op jit(solution)/shard_map/ppermute | solution.py:476
  7.2 0.7 copy-start.2
  11.4 20.5 %copy-start.1 = (bf16[1,2048,128]{2,1,0:T(8,128)(2,1)S(1)}, bf16[1,2048,128]{2,1,0:T(8,128)(2,1)}, u32[]{:S(2)}) copy-start(bf16[1,2048,128]{2,1,0:T(8,128)(2,1)} %param.19) | copy-start | bytes 1572868
  11.4 20.5 %copy-start.4 = (f32[1,1,4]{2,1,0:T(1,128)S(1)}, f32[1,1,4]{2,1,0:T(1,128)}, u32[]{:S(2)}) copy-start(f32[1,1,4]{2,1,0:T(1,128)} %param.14) | copy-start | bytes 52
  11.4 15.5 %collective-permute-start.2 = (bf16[256,512]{1,0:T(8,128)(2,1)S(1)}, bf16[256,512]{1,0:T(8,128)(2,1)S(1)}, u32[]{:S(2)}, u32[]{:S(2)}) collective-permute-start(bf16[256,512]{1,0:T(8,128)(2,1)S(1)} %get-tuple-element.66.refs_1_), channel_id=1, source_target_pairs={{0,8},{8,16},{16,24},{24,32},{32,40},{40,48},{48,56},{56,64},{64,7... | collective-permute-start | bytes 786440 | tf_op jit(solution)/shard_map/ppermute | solution.py:485
  11.5 15.5 %collective-permute-start.3 = (bf16[256,512]{1,0:T(8,128)(2,1)S(1)}, bf16[256,512]{1,0:T(8,128)(2,1)S(1)}, u32[]{:S(2)}, u32[]{:S(2)}) collective-permute-start(bf16[256,512]{1,0:T(8,128)(2,1)S(1)} %get-tuple-element.65.refs_0_), channel_id=1, source_target_pairs={{0,248},{8,0},{16,8},{24,16},{32,24},{40,32},{48,40},{56,48},{64,5... | collective-permute-start | bytes 786440 | tf_op jit(solution)/shard_map/ppermute | solution.py:485
  16.3 15.7 %collective-permute-start.4 = (bf16[256,512]{1,0:T(8,128)(2,1)S(1)}, bf16[256,512]{1,0:T(8,128)(2,1)S(1)}, u32[]{:S(2)}, u32[]{:S(2)}) collective-permute-start(bf16[256,512]{1,0:T(8,128)(2,1)S(1)} %get-tuple-element.68.refs_3_), channel_id=1, source_target_pairs={{0,1},{1,2},{2,3},{3,4},{4,5},{5,6},{6,7},{7,0},{8,9},{9,10},{10,1... | collective-permute-start | bytes 786440 | tf_op jit(solution)/shard_map/ppermute | solution.py:485
  17.8 14.1 %collective-permute-start.5 = (bf16[256,512]{1,0:T(8,128)(2,1)S(1)}, bf16[256,512]{1,0:T(8,128)(2,1)S(1)}, u32[]{:S(2)}, u32[]{:S(2)}) collective-permute-start(bf16[256,512]{1,0:T(8,128)(2,1)S(1)} %get-tuple-element.67.refs_2_), channel_id=1, source_target_pairs={{0,7},{1,0},{2,1},{3,2},{4,3},{5,4},{6,5},{7,6},{8,15},{9,8},{10,9... | collective-permute-start | bytes 786440 | tf_op jit(solution)/shard_map/ppermute | solution.py:485
  21.3 12.7 %collective-permute-start.1 = (f32[2,128,128]{2,1,0:T(8,128)S(1)}, f32[2,128,128]{2,1,0:T(8,128)S(1)}, u32[]{:S(2)}, u32[]{:S(2)}) collective-permute-start(f32[2,128,128]{2,1,0:T(8,128)S(1)} %pad_maximum_fusion.7), channel_id=1, source_target_pairs={{0,16},{8,24},{16,0},{24,8},{32,48},{40,56},{48,32},{56,40},{64,80... | collective-permute-start | bytes 393224 | tf_op jit(solution)/shard_map/ppermute | solution.py:476
  27.0 7.0 %copy-start.5 = (f32[1,128,128]{2,1,0:T(8,128)S(1)}, f32[1,128,128]{2,1,0:T(8,128)}, u32[]{:S(2)}) copy-start(f32[1,128,128]{2,1,0:T(8,128)} %param.20) | copy-start | bytes 196612
  34.0 12.6 %collective-permute-start.6 = (f32[4,128,128]{2,1,0:T(8,128)S(1)}, f32[4,128,128]{2,1,0:T(8,128)S(1)}, u32[]{:S(2)}, u32[]{:S(2)}) collective-permute-start(f32[4,128,128]{2,1,0:T(8,128)S(1)} %pad_maximum_fusion.4), channel_id=1, source_target_pairs={{0,8},{8,0},{16,24},{24,16},{32,40},{40,32},{48,56},{56,48},{64,72... | collective-permute-start | bytes 786440 | tf_op jit(solution)/shard_map/ppermute | solution.py:476
  34.1 11.8 %all-to-all-start = ((f32[8,32,128]{2,1,0:T(8,128)}), f32[8,32,128]{2,1,0:T(8,128)S(1)}, u32[]{:S(2)}, u32[]{:S(2)}) async-start(f32[8,32,128]{2,1,0:T(8,128)} %bitcast.6), calls=%async_computation | async-start | bytes 262144 | tf_op jit(solution)/shard_map/all_to_all | solution.py:543
  38.2 8.7 %collective-permute-start.7 = (bf16[1,256,256]{2,1,0:T(8,128)(2,1)S(1)}, bf16[1,256,256]{2,1,0:T(8,128)(2,1)S(1)}, u32[]{:S(2)}, u32[]{:S(2)}) collective-permute-start(bf16[1,256,256]{2,1,0:T(8,128)(2,1)S(1)} %bitcast.16), channel_id=1, source_target_pairs={{0,2},{1,3},{2,0},{3,1},{4,6},{5,7},{6,4},{7,5},{8,10},{9,11},{10,... | collective-permute-start | bytes 393224 | tf_op jit(solution)/shard_map/ppermute | solution.py:476
  46.9 19.2 %collective-permute-start.9 = (bf16[2,256,256]{2,1,0:T(8,128)(2,1)S(1)}, bf16[2,256,256]{2,1,0:T(8,128)(2,1)S(1)}, u32[]{:S(2)}, u32[]{:S(2)}) collective-permute-start(bf16[2,256,256]{2,1,0:T(8,128)(2,1)S(1)} %pad_maximum_fusion.5), channel_id=1, source_target_pairs={{0,1},{1,0},{2,3},{3,2},{4,5},{5,4},{6,7},{7,6},{8,9},{9,8},{10,11... | collective-permute-start | bytes 786440 | tf_op jit(solution)/shard_map/ppermute | solution.py:476
  48.0 15.9 %all-to-all-start.1 = ((f32[8,32,128]{2,1,0:T(8,128)}), f32[8,32,128]{2,1,0:T(8,128)S(1)}, u32[]{:S(2)}, u32[]{:S(2)}) async-start(f32[8,32,128]{2,1,0:T(8,128)} %shared_sum.1), calls=%async_computation.1 | async-start | bytes 262144 | tf_op jit(solution)/shard_map/all_to_all | solution.py:549
  61.5 4.6 %collective-permute-start.8 = (f32[1,136,128]{2,1,0:T(8,128)S(1)}, f32[1,136,128]{2,1,0:T(8,128)S(1)}, u32[]{:S(2)}, u32[]{:S(2)}) collective-permute-start(f32[1,136,128]{2,1,0:T(8,128)S(1)} %get-tuple-element.86), channel_id=1, source_target_pairs={{0,64},{8,72},{16,80},{24,88},{32,96},{40,104},{48,112},{56,120},{... | collective-permute-start | bytes 208904 | tf_op jit(solution)/shard_map/ppermute | solution.py:476
  66.2 19.1 %collective-permute-start.10 = (bf16[4,256,256]{2,1,0:T(8,128)(2,1)S(1)}, bf16[4,256,256]{2,1,0:T(8,128)(2,1)S(1)}, u32[]{:S(2)}, u32[]{:S(2)}) collective-permute-start(bf16[4,256,256]{2,1,0:T(8,128)(2,1)S(1)} %pad_maximum_fusion.2), channel_id=1, source_target_pairs={{0,4},{1,5},{2,6},{3,7},{4,0},{5,1},{6,2},{7,3},{8,12},{9,13},{10,... | collective-permute-start | bytes 1572872 | tf_op jit(solution)/shard_map/ppermute | solution.py:476
  67.4 11.8 %collective-permute-start.11 = (f32[32,128]{1,0:T(8,128)S(1)}, f32[32,128]{1,0:T(8,128)S(1)}, u32[]{:S(2)}, u32[]{:S(2)}) collective-permute-start(f32[32,128]{1,0:T(8,128)S(1)} %group_outflow.1), channel_id=1, source_target_pairs={{0,192},{8,200},{16,208},{24,216},{32,224},{40,232},{48,240},{56,2... | collective-permute-start | bytes 49160 | tf_op jit(solution)/shard_map/ppermute | solution.py:485
  67.8 11.4 %collective-permute-start.12 = (f32[32,128]{1,0:T(8,128)S(1)}, f32[32,128]{1,0:T(8,128)S(1)}, u32[]{:S(2)}, u32[]{:S(2)}) collective-permute-start(f32[32,128]{1,0:T(8,128)S(1)} %group_outflow.1), channel_id=1, source_target_pairs={{0,128},{8,136},{16,144},{24,152},{32,160},{40,168},{48,176},{56,1... | collective-permute-start | bytes 49160 | tf_op jit(solution)/shard_map/ppermute | solution.py:485
  70.3 8.9 %collective-permute-start.13 = (f32[32,128]{1,0:T(8,128)S(1)}, f32[32,128]{1,0:T(8,128)S(1)}, u32[]{:S(2)}, u32[]{:S(2)}) collective-permute-start(f32[32,128]{1,0:T(8,128)S(1)} %group_outflow.1), channel_id=1, source_target_pairs={{0,64},{8,72},{16,80},{24,88},{32,96},{40,104},{48,112},{56,120},{... | collective-permute-start | bytes 49160 | tf_op jit(solution)/shard_map/ppermute | solution.py:485
  72.2 7.1 %collective-permute-start.14 = (f32[2,136,128]{2,1,0:T(8,128)S(1)}, f32[2,136,128]{2,1,0:T(8,128)S(1)}, u32[]{:S(2)}, u32[]{:S(2)}) collective-permute-start(f32[2,136,128]{2,1,0:T(8,128)S(1)} %pad_maximum_fusion.6), channel_id=1, source_target_pairs={{0,128},{8,136},{16,144},{24,152},{32,160},{40,168},{48,176},{56,1... | collective-permute-start | bytes 417800 | tf_op jit(solution)/shard_map/ppermute | solution.py:476
  81.4 10.4 %all-to-all-start.2 = ((f32[8,32,128]{2,1,0:T(8,128)}), f32[8,32,128]{2,1,0:T(8,128)S(1)}, u32[]{:S(2)}, u32[]{:S(2)}) async-start(f32[8,32,128]{2,1,0:T(8,128)} %carried_states.1), calls=%async_computation.2 | async-start | bytes 262144 | tf_op jit(solution)/shard_map/all_to_all | solution.py:572
  87.0 26.4 %copy-start = (bf16[4,512,512]{2,1,0:T(8,128)(2,1)S(1)}, bf16[4,512,512]{2,1,0:T(8,128)(2,1)}, u32[]{:S(2)}) copy-start(bf16[4,512,512]{2,1,0:T(8,128)(2,1)} %get-tuple-element.74.restore.refs_8_) | copy-start | bytes 6291460
  94.4 9.8 %collective-permute-start.15 = (bf16[256,512]{1,0:T(8,128)(2,1)S(1)}, bf16[256,512]{1,0:T(8,128)(2,1)S(1)}, u32[]{:S(2)}, u32[]{:S(2)}) collective-permute-start(bf16[256,512]{1,0:T(8,128)(2,1)S(1)} %get-tuple-element.104.refs_1_), channel_id=1, source_target_pairs={{0,8},{8,16},{16,24},{24,32},{32,40},{40,48},{48,56},{56,64},{64,7... | collective-permute-start | bytes 786440 | tf_op jit(solution)/shard_map/ppermute | solution.py:485
  94.5 10.7 %collective-permute-start.16 = (bf16[256,512]{1,0:T(8,128)(2,1)S(1)}, bf16[256,512]{1,0:T(8,128)(2,1)S(1)}, u32[]{:S(2)}, u32[]{:S(2)}) collective-permute-start(bf16[256,512]{1,0:T(8,128)(2,1)S(1)} %get-tuple-element.103.refs_0_), channel_id=1, source_target_pairs={{0,248},{8,0},{16,8},{24,16},{32,24},{40,32},{48,40},{56,48},{64,5... | collective-permute-start | bytes 786440 | tf_op jit(solution)/shard_map/ppermute | solution.py:485
  99.2 14.2 %collective-permute-start.17 = (bf16[256,512]{1,0:T(8,128)(2,1)S(1)}, bf16[256,512]{1,0:T(8,128)(2,1)S(1)}, u32[]{:S(2)}, u32[]{:S(2)}) collective-permute-start(bf16[256,512]{1,0:T(8,128)(2,1)S(1)} %get-tuple-element.106.refs_3_), channel_id=1, source_target_pairs={{0,1},{1,2},{2,3},{3,4},{4,5},{5,6},{6,7},{7,0},{8,9},{9,10},{10,1... | collective-permute-start | bytes 786440 | tf_op jit(solution)/shard_map/ppermute | solution.py:485
  99.7 13.6 %collective-permute-start.18 = (bf16[256,512]{1,0:T(8,128)(2,1)S(1)}, bf16[256,512]{1,0:T(8,128)(2,1)S(1)}, u32[]{:S(2)}, u32[]{:S(2)}) collective-permute-start(bf16[256,512]{1,0:T(8,128)(2,1)S(1)} %get-tuple-element.105.refs_2_), channel_id=1, source_target_pairs={{0,7},{1,0},{2,1},{3,2},{4,3},{5,4},{6,5},{7,6},{8,15},{9,8},{10,9... | collective-permute-start | bytes 786440 | tf_op jit(solution)/shard_map/ppermute | solution.py:485

commit v4 on v3

--- a/solution.py
+++ b/solution.py
@@ -50,14 +50,9 @@
 
 
 def canon_kernel(slot, parts, order, *outs):
-    d = pl.program_id(0)
-    table = sorting_table(order, slot[d]).astype(BF16)
-    value = times(parts[0], table).astype(BF16)
-    for i, out in enumerate(outs):
-
-        @pl.when(d == i)
-        def _():
-            out[...] = value
+    for d, out in enumerate(outs):
+        s = slot[d]
+        out[...] = times(parts[s], sorting_table(order, s).astype(BF16)).astype(BF16)
 
 
 def to_canonical(slot, parts, order):
@@ -67,11 +62,8 @@
         out_shape=[jax.ShapeDtypeStruct((samples, size), BF16)] * faces,
         grid_spec=pltpu.PrefetchScalarGridSpec(
             num_scalar_prefetch=1,
-            grid=(faces,),
-            in_specs=[
-                pl.BlockSpec((1, samples, size), lambda d, slot: (slot[d], 0, 0)),
-                resident((faces, size)),
-            ],
+            grid=(1,),
+            in_specs=[resident(parts.shape), resident((faces, size))],
             out_specs=[IN_VMEM] * faces,
         ),
         compiler_params=params(8),
@@ -80,11 +72,12 @@
     )(slot, in_hbm(parts), in_hbm(order))
 
 
-def tables_kernel(slot, order, basis, sort, restore, ordered, ordered_columns):
+def tables_kernel(slot, order, basis, sort, restore, restore_near, ordered, ordered_columns):
     d = pl.program_id(0)
     table = sorting_table(order, slot[d])
     sort[0] = table.astype(BF16)
     restore[0] = table.T.astype(BF16)
+    restore_near[0] = restore[0]
     ordered[0] = times(restore[0], basis[0]).astype(BF16)
     ordered_columns[0] = times_columns(basis[0], sort[0]).astype(BF16)
 
@@ -100,6 +93,7 @@
         out_shape=[
             pltpu.HBM((faces, size, size), BF16),
             pltpu.HBM((faces, size, size), BF16),
+            jax.ShapeDtypeStruct((faces, size, size), BF16),
             jax.ShapeDtypeStruct((faces, size, primal), BF16),
             pltpu.HBM((faces, primal, size), BF16),
         ],
@@ -113,6 +107,7 @@
             out_specs=[
                 by_direction(size, size),
                 by_direction(size, size),
+                by_direction(size, size),
                 by_direction(size, primal),
                 by_direction(primal, size),
             ],
@@ -136,16 +131,17 @@
     return own + jnp.where(has_neighbour(d), beside, 0.0)
 
 
-def residual_kernel(scale, *refs):
+def residual_kernel(slot, scale, *refs):
     faces = scale.shape[0]
     canon, beside = refs[:faces], refs[faces : 2 * faces]
-    ordered, handoff, averaged, coarse, heat = refs[2 * faces :]
+    ordered, restore, handoff, mask, masked, coarse, heat = refs[2 * faces :]
     total = None
     for d in range(faces):
         value = (scale[d] * sum_across(canon[d], beside[d], d)).astype(BF16)
-        averaged[d] = value
         term = times(value, ordered[d])
         total = term if total is None else total + term
+        s = slot[d]
+        masked[s] = (times(value, restore[d]) * mask[s]).astype(BF16)
     rounded = total.astype(BF16)
     coarse[...] = rounded
     primal = rounded.shape[1]
@@ -153,7 +149,7 @@
     heat[...] = times(rounded, handoff[pl.ds(start, primal), :])
 
 
-def residuals(scale, canon, beside, ordered, handoff):
+def residuals(slot, scale, canon, beside, ordered, restore, handoff, mask):
     faces, size, primal = ordered.shape
     samples = canon[0].shape[0]
     channels = handoff.shape[1]
@@ -164,15 +160,19 @@
             jax.ShapeDtypeStruct((samples, primal), BF16),
             jax.ShapeDtypeStruct((samples, channels), F32),
         ],
-        grid=(1,),
-        in_specs=[pl.BlockSpec(memory_space=pltpu.SMEM)] + [IN_VMEM] * (2 * faces + 2),
-        out_specs=[resident((faces, samples, size)), IN_VMEM, IN_VMEM],
-        compiler_params=params(8),
-        cost_estimate=cost(
-            2 * faces * samples * size * primal, 6 * faces * samples * size + 2 * faces * size * primal
+        grid_spec=pltpu.PrefetchScalarGridSpec(
+            num_scalar_prefetch=1,
+            grid=(1,),
+            in_specs=[pl.BlockSpec(memory_space=pltpu.SMEM)] + [IN_VMEM] * (2 * faces + 4),
+            out_specs=[resident((faces, samples, size)), IN_VMEM, IN_VMEM],
+        ),
+        compiler_params=params(8),
+        cost_estimate=cost(
+            2 * faces * samples * size * (primal + size),
+            6 * faces * samples * size + 2 * faces * size * (primal + size),
         ),
         name="residuals",
-    )(scale, *canon, *beside, ordered, handoff)
+    )(slot, scale, *canon, *beside, ordered, restore, handoff, mask)
 
 
 def share_kernel(inflow, out):
@@ -191,31 +191,6 @@
         cost_estimate=cost(members * share * channels, 4 * (copies + members) * share * channels),
         name="shared_sum",
     )(inflow)
-
-
-def local_kernel(slot, averaged, restore, mask, out):
-    for d in range(averaged.shape[0]):
-        s = slot[d]
-        out[s] = (times(averaged[d], restore[d]) * mask[s]).astype(BF16)
-
-
-def masked_local(slot, averaged, restore, mask):
-    faces, samples, size = averaged.shape
-    return pl.pallas_call(
-        local_kernel,
-        out_shape=pltpu.HBM(averaged.shape, BF16),
-        grid_spec=pltpu.PrefetchScalarGridSpec(
-            num_scalar_prefetch=1,
-            grid=(1,),
-            in_specs=[resident(averaged.shape), resident(restore.shape), resident(mask.shape)],
-            out_specs=resident(averaged.shape),
-        ),
-        compiler_params=params(12),
-        cost_estimate=cost(
-            2 * faces * samples * size * size, 4 * faces * samples * size + 2 * faces * size * size
-        ),
-        name="masked_local",
-    )(slot, in_hbm(averaged), in_hbm(restore), mask)
 
 
 def dual_kernel(first, slot, scale, masked, sort, mask, inverse, out):
@@ -520,47 +495,44 @@
     groups = lines // GROUP
     inside = [[a * GROUP + b for b in range(GROUP)] for a in range(groups)]
     copied = exchange(chain_transfer, "sub", DOUBLING[0])
+    positions = lax.broadcasted_iota(jnp.int32, (vertex_unknowns.shape[2], faces * size), 1)
+    hits = jnp.sum((vertex_unknowns[0, 0][:, None] == positions).astype(F32), axis=0)
+    mask = (1.0 - hits).reshape(faces, 1, size)
 
     canon = to_canonical(slot, parts, order)
-    copied, canon = lax.optimization_barrier((copied, canon))
+    beside = neighbours(canon)
+    copied, basis, canon, mask = lax.optimization_barrier((copied, basis, canon, mask))
     transfer = jnp.concatenate([chain_transfer, copied])
     copied = exchange(transfer, "sub", DOUBLING[1])
-    beside = neighbours(canon)
-    basis, canon = lax.optimization_barrier((basis, canon))
-    sort, restore, ordered, ordered_columns = tables(slot, order, basis)
-    averaged, coarse_residual, heat = residuals(
-        scale, canon, beside, ordered, thermal_handoff[0]
+    sort, restore, restore_near, ordered, ordered_columns = tables(slot, order, basis)
+    masked, coarse_residual, heat = residuals(
+        slot, scale, canon, beside, ordered, restore_near, thermal_handoff[0], mask
     )
     copied, heat = lax.optimization_barrier((copied, heat))
     transfer = doubled(jnp.concatenate([transfer, copied]), "sub", DOUBLING[2])
-    positions = lax.broadcasted_iota(jnp.int32, (vertex_unknowns.shape[2], faces * size), 1)
-    hits = jnp.sum((vertex_unknowns[0, 0][:, None] == positions).astype(F32), axis=0)
-    mask = (1.0 - hits).reshape(faces, 1, size)
 
     channels = heat.shape[1]
     gathered = coarse_residual[None]
     received = exchange(gathered, "coarse", GATHER_STAGES[0])
     inflow = lax.all_to_all(heat.reshape(members, share, channels), "coarse", 0, 0)
-    masked = masked_local(slot, averaged, restore, mask)
-    inflow, masked = lax.optimization_barrier((inflow, masked))
+    maps, product = group_maps(transfer)
+    inflow, maps, product = lax.optimization_barrier((inflow, maps, product))
     inflow = shared_sum(inflow, GROUP)
-    masked, transfer, received, inflow = lax.optimization_barrier((masked, transfer, received, inflow))
+    masked, received, inflow = lax.optimization_barrier((masked, received, inflow))
 
     inflow = lax.all_to_all(inflow, "sub", 0, 0, axis_index_groups=inside)
-    half = faces // 2
-    dual0 = dual(0, half, slot, scale, masked, sort, mask, front_inverse[0, 0])
-    transfer, dual0 = lax.optimization_barrier((transfer, dual0))
-    maps, product = group_maps(transfer)
     others = exchange(product, "sub", GROUP)
     gathered = jnp.concatenate([gathered, received])
     received = exchange(gathered, "coarse", GATHER_STAGES[1])
-    inflow, maps, masked = lax.optimization_barrier((inflow, maps, masked))
-
-    outflow = group_outflow(inflow, maps)
-    masked, others, received, outflow = lax.optimization_barrier((masked, others, received, outflow))
-    outflows = [shifted(outflow, "sub", GROUP * step) for step in range(groups - 1, 0, -1)]
+    half = faces // 2
+    dual0 = dual(0, half, slot, scale, masked, sort, mask, front_inverse[0, 0])
+    inflow, others, dual0, masked = lax.optimization_barrier((inflow, others, dual0, masked))
     product = jnp.concatenate([product, others])
     others = exchange(product, "sub", 2 * GROUP)
+
+    outflow = group_outflow(inflow, maps)
+    masked, received, outflow = lax.optimization_barrier((masked, received, outflow))
+    outflows = [shifted(outflow, "sub", GROUP * step) for step in range(groups - 1, 0, -1)]
     gathered = jnp.concatenate([gathered, received])
     masked, gathered = lax.optimization_barrier((masked, gathered))
     dual1 = dual(half, half, slot, scale, masked, sort, mask, front_inverse[0, 0])

time: 117 us -> 112 us (0.957)
  Pallas kernels: 40.1 us -> 36 us
  starting transfers between devices: 51.8 us -> 48.8 us
  waiting for transfers between devices: 22.2 us -> 23.4 us
    pallas_call x1 -> x0, Pallas kernels: 4.21 us -> none  [masked_local(): pl.pallas_call(local_kernel, out_shape=pltpu.HBM(averaged.shape, BF16), g...]
    all_to_all x1, starting transfers between devices: 6.18 us -> 3.37 us  [per_device(): inflow = lax.all_to_all(inflow, 'sub', 0, 0, axis_index_groups=inside)]
    ppermute x11, waiting for transfers between devices: 15 us -> 12.5 us  [shifted(): lax.ppermute(value, axis, [(i, (i + step) % count) for i in range(count)])]
    all_to_all x1, waiting for transfers between devices: 0.01 us -> 1.5 us  [per_device(): lax.all_to_all(heat.reshape(members, share, channels), 'coarse', 0, 0)]
    all_to_all x1, waiting for transfers between devices: 1.93 us -> 3.27 us  [per_device(): inflow = lax.all_to_all(inflow, 'sub', 0, 0, axis_index_groups=inside)]
    pallas_call x1, Pallas kernels: 2.02 us -> 3.21 us  [residuals(): pl.pallas_call(residual_kernel, out_shape=[pltpu.HBM((faces, samples, siz...]
  transfers between devices with their start and end apart: 22 -> 22, of which waited for: 8 -> 7; matrix products, arithmetic and copies ran while one was open for 1% -> 2% of each run, Pallas kernels for 30% -> 27%
where the time goes in v4:
time: 112 us; the launch traced here: 111 us
  starting transfers between devices  48.8 us (44%)
  Pallas kernels  36 us (32%)
  waiting for transfers between devices  23.4 us (21%)
  other arithmetic  2.15 us (2%)
    ppermute x11, starting transfers between devices, shifted(): lax.ppermute(value, axis, [(i, (i + step) % count) for i in range(count)])  22 us
    ppermute x8, starting transfers between devices, exchange(): lax.ppermute(value, axis, [(i, i ^ bit) for i in range(lax.axis_size(axis...  15.9 us
    ppermute x11, waiting for transfers between devices, shifted(): lax.ppermute(value, axis, [(i, (i + step) % count) for i in range(count)])  12.5 us
    pallas_call x2, Pallas kernels, dual(): pl.pallas_call(functools.partial(dual_kernel, first), out_shape=pltpu.HBM...  11.3 us
    pallas_call x1, Pallas kernels, tables(): pl.pallas_call(tables_kernel, out_shape=[pltpu.HBM((faces, size, size), B...  5.26 us
    all_to_all x1, waiting for transfers between devices, per_device(): carried = lax.all_to_all(carried, 'coarse', 0, 0).reshape(samples, channels)  4.79 us
    all_to_all x1, starting transfers between devices, per_device(): carried = lax.all_to_all(carried, 'coarse', 0, 0).reshape(samples, channels)  3.91 us
    all_to_all x1, starting transfers between devices, per_device(): lax.all_to_all(heat.reshape(members, share, channels), 'coarse', 0, 0)  3.66 us
  transfers between devices with their start and end apart: 22, of which 7 were waited for; matrix products, arithmetic and copies ran while one was open for 2% of the time, Pallas kernels for 27%

profile of v4, /device:TPU:2, one launch (start us, length us, event | category | flops | bytes accessed | tf_op | source)
XLA Modules:
  0.0 111.3 jit_solution(18354132618991324360)
XLA Ops:
  0.0 7.2 %collective-permute-start = (f32[1,128,128]{2,1,0:T(8,128)}, f32[1,128,128]{2,1,0:T(8,128)S(1)}, u32[]{:S(2)}, u32[]{:S(2)}) collective-permute-start(f32[1,128,128]{2,1,0:T(8,128)} %param.20), channel_id=1, source_target_pairs={{0,32},{8,40},{16,48},{24,56},{32,0},{40,8},{48,16},{56,24},{64,96... | collective-permute-start | bytes 196616 | tf_op jit(solution)/shard_map/ppermute | solution.py:451
  7.8 2.5 %canon.1 = (bf16[256,512]{1,0:T(8,128)(2,1)S(1)}, bf16[256,512]{1,0:T(8,128)(2,1)S(1)}, bf16[256,512]{1,0:T(8,128)(2,1)S(1)}, bf16[256,512]{1,0:T(8,128)(2,1)S(1)}) custom-call(s32[4]{0:T(128)S(1)} %bitcast.27, bf16[4,256,512]{2,1,0:T(8,128)(2,1)} %bitcast.38, s32[4,512]{1,0:T(4,128)} %bitcast.40), custom_call_target="tpu_custom_call" | custom-call | flops 536870912 | bytes 2097152 | tf_op jit(solution)/shard_map/canon/pallas_call | solution.py:60
  10.4 4.7 %collective-permute-start.2 = (bf16[256,512]{1,0:T(8,128)(2,1)S(1)}, bf16[256,512]{1,0:T(8,128)(2,1)S(1)}, u32[]{:S(2)}, u32[]{:S(2)}) collective-permute-start(bf16[256,512]{1,0:T(8,128)(2,1)S(1)} %get-tuple-element.56.refs_0_), channel_id=1, source_target_pairs={{0,248},{8,0},{16,8},{24,16},{32,24},{40,32},{48,40},{56,48},{64,5... | collective-permute-start | bytes 786440 | tf_op jit(solution)/shard_map/ppermute | solution.py:460
  15.2 1.6 %collective-permute-start.3 = (bf16[256,512]{1,0:T(8,128)(2,1)S(1)}, bf16[256,512]{1,0:T(8,128)(2,1)S(1)}, u32[]{:S(2)}, u32[]{:S(2)}) collective-permute-start(bf16[256,512]{1,0:T(8,128)(2,1)S(1)} %get-tuple-element.59.refs_3_), channel_id=1, source_target_pairs={{0,1},{1,2},{2,3},{3,4},{4,5},{5,6},{6,7},{7,0},{8,9},{9,10},{10,1... | collective-permute-start | bytes 786440 | tf_op jit(solution)/shard_map/ppermute | solution.py:460
  16.8 2.6 %collective-permute-start.4 = (bf16[256,512]{1,0:T(8,128)(2,1)S(1)}, bf16[256,512]{1,0:T(8,128)(2,1)S(1)}, u32[]{:S(2)}, u32[]{:S(2)}) collective-permute-start(bf16[256,512]{1,0:T(8,128)(2,1)S(1)} %get-tuple-element.58.refs_2_), channel_id=1, source_target_pairs={{0,7},{1,0},{2,1},{3,2},{4,3},{5,4},{6,5},{7,6},{8,15},{9,8},{10,9... | collective-permute-start | bytes 786440 | tf_op jit(solution)/shard_map/ppermute | solution.py:460
  21.4 5.3 %tables.1 = (bf16[4,512,512]{2,1,0:T(8,128)(2,1)}, bf16[4,512,512]{2,1,0:T(8,128)(2,1)}, bf16[4,512,512]{2,1,0:T(8,128)(2,1)S(1)}, bf16[4,512,256]{2,1,0:T(8,128)(2,1)S(1)}, bf16[4,256,512]{2,1,0:T(8,128)(2,1)}) custom-call(s32[4]{0:T(128)S(1)} %bitcast.28, s32[4,512]{1,0:T(4,128)} %bitcast.41, bf16[4,512,256]{2,1,0:T(8,128)(2,1)} %bitcast.39), custom_call_target="tpu_custom_call" | custom-call | flops 1073741824 | bytes 7340032 | tf_op jit(solution)/shard_map/tables/pallas_call | solution.py:91
  26.6 4.1 %collective-permute-done.3.refs_6_ = bf16[256,512]{1,0:T(8,128)(2,1)S(1)} collective-permute-done((bf16[256,512]{1,0:T(8,128)(2,1)S(1)}, bf16[256,512]{1,0:T(8,128)(2,1)S(1)}, u32[]{:S(2)}, u32[]{:S(2)}) %collective-permute-start.3) | collective-permute-done | bytes 262176 | tf_op jit(solution)/shard_map/ppermute | solution.py:460
  30.8 3.2 %residuals.1 = (bf16[4,256,512]{2,1,0:T(8,128)(2,1)}, bf16[256,256]{1,0:T(8,128)(2,1)S(1)}, f32[256,128]{1,0:T(8,128)}) custom-call(s32[4]{0:T(128)S(1)} %bitcast.29, f32[4]{0:T(128)S(1)} %bitcast.23, bf16[256,512]{1,0:T(8,128)(2,1)S(1)} %get-tuple-element.56.refs_0_, bf16[256,512]{1,0:T(8,128)(2,1)S(1)} %get-tuple-element.57.refs_1_, ...), custom_call_target="tpu_custom_call" | custom-call | flops 805306368 | bytes 6291456 | tf_op jit(solution)/shard_map/residuals/pallas_call | solution.py:156
  34.1 3.7 %all-to-all-start = ((f32[8,32,128]{2,1,0:T(8,128)}), f32[8,32,128]{2,1,0:T(8,128)S(1)}, u32[]{:S(2)}, u32[]{:S(2)}) async-start(f32[8,32,128]{2,1,0:T(8,128)} %bitcast.9), calls=%async_computation | async-start | bytes 262144 | tf_op jit(solution)/shard_map/all_to_all | solution.py:517
  37.8 3.5 %collective-permute-start.5 = (bf16[1,256,256]{2,1,0:T(8,128)(2,1)S(1)}, bf16[1,256,256]{2,1,0:T(8,128)(2,1)S(1)}, u32[]{:S(2)}, u32[]{:S(2)}) collective-permute-start(bf16[1,256,256]{2,1,0:T(8,128)(2,1)S(1)} %bitcast.16), channel_id=1, source_target_pairs={{0,2},{1,3},{2,0},{3,1},{4,6},{5,7},{6,4},{7,5},{8,10},{9,11},{10,... | collective-permute-start | bytes 393224 | tf_op jit(solution)/shard_map/ppermute | solution.py:451
  41.3 1.6 %group_maps.1 = (bf16[16,128,128]{2,1,0:T(8,128)(2,1)}, f32[1,136,128]{2,1,0:T(8,128)S(1)}) custom-call(f32[8,128,128]{2,1,0:T(8,128)S(1)} %pad_maximum_fusion.1.transfer), custom_call_target="tpu_custom_call" | custom-call | flops 100663296 | bytes 1048576 | tf_op jit(solution)/shard_map/group_maps/pallas_call | solution.py:264
  43.0 1.5 %all-to-all-done.inflow = f32[8,32,128]{2,1,0:T(8,128)S(1)} async-done(((f32[8,32,128]{2,1,0:T(8,128)}), f32[8,32,128]{2,1,0:T(8,128)S(1)}, u32[]{:S(2)}, u32[]{:S(2)}) %all-to-all-start) | async-done | bytes 131104 | tf_op jit(solution)/shard_map/all_to_all | solution.py:517
  45.1 1.4 %collective-permute-done.5 = bf16[1,256,256]{2,1,0:T(8,128)(2,1)S(1)} collective-permute-done((bf16[1,256,256]{2,1,0:T(8,128)(2,1)S(1)}, bf16[1,256,256]{2,1,0:T(8,128)(2,1)S(1)}, u32[]{:S(2)}, u32[]{:S(2)}) %collective-permute-start.5) | collective-permute-done | bytes 131104 | tf_op jit(solution)/shard_map/ppermute | solution.py:451
  47.6 3.4 %all-to-all-start.1 = ((f32[8,32,128]{2,1,0:T(8,128)}), f32[8,32,128]{2,1,0:T(8,128)S(1)}, u32[]{:S(2)}, u32[]{:S(2)}) async-start(f32[8,32,128]{2,1,0:T(8,128)} %shared_sum.1), calls=%async_computation.1 | async-start | bytes 262144 | tf_op jit(solution)/shard_map/all_to_all | solution.py:523
  51.6 5.7 %dual0.1 = f32[2,256,512]{2,1,0:T(8,128)} custom-call(s32[4]{0:T(128)S(1)} %bitcast.30, f32[4]{0:T(128)S(1)} %bitcast.24, bf16[4,256,512]{2,1,0:T(8,128)(2,1)} %get-tuple-element.86.masked, bf16[4,512,512]{2,1,0:T(8,128)(2,1)} %get-tuple-element.76.sort, f32[4,1,512]{2,1,0:T(1,128)S(1)} %bitcast.21, bf16[2048,2048]{1,0:T(8,128)(2,1)} %bitcast.33), custom_call_target="tpu_custom_call" | custom-call | flops 1610612736 | bytes 8388608 | tf_op jit(solution)/shard_map/dual0/pallas_call | solution.py:209
  57.3 3.3 %all-to-all-done.1.inflow = f32[8,32,128]{2,1,0:T(8,128)S(1)} async-done(((f32[8,32,128]{2,1,0:T(8,128)}), f32[8,32,128]{2,1,0:T(8,128)S(1)}, u32[]{:S(2)}, u32[]{:S(2)}) %all-to-all-start.1) | async-done | bytes 131104 | tf_op jit(solution)/shard_map/all_to_all | solution.py:523
  60.6 2.1 %group_outflow.1 = f32[32,128]{1,0:T(8,128)S(1)} custom-call(f32[8,32,128]{2,1,0:T(8,128)S(1)} %all-to-all-done.1.inflow, bf16[16,128,128]{2,1,0:T(8,128)(2,1)} %get-tuple-element.80.maps), custom_call_target="tpu_custom_call" | custom-call | flops 25165824 | bytes 655360 | tf_op jit(solution)/shard_map/group_outflow/pallas_call | solution.py:299
  62.7 1.1 collective-permute-start.10
  63.9 2.2 %collective-permute-start.14 = (f32[2,136,128]{2,1,0:T(8,128)S(1)}, f32[2,136,128]{2,1,0:T(8,128)S(1)}, u32[]{:S(2)}, u32[]{:S(2)}) collective-permute-start(f32[2,136,128]{2,1,0:T(8,128)S(1)} %pad_maximum_fusion.6), channel_id=1, source_target_pairs={{0,128},{8,136},{16,144},{24,152},{32,160},{40,168},{48,176},{56,1... | collective-permute-start | bytes 417800 | tf_op jit(solution)/shard_map/ppermute | solution.py:451
  66.1 1.4 %collective-permute-start.11 = (f32[32,128]{1,0:T(8,128)S(1)}, f32[32,128]{1,0:T(8,128)S(1)}, u32[]{:S(2)}, u32[]{:S(2)}) collective-permute-start(f32[32,128]{1,0:T(8,128)S(1)} %group_outflow.1), channel_id=1, source_target_pairs={{0,192},{8,200},{16,208},{24,216},{32,224},{40,232},{48,240},{56,2... | collective-permute-start | bytes 49160 | tf_op jit(solution)/shard_map/ppermute | solution.py:460
  67.5 2.6 %collective-permute-start.13 = (f32[32,128]{1,0:T(8,128)S(1)}, f32[32,128]{1,0:T(8,128)S(1)}, u32[]{:S(2)}, u32[]{:S(2)}) collective-permute-start(f32[32,128]{1,0:T(8,128)S(1)} %group_outflow.1), channel_id=1, source_target_pairs={{0,64},{8,72},{16,80},{24,88},{32,96},{40,104},{48,112},{56,120},{... | collective-permute-start | bytes 49160 | tf_op jit(solution)/shard_map/ppermute | solution.py:460
  70.1 5.6 %dual2.1.dual1 = f32[2,256,512]{2,1,0:T(8,128)} custom-call(s32[4]{0:T(128)S(1)} %bitcast.31, f32[4]{0:T(128)S(1)} %bitcast.25, bf16[4,256,512]{2,1,0:T(8,128)(2,1)} %get-tuple-element.86.masked, bf16[4,512,512]{2,1,0:T(8,128)(2,1)} %get-tuple-element.76.sort, f32[4,1,512]{2,1,0:T(1,128)S(1)} %bitcast.22, bf16[2048,2048]{1,0:T(8,128)(2,1)} %bitcast.34), custom_call_target="tpu_custom_call" | custom-call | flops 1610612736 | bytes 8388608 | tf_op jit(solution)/shard_map/dual2/pallas_call | solution.py:209
  75.7 2.2 %carried_states.1 = f32[8,32,128]{2,1,0:T(8,128)} custom-call(f32[4,136,128]{2,1,0:T(8,128)S(1)} %pad_maximum_fusion.3.products, f32[8,32,128]{2,1,0:T(8,128)S(1)} %all-to-all-done.1.inflow, bf16[16,128,128]{2,1,0:T(8,128)(2,1)} %get-tuple-element.80.maps, f32[32,128]{1,0:T(8,128)S(1)} %collective-permute-done.11.refs_0_, ...), custom_call_target="tpu_custom_call" | custom-call | flops 25165824 | bytes 1310720 | tf_op jit(solution)/shard_map/carried_states/pallas_call | solution.py:331
  77.9 3.9 %all-to-all-start.2 = ((f32[8,32,128]{2,1,0:T(8,128)}), f32[8,32,128]{2,1,0:T(8,128)S(1)}, u32[]{:S(2)}, u32[]{:S(2)}) async-start(f32[8,32,128]{2,1,0:T(8,128)} %carried_states.1), calls=%async_computation.2 | async-start | bytes 262144 | tf_op jit(solution)/shard_map/all_to_all | solution.py:544
  81.9 1.7 %line_base.1.base = f32[256,256]{1,0:T(8,128)S(1)} custom-call(bf16[8,256,256]{2,1,0:T(8,128)(2,1)S(1)} %pad_maximum_fusion.gathered, bf16[2048,256]{1,0:T(8,128)(2,1)} %bitcast.35), custom_call_target="tpu_custom_call" | custom-call | flops 268435456 | bytes 2097152 | tf_op jit(solution)/shard_map/line_base/pallas_call | solution.py:363
  83.6 4.8 %all-to-all-done.2 = f32[8,32,128]{2,1,0:T(8,128)S(1)} async-done(((f32[8,32,128]{2,1,0:T(8,128)}), f32[8,32,128]{2,1,0:T(8,128)S(1)}, u32[]{:S(2)}, u32[]{:S(2)}) %all-to-all-start.2) | async-done | bytes 131104 | tf_op jit(solution)/shard_map/all_to_all | solution.py:544
  88.4 2.6 %extend.1 = (bf16[256,512]{1,0:T(8,128)(2,1)S(1)}, bf16[256,512]{1,0:T(8,128)(2,1)S(1)}, bf16[256,512]{1,0:T(8,128)(2,1)S(1)}, bf16[256,512]{1,0:T(8,128)(2,1)S(1)}) custom-call(f32[4]{0:T(128)S(1)} %bitcast.26, f32[256,256]{1,0:T(8,128)S(1)} %line_base.1.base, f32[256,128]{1,0:T(8,128)S(1)} %bitcast.19, bf16[128,256]{1,0:T(8,128)(2,1)} %bitcast.36, ...), custom_call_target="tpu_custom_call" | custom-call | flops 268435456 | bytes 4194304 | tf_op jit(solution)/shard_map/extend/pallas_call | solution.py:391
  91.1 4.7 %collective-permute-start.16 = (bf16[256,512]{1,0:T(8,128)(2,1)S(1)}, bf16[256,512]{1,0:T(8,128)(2,1)S(1)}, u32[]{:S(2)}, u32[]{:S(2)}) collective-permute-start(bf16[256,512]{1,0:T(8,128)(2,1)S(1)} %get-tuple-element.94.refs_0_), channel_id=1, source_target_pairs={{0,248},{8,0},{16,8},{24,16},{32,24},{40,32},{48,40},{56,48},{64,5... | collective-permute-start | bytes 786440 | tf_op jit(solution)/shard_map/ppermute | solution.py:460
  96.3 3.6 %collective-permute-start.18 = (bf16[256,512]{1,0:T(8,128)(2,1)S(1)}, bf16[256,512]{1,0:T(8,128)(2,1)S(1)}, u32[]{:S(2)}, u32[]{:S(2)}) collective-permute-start(bf16[256,512]{1,0:T(8,128)(2,1)S(1)} %get-tuple-element.96.refs_2_), channel_id=1, source_target_pairs={{0,7},{1,0},{2,1},{3,2},{4,3},{5,4},{6,5},{7,6},{8,15},{9,8},{10,9... | collective-permute-start | bytes 786440 | tf_op jit(solution)/shard_map/ppermute | solution.py:460
  99.9 2.8 %collective-permute-done.15.refs_4_ = bf16[256,512]{1,0:T(8,128)(2,1)S(1)} collective-permute-done((bf16[256,512]{1,0:T(8,128)(2,1)S(1)}, bf16[256,512]{1,0:T(8,128)(2,1)S(1)}, u32[]{:S(2)}, u32[]{:S(2)}) %collective-permute-start.15) | collective-permute-done | bytes 262176 | tf_op jit(solution)/shard_map/ppermute | solution.py:460
  102.7 5.6 %collective-permute-done.17.refs_6_ = bf16[256,512]{1,0:T(8,128)(2,1)S(1)} collective-permute-done((bf16[256,512]{1,0:T(8,128)(2,1)S(1)}, bf16[256,512]{1,0:T(8,128)(2,1)S(1)}, u32[]{:S(2)}, u32[]{:S(2)}) %collective-permute-start.17) | collective-permute-done | bytes 262176 | tf_op jit(solution)/shard_map/ppermute | solution.py:460
  108.3 3.0 %finish.1 = bf16[4,256,512]{2,1,0:T(8,128)(2,1)} custom-call(s32[4]{0:T(128)S(1)} %bitcast.32, bf16[256,512]{1,0:T(8,128)(2,1)S(1)} %get-tuple-element.94.refs_0_, bf16[256,512]{1,0:T(8,128)(2,1)S(1)} %get-tuple-element.95.refs_1_, bf16[256,512]{1,0:T(8,128)(2,1)S(1)} %get-tuple-element.96.refs_2_, bf16[256,512]{1,0:T(8,128)(2,1)S(1)} %get-tuple-element.97.refs_3_, ...), custom_call_target="tpu_custom_call" | custom-call | flops 536870912 | bytes 5242880 | tf_op jit(solution)/shard_map/finish/pallas_call | solution.py:428
  (46 shorter events, 6.1 us)
Async XLA Ops:
  0.0 21.4 %copy-start.4 = (s32[1,1,4]{2,1,0:T(1,128)S(1)}, s32[1,1,4]{2,1,0:T(1,128)}, u32[]{:S(2)}) copy-start(s32[1,1,4]{2,1,0:T(1,128)} %param.12) | copy-start | bytes 52
  0.0 20.3 %collective-permute-start = (f32[1,128,128]{2,1,0:T(8,128)}, f32[1,128,128]{2,1,0:T(8,128)S(1)}, u32[]{:S(2)}, u32[]{:S(2)}) collective-permute-start(f32[1,128,128]{2,1,0:T(8,128)} %param.20), channel_id=1, source_target_pairs={{0,32},{8,40},{16,48},{24,56},{32,0},{40,8},{48,16},{56,24},{64,96... | collective-permute-start | bytes 196616 | tf_op jit(solution)/shard_map/ppermute | solution.py:451
  7.2 0.7 copy-start.3
  10.3 16.3 %collective-permute-start.1 = (bf16[256,512]{1,0:T(8,128)(2,1)S(1)}, bf16[256,512]{1,0:T(8,128)(2,1)S(1)}, u32[]{:S(2)}, u32[]{:S(2)}) collective-permute-start(bf16[256,512]{1,0:T(8,128)(2,1)S(1)} %get-tuple-element.57.refs_1_), channel_id=1, source_target_pairs={{0,8},{8,16},{16,24},{24,32},{32,40},{40,48},{48,56},{56,64},{64,7... | collective-permute-start | bytes 786440 | tf_op jit(solution)/shard_map/ppermute | solution.py:460
  10.4 16.2 %collective-permute-start.2 = (bf16[256,512]{1,0:T(8,128)(2,1)S(1)}, bf16[256,512]{1,0:T(8,128)(2,1)S(1)}, u32[]{:S(2)}, u32[]{:S(2)}) collective-permute-start(bf16[256,512]{1,0:T(8,128)(2,1)S(1)} %get-tuple-element.56.refs_0_), channel_id=1, source_target_pairs={{0,248},{8,0},{16,8},{24,16},{32,24},{40,32},{48,40},{56,48},{64,5... | collective-permute-start | bytes 786440 | tf_op jit(solution)/shard_map/ppermute | solution.py:460
  15.2 15.6 %collective-permute-start.3 = (bf16[256,512]{1,0:T(8,128)(2,1)S(1)}, bf16[256,512]{1,0:T(8,128)(2,1)S(1)}, u32[]{:S(2)}, u32[]{:S(2)}) collective-permute-start(bf16[256,512]{1,0:T(8,128)(2,1)S(1)} %get-tuple-element.59.refs_3_), channel_id=1, source_target_pairs={{0,1},{1,2},{2,3},{3,4},{4,5},{5,6},{6,7},{7,0},{8,9},{9,10},{10,1... | collective-permute-start | bytes 786440 | tf_op jit(solution)/shard_map/ppermute | solution.py:460
  16.8 14.0 %collective-permute-start.4 = (bf16[256,512]{1,0:T(8,128)(2,1)S(1)}, bf16[256,512]{1,0:T(8,128)(2,1)S(1)}, u32[]{:S(2)}, u32[]{:S(2)}) collective-permute-start(bf16[256,512]{1,0:T(8,128)(2,1)S(1)} %get-tuple-element.58.refs_2_), channel_id=1, source_target_pairs={{0,7},{1,0},{2,1},{3,2},{4,3},{5,4},{6,5},{7,6},{8,15},{9,8},{10,9... | collective-permute-start | bytes 786440 | tf_op jit(solution)/shard_map/ppermute | solution.py:460
  20.3 10.4 %copy-start.1 = (bf16[1,2048,128]{2,1,0:T(8,128)(2,1)S(1)}, bf16[1,2048,128]{2,1,0:T(8,128)(2,1)}, u32[]{:S(2)}) copy-start(bf16[1,2048,128]{2,1,0:T(8,128)(2,1)} %param.19) | copy-start | bytes 1572868
  20.3 10.4 %copy-start.2 = (f32[1,1,4]{2,1,0:T(1,128)S(1)}, f32[1,1,4]{2,1,0:T(1,128)}, u32[]{:S(2)}) copy-start(f32[1,1,4]{2,1,0:T(1,128)} %param.14) | copy-start | bytes 52
  21.2 12.7 %collective-permute-start.6 = (f32[2,128,128]{2,1,0:T(8,128)S(1)}, f32[2,128,128]{2,1,0:T(8,128)S(1)}, u32[]{:S(2)}, u32[]{:S(2)}) collective-permute-start(f32[2,128,128]{2,1,0:T(8,128)S(1)} %pad_maximum_fusion.7), channel_id=1, source_target_pairs={{0,16},{8,24},{16,0},{24,8},{32,48},{40,56},{48,32},{56,40},{64,80... | collective-permute-start | bytes 393224 | tf_op jit(solution)/shard_map/ppermute | solution.py:451
  30.8 3.2 %copy-start.5 = (f32[1,128,128]{2,1,0:T(8,128)S(1)}, f32[1,128,128]{2,1,0:T(8,128)}, u32[]{:S(2)}) copy-start(f32[1,128,128]{2,1,0:T(8,128)} %param.20) | copy-start | bytes 196612
  34.0 7.3 %collective-permute-start.7 = (f32[4,128,128]{2,1,0:T(8,128)S(1)}, f32[4,128,128]{2,1,0:T(8,128)S(1)}, u32[]{:S(2)}, u32[]{:S(2)}) collective-permute-start(f32[4,128,128]{2,1,0:T(8,128)S(1)} %pad_maximum_fusion.4), channel_id=1, source_target_pairs={{0,8},{8,0},{16,24},{24,16},{32,40},{40,32},{48,56},{56,48},{64,72... | collective-permute-start | bytes 786440 | tf_op jit(solution)/shard_map/ppermute | solution.py:451
  34.1 10.4 %all-to-all-start = ((f32[8,32,128]{2,1,0:T(8,128)}), f32[8,32,128]{2,1,0:T(8,128)S(1)}, u32[]{:S(2)}, u32[]{:S(2)}) async-start(f32[8,32,128]{2,1,0:T(8,128)} %bitcast.9), calls=%async_computation | async-start | bytes 262144 | tf_op jit(solution)/shard_map/all_to_all | solution.py:517
  37.8 8.7 %collective-permute-start.5 = (bf16[1,256,256]{2,1,0:T(8,128)(2,1)S(1)}, bf16[1,256,256]{2,1,0:T(8,128)(2,1)S(1)}, u32[]{:S(2)}, u32[]{:S(2)}) collective-permute-start(bf16[1,256,256]{2,1,0:T(8,128)(2,1)S(1)} %bitcast.16), channel_id=1, source_target_pairs={{0,2},{1,3},{2,0},{3,1},{4,6},{5,7},{6,4},{7,5},{8,10},{9,11},{10,... | collective-permute-start | bytes 393224 | tf_op jit(solution)/shard_map/ppermute | solution.py:451
  46.5 16.2 %collective-permute-start.9 = (bf16[2,256,256]{2,1,0:T(8,128)(2,1)S(1)}, bf16[2,256,256]{2,1,0:T(8,128)(2,1)S(1)}, u32[]{:S(2)}, u32[]{:S(2)}) collective-permute-start(bf16[2,256,256]{2,1,0:T(8,128)(2,1)S(1)} %pad_maximum_fusion.5), channel_id=1, source_target_pairs={{0,1},{1,0},{2,3},{3,2},{4,5},{5,4},{6,7},{7,6},{8,9},{9,8},{10,11... | collective-permute-start | bytes 786440 | tf_op jit(solution)/shard_map/ppermute | solution.py:451
  47.6 13.0 %all-to-all-start.1 = ((f32[8,32,128]{2,1,0:T(8,128)}), f32[8,32,128]{2,1,0:T(8,128)S(1)}, u32[]{:S(2)}, u32[]{:S(2)}) async-start(f32[8,32,128]{2,1,0:T(8,128)} %shared_sum.1), calls=%async_computation.1 | async-start | bytes 262144 | tf_op jit(solution)/shard_map/all_to_all | solution.py:523
  51.0 6.3 %collective-permute-start.8 = (f32[1,136,128]{2,1,0:T(8,128)S(1)}, f32[1,136,128]{2,1,0:T(8,128)S(1)}, u32[]{:S(2)}, u32[]{:S(2)}) collective-permute-start(f32[1,136,128]{2,1,0:T(8,128)S(1)} %get-tuple-element.74), channel_id=1, source_target_pairs={{0,64},{8,72},{16,80},{24,88},{32,96},{40,104},{48,112},{56,120},{... | collective-permute-start | bytes 208904 | tf_op jit(solution)/shard_map/ppermute | solution.py:451
  62.7 19.1 %collective-permute-start.10 = (bf16[4,256,256]{2,1,0:T(8,128)(2,1)S(1)}, bf16[4,256,256]{2,1,0:T(8,128)(2,1)S(1)}, u32[]{:S(2)}, u32[]{:S(2)}) collective-permute-start(bf16[4,256,256]{2,1,0:T(8,128)(2,1)S(1)} %pad_maximum_fusion.2), channel_id=1, source_target_pairs={{0,4},{1,5},{2,6},{3,7},{4,0},{5,1},{6,2},{7,3},{8,12},{9,13},{10,... | collective-permute-start | bytes 1572872 | tf_op jit(solution)/shard_map/ppermute | solution.py:451
  63.9 11.8 %collective-permute-start.14 = (f32[2,136,128]{2,1,0:T(8,128)S(1)}, f32[2,136,128]{2,1,0:T(8,128)S(1)}, u32[]{:S(2)}, u32[]{:S(2)}) collective-permute-start(f32[2,136,128]{2,1,0:T(8,128)S(1)} %pad_maximum_fusion.6), channel_id=1, source_target_pairs={{0,128},{8,136},{16,144},{24,152},{32,160},{40,168},{48,176},{56,1... | collective-permute-start | bytes 417800 | tf_op jit(solution)/shard_map/ppermute | solution.py:451
  66.1 9.6 %collective-permute-start.11 = (f32[32,128]{1,0:T(8,128)S(1)}, f32[32,128]{1,0:T(8,128)S(1)}, u32[]{:S(2)}, u32[]{:S(2)}) collective-permute-start(f32[32,128]{1,0:T(8,128)S(1)} %group_outflow.1), channel_id=1, source_target_pairs={{0,192},{8,200},{16,208},{24,216},{32,224},{40,232},{48,240},{56,2... | collective-permute-start | bytes 49160 | tf_op jit(solution)/shard_map/ppermute | solution.py:460
  67.5 8.2 %collective-permute-start.12 = (f32[32,128]{1,0:T(8,128)S(1)}, f32[32,128]{1,0:T(8,128)S(1)}, u32[]{:S(2)}, u32[]{:S(2)}) collective-permute-start(f32[32,128]{1,0:T(8,128)S(1)} %group_outflow.1), channel_id=1, source_target_pairs={{0,128},{8,136},{16,144},{24,152},{32,160},{40,168},{48,176},{56,1... | collective-permute-start | bytes 49160 | tf_op jit(solution)/shard_map/ppermute | solution.py:460
  67.5 8.2 %collective-permute-start.13 = (f32[32,128]{1,0:T(8,128)S(1)}, f32[32,128]{1,0:T(8,128)S(1)}, u32[]{:S(2)}, u32[]{:S(2)}) collective-permute-start(f32[32,128]{1,0:T(8,128)S(1)} %group_outflow.1), channel_id=1, source_target_pairs={{0,64},{8,72},{16,80},{24,88},{32,96},{40,104},{48,112},{56,120},{... | collective-permute-start | bytes 49160 | tf_op jit(solution)/shard_map/ppermute | solution.py:460
  77.9 10.5 %all-to-all-start.2 = ((f32[8,32,128]{2,1,0:T(8,128)}), f32[8,32,128]{2,1,0:T(8,128)S(1)}, u32[]{:S(2)}, u32[]{:S(2)}) async-start(f32[8,32,128]{2,1,0:T(8,128)} %carried_states.1), calls=%async_computation.2 | async-start | bytes 262144 | tf_op jit(solution)/shard_map/all_to_all | solution.py:544
  83.6 24.7 %copy-start = (bf16[4,512,512]{2,1,0:T(8,128)(2,1)S(1)}, bf16[4,512,512]{2,1,0:T(8,128)(2,1)}, u32[]{:S(2)}) copy-start(bf16[4,512,512]{2,1,0:T(8,128)(2,1)} %get-tuple-element.98.refs_8_) | copy-start | bytes 6291460
  91.0 11.7 %collective-permute-start.15 = (bf16[256,512]{1,0:T(8,128)(2,1)S(1)}, bf16[256,512]{1,0:T(8,128)(2,1)S(1)}, u32[]{:S(2)}, u32[]{:S(2)}) collective-permute-start(bf16[256,512]{1,0:T(8,128)(2,1)S(1)} %get-tuple-element.95.refs_1_), channel_id=1, source_target_pairs={{0,8},{8,16},{16,24},{24,32},{32,40},{40,48},{48,56},{56,64},{64,7... | collective-permute-start | bytes 786440 | tf_op jit(solution)/shard_map/ppermute | solution.py:460
  91.1 11.6 %collective-permute-start.16 = (bf16[256,512]{1,0:T(8,128)(2,1)S(1)}, bf16[256,512]{1,0:T(8,128)(2,1)S(1)}, u32[]{:S(2)}, u32[]{:S(2)}) collective-permute-start(bf16[256,512]{1,0:T(8,128)(2,1)S(1)} %get-tuple-element.94.refs_0_), channel_id=1, source_target_pairs={{0,248},{8,0},{16,8},{24,16},{32,24},{40,32},{48,40},{56,48},{64,5... | collective-permute-start | bytes 786440 | tf_op jit(solution)/shard_map/ppermute | solution.py:460
  95.8 12.5 %collective-permute-start.17 = (bf16[256,512]{1,0:T(8,128)(2,1)S(1)}, bf16[256,512]{1,0:T(8,128)(2,1)S(1)}, u32[]{:S(2)}, u32[]{:S(2)}) collective-permute-start(bf16[256,512]{1,0:T(8,128)(2,1)S(1)} %get-tuple-element.97.refs_3_), channel_id=1, source_target_pairs={{0,1},{1,2},{2,3},{3,4},{4,5},{5,6},{6,7},{7,0},{8,9},{9,10},{10,1... | collective-permute-start | bytes 786440 | tf_op jit(solution)/shard_map/ppermute | solution.py:460
  96.3 12.0 %collective-permute-start.18 = (bf16[256,512]{1,0:T(8,128)(2,1)S(1)}, bf16[256,512]{1,0:T(8,128)(2,1)S(1)}, u32[]{:S(2)}, u32[]{:S(2)}) collective-permute-start(bf16[256,512]{1,0:T(8,128)(2,1)S(1)} %get-tuple-element.96.refs_2_), channel_id=1, source_target_pairs={{0,7},{1,0},{2,1},{3,2},{4,3},{5,4},{6,5},{7,6},{8,15},{9,8},{10,9... | collective-permute-start | bytes 786440 | tf_op jit(solution)/shard_map/ppermute | solution.py:460

commit v5 on v4

--- a/solution.py
+++ b/solution.py
@@ -518,7 +518,7 @@
     maps, product = group_maps(transfer)
     inflow, maps, product = lax.optimization_barrier((inflow, maps, product))
     inflow = shared_sum(inflow, GROUP)
-    masked, received, inflow = lax.optimization_barrier((masked, received, inflow))
+    masked, inflow = lax.optimization_barrier((masked, inflow))
 
     inflow = lax.all_to_all(inflow, "sub", 0, 0, axis_index_groups=inside)
     others = exchange(product, "sub", GROUP)

time: 112 us -> 110 us (0.982)
  starting transfers between devices: 48.8 us -> 45.1 us
  waiting for transfers between devices: 23.4 us -> 25 us
    ppermute x8, starting transfers between devices: 15.9 us -> 10.9 us  [exchange(): lax.ppermute(value, axis, [(i, i ^ bit) for i in range(lax.axis_size(axis...]
    ppermute x8, waiting for transfers between devices: 1.37 us -> 2.55 us  [exchange(): lax.ppermute(value, axis, [(i, i ^ bit) for i in range(lax.axis_size(axis...]
    all_to_all x1, starting transfers between devices: 3.66 us -> 4.79 us  [per_device(): lax.all_to_all(heat.reshape(members, share, channels), 'coarse', 0, 0)]
  transfers between devices with their start and end apart: 22 -> 22, of which waited for: 7 -> 7; matrix products, arithmetic and copies ran while one was open for 2% -> 2% of each run, Pallas kernels for 27% -> 28%
where the time goes in v5:
time: 110 us; the launch traced here: 109 us
  starting transfers between devices  45.1 us (41%)
  Pallas kernels  36 us (33%)
  waiting for transfers between devices  25 us (23%)
  other arithmetic  2.16 us (2%)
    ppermute x11, starting transfers between devices, shifted(): lax.ppermute(value, axis, [(i, (i + step) % count) for i in range(count)])  22.4 us
    ppermute x11, waiting for transfers between devices, shifted(): lax.ppermute(value, axis, [(i, (i + step) % count) for i in range(count)])  12.2 us
    pallas_call x2, Pallas kernels, dual(): pl.pallas_call(functools.partial(dual_kernel, first), out_shape=pltpu.HBM...  11.3 us
    ppermute x8, starting transfers between devices, exchange(): lax.ppermute(value, axis, [(i, i ^ bit) for i in range(lax.axis_size(axis...  10.9 us
    pallas_call x1, Pallas kernels, tables(): pl.pallas_call(tables_kernel, out_shape=[pltpu.HBM((faces, size, size), B...  5.26 us
    all_to_all x1, starting transfers between devices, per_device(): lax.all_to_all(heat.reshape(members, share, channels), 'coarse', 0, 0)  4.79 us
    all_to_all x1, waiting for transfers between devices, per_device(): carried = lax.all_to_all(carried, 'coarse', 0, 0).reshape(samples, channels)  4.72 us
    all_to_all x1, starting transfers between devices, per_device(): inflow = lax.all_to_all(inflow, 'sub', 0, 0, axis_index_groups=inside)  3.66 us
  transfers between devices with their start and end apart: 22, of which 7 were waited for; matrix products, arithmetic and copies ran while one was open for 2% of the time, Pallas kernels for 28%

profile of v5, /device:TPU:2, one launch (start us, length us, event | category | flops | bytes accessed | tf_op | source)
XLA Modules:
  0.0 109.2 jit_solution(18173171005454715775)
XLA Ops:
  0.0 7.2 %collective-permute-start = (f32[1,128,128]{2,1,0:T(8,128)}, f32[1,128,128]{2,1,0:T(8,128)S(1)}, u32[]{:S(2)}, u32[]{:S(2)}) collective-permute-start(f32[1,128,128]{2,1,0:T(8,128)} %param.20), channel_id=1, source_target_pairs={{0,32},{8,40},{16,48},{24,56},{32,0},{40,8},{48,16},{56,24},{64,96... | collective-permute-start | bytes 196616 | tf_op jit(solution)/shard_map/ppermute | solution.py:451
  7.8 2.5 %canon.1 = (bf16[256,512]{1,0:T(8,128)(2,1)S(1)}, bf16[256,512]{1,0:T(8,128)(2,1)S(1)}, bf16[256,512]{1,0:T(8,128)(2,1)S(1)}, bf16[256,512]{1,0:T(8,128)(2,1)S(1)}) custom-call(s32[4]{0:T(128)S(1)} %bitcast.27, bf16[4,256,512]{2,1,0:T(8,128)(2,1)} %bitcast.38, s32[4,512]{1,0:T(4,128)} %bitcast.40), custom_call_target="tpu_custom_call" | custom-call | flops 536870912 | bytes 2097152 | tf_op jit(solution)/shard_map/canon/pallas_call | solution.py:60
  10.4 4.7 %collective-permute-start.2 = (bf16[256,512]{1,0:T(8,128)(2,1)S(1)}, bf16[256,512]{1,0:T(8,128)(2,1)S(1)}, u32[]{:S(2)}, u32[]{:S(2)}) collective-permute-start(bf16[256,512]{1,0:T(8,128)(2,1)S(1)} %get-tuple-element.55.refs_0_), channel_id=1, source_target_pairs={{0,248},{8,0},{16,8},{24,16},{32,24},{40,32},{48,40},{56,48},{64,5... | collective-permute-start | bytes 786440 | tf_op jit(solution)/shard_map/ppermute | solution.py:460
  15.2 1.6 %collective-permute-start.3 = (bf16[256,512]{1,0:T(8,128)(2,1)S(1)}, bf16[256,512]{1,0:T(8,128)(2,1)S(1)}, u32[]{:S(2)}, u32[]{:S(2)}) collective-permute-start(bf16[256,512]{1,0:T(8,128)(2,1)S(1)} %get-tuple-element.58.refs_3_), channel_id=1, source_target_pairs={{0,1},{1,2},{2,3},{3,4},{4,5},{5,6},{6,7},{7,0},{8,9},{9,10},{10,1... | collective-permute-start | bytes 786440 | tf_op jit(solution)/shard_map/ppermute | solution.py:460
  16.8 2.6 %collective-permute-start.4 = (bf16[256,512]{1,0:T(8,128)(2,1)S(1)}, bf16[256,512]{1,0:T(8,128)(2,1)S(1)}, u32[]{:S(2)}, u32[]{:S(2)}) collective-permute-start(bf16[256,512]{1,0:T(8,128)(2,1)S(1)} %get-tuple-element.57.refs_2_), channel_id=1, source_target_pairs={{0,7},{1,0},{2,1},{3,2},{4,3},{5,4},{6,5},{7,6},{8,15},{9,8},{10,9... | collective-permute-start | bytes 786440 | tf_op jit(solution)/shard_map/ppermute | solution.py:460
  19.3 1.0 convert_reduce_fusion
  21.4 5.3 %tables.1 = (bf16[4,512,512]{2,1,0:T(8,128)(2,1)}, bf16[4,512,512]{2,1,0:T(8,128)(2,1)}, bf16[4,512,512]{2,1,0:T(8,128)(2,1)S(1)}, bf16[4,512,256]{2,1,0:T(8,128)(2,1)S(1)}, bf16[4,256,512]{2,1,0:T(8,128)(2,1)}) custom-call(s32[4]{0:T(128)S(1)} %bitcast.28, s32[4,512]{1,0:T(4,128)} %bitcast.41, bf16[4,512,256]{2,1,0:T(8,128)(2,1)} %bitcast.39), custom_call_target="tpu_custom_call" | custom-call | flops 1073741824 | bytes 7340032 | tf_op jit(solution)/shard_map/tables/pallas_call | solution.py:91
  26.6 4.1 %collective-permute-done.3.refs_6_ = bf16[256,512]{1,0:T(8,128)(2,1)S(1)} collective-permute-done((bf16[256,512]{1,0:T(8,128)(2,1)S(1)}, bf16[256,512]{1,0:T(8,128)(2,1)S(1)}, u32[]{:S(2)}, u32[]{:S(2)}) %collective-permute-start.3) | collective-permute-done | bytes 262176 | tf_op jit(solution)/shard_map/ppermute | solution.py:460
  30.8 3.2 %residuals.1 = (bf16[4,256,512]{2,1,0:T(8,128)(2,1)}, bf16[256,256]{1,0:T(8,128)(2,1)S(1)}, f32[256,128]{1,0:T(8,128)}) custom-call(s32[4]{0:T(128)S(1)} %bitcast.29, f32[4]{0:T(128)S(1)} %bitcast.23, bf16[256,512]{1,0:T(8,128)(2,1)S(1)} %get-tuple-element.55.refs_0_, bf16[256,512]{1,0:T(8,128)(2,1)S(1)} %get-tuple-element.56.refs_1_, ...), custom_call_target="tpu_custom_call" | custom-call | flops 805306368 | bytes 6291456 | tf_op jit(solution)/shard_map/residuals/pallas_call | solution.py:156
  34.2 4.8 %all-to-all-start = ((f32[8,32,128]{2,1,0:T(8,128)}), f32[8,32,128]{2,1,0:T(8,128)S(1)}, u32[]{:S(2)}, u32[]{:S(2)}) async-start(f32[8,32,128]{2,1,0:T(8,128)} %bitcast.8), calls=%async_computation | async-start | bytes 262144 | tf_op jit(solution)/shard_map/all_to_all | solution.py:517
  39.0 2.5 %collective-permute-done.8 = bf16[1,256,256]{2,1,0:T(8,128)(2,1)S(1)} collective-permute-done((bf16[1,256,256]{2,1,0:T(8,128)(2,1)S(1)}, bf16[1,256,256]{2,1,0:T(8,128)(2,1)S(1)}, u32[]{:S(2)}, u32[]{:S(2)}) %collective-permute-start.8) | collective-permute-done | bytes 131104 | tf_op jit(solution)/shard_map/ppermute | solution.py:451
  41.7 1.6 %group_maps.1 = (bf16[16,128,128]{2,1,0:T(8,128)(2,1)}, f32[1,136,128]{2,1,0:T(8,128)S(1)}) custom-call(f32[8,128,128]{2,1,0:T(8,128)S(1)} %pad_maximum_fusion.1.transfer), custom_call_target="tpu_custom_call" | custom-call | flops 100663296 | bytes 1048576 | tf_op jit(solution)/shard_map/group_maps/pallas_call | solution.py:264
  43.4 2.2 %all-to-all-done.inflow = f32[8,32,128]{2,1,0:T(8,128)S(1)} async-done(((f32[8,32,128]{2,1,0:T(8,128)}), f32[8,32,128]{2,1,0:T(8,128)S(1)}, u32[]{:S(2)}, u32[]{:S(2)}) %all-to-all-start) | async-done | bytes 131104 | tf_op jit(solution)/shard_map/all_to_all | solution.py:517
  46.3 3.7 %all-to-all-start.1 = ((f32[8,32,128]{2,1,0:T(8,128)}), f32[8,32,128]{2,1,0:T(8,128)S(1)}, u32[]{:S(2)}, u32[]{:S(2)}) async-start(f32[8,32,128]{2,1,0:T(8,128)} %shared_sum.1), calls=%async_computation.1 | async-start | bytes 262144 | tf_op jit(solution)/shard_map/all_to_all | solution.py:523
  50.4 5.7 %dual0.1 = f32[2,256,512]{2,1,0:T(8,128)} custom-call(s32[4]{0:T(128)S(1)} %bitcast.30, f32[4]{0:T(128)S(1)} %bitcast.24, bf16[4,256,512]{2,1,0:T(8,128)(2,1)} %get-tuple-element.84.masked, bf16[4,512,512]{2,1,0:T(8,128)(2,1)} %get-tuple-element.74.sort, f32[4,1,512]{2,1,0:T(1,128)S(1)} %bitcast.21, bf16[2048,2048]{1,0:T(8,128)(2,1)} %bitcast.33), custom_call_target="tpu_custom_call" | custom-call | flops 1610612736 | bytes 8388608 | tf_op jit(solution)/shard_map/dual0/pallas_call | solution.py:209
  56.2 3.3 %all-to-all-done.1.inflow = f32[8,32,128]{2,1,0:T(8,128)S(1)} async-done(((f32[8,32,128]{2,1,0:T(8,128)}), f32[8,32,128]{2,1,0:T(8,128)S(1)}, u32[]{:S(2)}, u32[]{:S(2)}) %all-to-all-start.1) | async-done | bytes 131104 | tf_op jit(solution)/shard_map/all_to_all | solution.py:523
  59.5 2.1 %group_outflow.1 = f32[32,128]{1,0:T(8,128)S(1)} custom-call(f32[8,32,128]{2,1,0:T(8,128)S(1)} %all-to-all-done.1.inflow, bf16[16,128,128]{2,1,0:T(8,128)(2,1)} %get-tuple-element.78.maps), custom_call_target="tpu_custom_call" | custom-call | flops 25165824 | bytes 655360 | tf_op jit(solution)/shard_map/group_outflow/pallas_call | solution.py:299
  61.6 1.0 collective-permute-start.10
  63.2 2.4 %collective-permute-start.12 = (f32[32,128]{1,0:T(8,128)S(1)}, f32[32,128]{1,0:T(8,128)S(1)}, u32[]{:S(2)}, u32[]{:S(2)}) collective-permute-start(f32[32,128]{1,0:T(8,128)S(1)} %group_outflow.1), channel_id=1, source_target_pairs={{0,128},{8,136},{16,144},{24,152},{32,160},{40,168},{48,176},{56,1... | collective-permute-start | bytes 49160 | tf_op jit(solution)/shard_map/ppermute | solution.py:460
  65.6 1.6 %collective-permute-start.13 = (f32[32,128]{1,0:T(8,128)S(1)}, f32[32,128]{1,0:T(8,128)S(1)}, u32[]{:S(2)}, u32[]{:S(2)}) collective-permute-start(f32[32,128]{1,0:T(8,128)S(1)} %group_outflow.1), channel_id=1, source_target_pairs={{0,64},{8,72},{16,80},{24,88},{32,96},{40,104},{48,112},{56,120},{... | collective-permute-start | bytes 49160 | tf_op jit(solution)/shard_map/ppermute | solution.py:460
  67.2 1.7 %collective-permute-start.14 = (f32[2,136,128]{2,1,0:T(8,128)S(1)}, f32[2,136,128]{2,1,0:T(8,128)S(1)}, u32[]{:S(2)}, u32[]{:S(2)}) collective-permute-start(f32[2,136,128]{2,1,0:T(8,128)S(1)} %pad_maximum_fusion.6), channel_id=1, source_target_pairs={{0,128},{8,136},{16,144},{24,152},{32,160},{40,168},{48,176},{56,1... | collective-permute-start | bytes 417800 | tf_op jit(solution)/shard_map/ppermute | solution.py:451
  69.0 5.6 %dual2.1.dual1 = f32[2,256,512]{2,1,0:T(8,128)} custom-call(s32[4]{0:T(128)S(1)} %bitcast.31, f32[4]{0:T(128)S(1)} %bitcast.25, bf16[4,256,512]{2,1,0:T(8,128)(2,1)} %get-tuple-element.84.masked, bf16[4,512,512]{2,1,0:T(8,128)(2,1)} %get-tuple-element.74.sort, f32[4,1,512]{2,1,0:T(1,128)S(1)} %bitcast.22, bf16[2048,2048]{1,0:T(8,128)(2,1)} %bitcast.34), custom_call_target="tpu_custom_call" | custom-call | flops 1610612736 | bytes 8388608 | tf_op jit(solution)/shard_map/dual2/pallas_call | solution.py:209
  74.6 2.2 %carried_states.1 = f32[8,32,128]{2,1,0:T(8,128)} custom-call(f32[4,136,128]{2,1,0:T(8,128)S(1)} %pad_maximum_fusion.3.products, f32[8,32,128]{2,1,0:T(8,128)S(1)} %all-to-all-done.1.inflow, bf16[16,128,128]{2,1,0:T(8,128)(2,1)} %get-tuple-element.78.maps, f32[32,128]{1,0:T(8,128)S(1)} %collective-permute-done.11.refs_0_, ...), custom_call_target="tpu_custom_call" | custom-call | flops 25165824 | bytes 1310720 | tf_op jit(solution)/shard_map/carried_states/pallas_call | solution.py:331
  76.7 3.4 %all-to-all-start.2 = ((f32[8,32,128]{2,1,0:T(8,128)}), f32[8,32,128]{2,1,0:T(8,128)S(1)}, u32[]{:S(2)}, u32[]{:S(2)}) async-start(f32[8,32,128]{2,1,0:T(8,128)} %carried_states.1), calls=%async_computation.2 | async-start | bytes 262144 | tf_op jit(solution)/shard_map/all_to_all | solution.py:544
  80.2 1.7 %line_base.1.base = f32[256,256]{1,0:T(8,128)S(1)} custom-call(bf16[8,256,256]{2,1,0:T(8,128)(2,1)S(1)} %pad_maximum_fusion.gathered, bf16[2048,256]{1,0:T(8,128)(2,1)} %bitcast.35), custom_call_target="tpu_custom_call" | custom-call | flops 268435456 | bytes 2097152 | tf_op jit(solution)/shard_map/line_base/pallas_call | solution.py:363
  81.9 4.7 %all-to-all-done.2 = f32[8,32,128]{2,1,0:T(8,128)S(1)} async-done(((f32[8,32,128]{2,1,0:T(8,128)}), f32[8,32,128]{2,1,0:T(8,128)S(1)}, u32[]{:S(2)}, u32[]{:S(2)}) %all-to-all-start.2) | async-done | bytes 131104 | tf_op jit(solution)/shard_map/all_to_all | solution.py:544
  86.6 2.6 %extend.1 = (bf16[256,512]{1,0:T(8,128)(2,1)S(1)}, bf16[256,512]{1,0:T(8,128)(2,1)S(1)}, bf16[256,512]{1,0:T(8,128)(2,1)S(1)}, bf16[256,512]{1,0:T(8,128)(2,1)S(1)}) custom-call(f32[4]{0:T(128)S(1)} %bitcast.26, f32[256,256]{1,0:T(8,128)S(1)} %line_base.1.base, f32[256,128]{1,0:T(8,128)S(1)} %bitcast.19, bf16[128,256]{1,0:T(8,128)(2,1)} %bitcast.36, ...), custom_call_target="tpu_custom_call" | custom-call | flops 268435456 | bytes 4194304 | tf_op jit(solution)/shard_map/extend/pallas_call | solution.py:391
  89.3 4.7 %collective-permute-start.16 = (bf16[256,512]{1,0:T(8,128)(2,1)S(1)}, bf16[256,512]{1,0:T(8,128)(2,1)S(1)}, u32[]{:S(2)}, u32[]{:S(2)}) collective-permute-start(bf16[256,512]{1,0:T(8,128)(2,1)S(1)} %get-tuple-element.92.refs_0_), channel_id=1, source_target_pairs={{0,248},{8,0},{16,8},{24,16},{32,24},{40,32},{48,40},{56,48},{64,5... | collective-permute-start | bytes 786440 | tf_op jit(solution)/shard_map/ppermute | solution.py:460
  94.6 3.6 %collective-permute-start.18 = (bf16[256,512]{1,0:T(8,128)(2,1)S(1)}, bf16[256,512]{1,0:T(8,128)(2,1)S(1)}, u32[]{:S(2)}, u32[]{:S(2)}) collective-permute-start(bf16[256,512]{1,0:T(8,128)(2,1)S(1)} %get-tuple-element.94.refs_2_), channel_id=1, source_target_pairs={{0,7},{1,0},{2,1},{3,2},{4,3},{5,4},{6,5},{7,6},{8,15},{9,8},{10,9... | collective-permute-start | bytes 786440 | tf_op jit(solution)/shard_map/ppermute | solution.py:460
  98.2 1.9 %collective-permute-done.15.refs_4_ = bf16[256,512]{1,0:T(8,128)(2,1)S(1)} collective-permute-done((bf16[256,512]{1,0:T(8,128)(2,1)S(1)}, bf16[256,512]{1,0:T(8,128)(2,1)S(1)}, u32[]{:S(2)}, u32[]{:S(2)}) %collective-permute-start.15) | collective-permute-done | bytes 262176 | tf_op jit(solution)/shard_map/ppermute | solution.py:460
  100.1 6.2 %collective-permute-done.17.refs_6_ = bf16[256,512]{1,0:T(8,128)(2,1)S(1)} collective-permute-done((bf16[256,512]{1,0:T(8,128)(2,1)S(1)}, bf16[256,512]{1,0:T(8,128)(2,1)S(1)}, u32[]{:S(2)}, u32[]{:S(2)}) %collective-permute-start.17) | collective-permute-done | bytes 262176 | tf_op jit(solution)/shard_map/ppermute | solution.py:460
  106.2 3.0 %finish.1 = bf16[4,256,512]{2,1,0:T(8,128)(2,1)} custom-call(s32[4]{0:T(128)S(1)} %bitcast.32, bf16[256,512]{1,0:T(8,128)(2,1)S(1)} %get-tuple-element.92.refs_0_, bf16[256,512]{1,0:T(8,128)(2,1)S(1)} %get-tuple-element.93.refs_1_, bf16[256,512]{1,0:T(8,128)(2,1)S(1)} %get-tuple-element.94.refs_2_, bf16[256,512]{1,0:T(8,128)(2,1)S(1)} %get-tuple-element.95.refs_3_, ...), custom_call_target="tpu_custom_call" | custom-call | flops 536870912 | bytes 5242880 | tf_op jit(solution)/shard_map/finish/pallas_call | solution.py:428
  (46 shorter events, 4.7 us)
Async XLA Ops:
  0.0 21.4 %copy-start.4 = (s32[1,1,4]{2,1,0:T(1,128)S(1)}, s32[1,1,4]{2,1,0:T(1,128)}, u32[]{:S(2)}) copy-start(s32[1,1,4]{2,1,0:T(1,128)} %param.12) | copy-start | bytes 52
  0.0 20.3 %collective-permute-start = (f32[1,128,128]{2,1,0:T(8,128)}, f32[1,128,128]{2,1,0:T(8,128)S(1)}, u32[]{:S(2)}, u32[]{:S(2)}) collective-permute-start(f32[1,128,128]{2,1,0:T(8,128)} %param.20), channel_id=1, source_target_pairs={{0,32},{8,40},{16,48},{24,56},{32,0},{40,8},{48,16},{56,24},{64,96... | collective-permute-start | bytes 196616 | tf_op jit(solution)/shard_map/ppermute | solution.py:451
  7.2 0.7 copy-start.3
  10.3 16.3 %collective-permute-start.1 = (bf16[256,512]{1,0:T(8,128)(2,1)S(1)}, bf16[256,512]{1,0:T(8,128)(2,1)S(1)}, u32[]{:S(2)}, u32[]{:S(2)}) collective-permute-start(bf16[256,512]{1,0:T(8,128)(2,1)S(1)} %get-tuple-element.56.refs_1_), channel_id=1, source_target_pairs={{0,8},{8,16},{16,24},{24,32},{32,40},{40,48},{48,56},{56,64},{64,7... | collective-permute-start | bytes 786440 | tf_op jit(solution)/shard_map/ppermute | solution.py:460
  10.4 16.2 %collective-permute-start.2 = (bf16[256,512]{1,0:T(8,128)(2,1)S(1)}, bf16[256,512]{1,0:T(8,128)(2,1)S(1)}, u32[]{:S(2)}, u32[]{:S(2)}) collective-permute-start(bf16[256,512]{1,0:T(8,128)(2,1)S(1)} %get-tuple-element.55.refs_0_), channel_id=1, source_target_pairs={{0,248},{8,0},{16,8},{24,16},{32,24},{40,32},{48,40},{56,48},{64,5... | collective-permute-start | bytes 786440 | tf_op jit(solution)/shard_map/ppermute | solution.py:460
  15.2 15.6 %collective-permute-start.3 = (bf16[256,512]{1,0:T(8,128)(2,1)S(1)}, bf16[256,512]{1,0:T(8,128)(2,1)S(1)}, u32[]{:S(2)}, u32[]{:S(2)}) collective-permute-start(bf16[256,512]{1,0:T(8,128)(2,1)S(1)} %get-tuple-element.58.refs_3_), channel_id=1, source_target_pairs={{0,1},{1,2},{2,3},{3,4},{4,5},{5,6},{6,7},{7,0},{8,9},{9,10},{10,1... | collective-permute-start | bytes 786440 | tf_op jit(solution)/shard_map/ppermute | solution.py:460
  16.8 14.0 %collective-permute-start.4 = (bf16[256,512]{1,0:T(8,128)(2,1)S(1)}, bf16[256,512]{1,0:T(8,128)(2,1)S(1)}, u32[]{:S(2)}, u32[]{:S(2)}) collective-permute-start(bf16[256,512]{1,0:T(8,128)(2,1)S(1)} %get-tuple-element.57.refs_2_), channel_id=1, source_target_pairs={{0,7},{1,0},{2,1},{3,2},{4,3},{5,4},{6,5},{7,6},{8,15},{9,8},{10,9... | collective-permute-start | bytes 786440 | tf_op jit(solution)/shard_map/ppermute | solution.py:460
  20.3 10.4 %copy-start.1 = (bf16[1,2048,128]{2,1,0:T(8,128)(2,1)S(1)}, bf16[1,2048,128]{2,1,0:T(8,128)(2,1)}, u32[]{:S(2)}) copy-start(bf16[1,2048,128]{2,1,0:T(8,128)(2,1)} %param.19) | copy-start | bytes 1572868
  20.3 10.4 %copy-start.2 = (f32[1,1,4]{2,1,0:T(1,128)S(1)}, f32[1,1,4]{2,1,0:T(1,128)}, u32[]{:S(2)}) copy-start(f32[1,1,4]{2,1,0:T(1,128)} %param.14) | copy-start | bytes 52
  21.2 12.7 %collective-permute-start.5 = (f32[2,128,128]{2,1,0:T(8,128)S(1)}, f32[2,128,128]{2,1,0:T(8,128)S(1)}, u32[]{:S(2)}, u32[]{:S(2)}) collective-permute-start(f32[2,128,128]{2,1,0:T(8,128)S(1)} %pad_maximum_fusion.7), channel_id=1, source_target_pairs={{0,16},{8,24},{16,0},{24,8},{32,48},{40,56},{48,32},{56,40},{64,80... | collective-permute-start | bytes 393224 | tf_op jit(solution)/shard_map/ppermute | solution.py:451
  30.8 3.2 %copy-start.5 = (f32[1,128,128]{2,1,0:T(8,128)S(1)}, f32[1,128,128]{2,1,0:T(8,128)}, u32[]{:S(2)}) copy-start(f32[1,128,128]{2,1,0:T(8,128)} %param.20) | copy-start | bytes 196612
  34.0 7.7 %collective-permute-start.6 = (f32[4,128,128]{2,1,0:T(8,128)S(1)}, f32[4,128,128]{2,1,0:T(8,128)S(1)}, u32[]{:S(2)}, u32[]{:S(2)}) collective-permute-start(f32[4,128,128]{2,1,0:T(8,128)S(1)} %pad_maximum_fusion.4), channel_id=1, source_target_pairs={{0,8},{8,0},{16,24},{24,16},{32,40},{40,32},{48,56},{56,48},{64,72... | collective-permute-start | bytes 786440 | tf_op jit(solution)/shard_map/ppermute | solution.py:451
  34.1 7.4 %collective-permute-start.8 = (bf16[1,256,256]{2,1,0:T(8,128)(2,1)S(1)}, bf16[1,256,256]{2,1,0:T(8,128)(2,1)S(1)}, u32[]{:S(2)}, u32[]{:S(2)}) collective-permute-start(bf16[1,256,256]{2,1,0:T(8,128)(2,1)S(1)} %bitcast.16), channel_id=1, source_target_pairs={{0,2},{1,3},{2,0},{3,1},{4,6},{5,7},{6,4},{7,5},{8,10},{9,11},{10,... | collective-permute-start | bytes 393224 | tf_op jit(solution)/shard_map/ppermute | solution.py:451
  34.2 11.4 %all-to-all-start = ((f32[8,32,128]{2,1,0:T(8,128)}), f32[8,32,128]{2,1,0:T(8,128)S(1)}, u32[]{:S(2)}, u32[]{:S(2)}) async-start(f32[8,32,128]{2,1,0:T(8,128)} %bitcast.8), calls=%async_computation | async-start | bytes 262144 | tf_op jit(solution)/shard_map/all_to_all | solution.py:517
  41.6 20.0 %collective-permute-start.9 = (bf16[2,256,256]{2,1,0:T(8,128)(2,1)S(1)}, bf16[2,256,256]{2,1,0:T(8,128)(2,1)S(1)}, u32[]{:S(2)}, u32[]{:S(2)}) collective-permute-start(bf16[2,256,256]{2,1,0:T(8,128)(2,1)S(1)} %pad_maximum_fusion.5), channel_id=1, source_target_pairs={{0,1},{1,0},{2,3},{3,2},{4,5},{5,4},{6,7},{7,6},{8,9},{9,8},{10,11... | collective-permute-start | bytes 786440 | tf_op jit(solution)/shard_map/ppermute | solution.py:451
  46.3 13.2 %all-to-all-start.1 = ((f32[8,32,128]{2,1,0:T(8,128)}), f32[8,32,128]{2,1,0:T(8,128)S(1)}, u32[]{:S(2)}, u32[]{:S(2)}) async-start(f32[8,32,128]{2,1,0:T(8,128)} %shared_sum.1), calls=%async_computation.1 | async-start | bytes 262144 | tf_op jit(solution)/shard_map/all_to_all | solution.py:523
  49.9 6.3 %collective-permute-start.7 = (f32[1,136,128]{2,1,0:T(8,128)S(1)}, f32[1,136,128]{2,1,0:T(8,128)S(1)}, u32[]{:S(2)}, u32[]{:S(2)}) collective-permute-start(f32[1,136,128]{2,1,0:T(8,128)S(1)} %get-tuple-element.72), channel_id=1, source_target_pairs={{0,64},{8,72},{16,80},{24,88},{32,96},{40,104},{48,112},{56,120},{... | collective-permute-start | bytes 208904 | tf_op jit(solution)/shard_map/ppermute | solution.py:451
  61.6 18.5 %collective-permute-start.10 = (bf16[4,256,256]{2,1,0:T(8,128)(2,1)S(1)}, bf16[4,256,256]{2,1,0:T(8,128)(2,1)S(1)}, u32[]{:S(2)}, u32[]{:S(2)}) collective-permute-start(bf16[4,256,256]{2,1,0:T(8,128)(2,1)S(1)} %pad_maximum_fusion.2), channel_id=1, source_target_pairs={{0,4},{1,5},{2,6},{3,7},{4,0},{5,1},{6,2},{7,3},{8,12},{9,13},{10,... | collective-permute-start | bytes 1572872 | tf_op jit(solution)/shard_map/ppermute | solution.py:451
  62.7 11.8 %collective-permute-start.11 = (f32[32,128]{1,0:T(8,128)S(1)}, f32[32,128]{1,0:T(8,128)S(1)}, u32[]{:S(2)}, u32[]{:S(2)}) collective-permute-start(f32[32,128]{1,0:T(8,128)S(1)} %group_outflow.1), channel_id=1, source_target_pairs={{0,192},{8,200},{16,208},{24,216},{32,224},{40,232},{48,240},{56,2... | collective-permute-start | bytes 49160 | tf_op jit(solution)/shard_map/ppermute | solution.py:460
  63.2 11.3 %collective-permute-start.12 = (f32[32,128]{1,0:T(8,128)S(1)}, f32[32,128]{1,0:T(8,128)S(1)}, u32[]{:S(2)}, u32[]{:S(2)}) collective-permute-start(f32[32,128]{1,0:T(8,128)S(1)} %group_outflow.1), channel_id=1, source_target_pairs={{0,128},{8,136},{16,144},{24,152},{32,160},{40,168},{48,176},{56,1... | collective-permute-start | bytes 49160 | tf_op jit(solution)/shard_map/ppermute | solution.py:460
  65.6 8.9 %collective-permute-start.13 = (f32[32,128]{1,0:T(8,128)S(1)}, f32[32,128]{1,0:T(8,128)S(1)}, u32[]{:S(2)}, u32[]{:S(2)}) collective-permute-start(f32[32,128]{1,0:T(8,128)S(1)} %group_outflow.1), channel_id=1, source_target_pairs={{0,64},{8,72},{16,80},{24,88},{32,96},{40,104},{48,112},{56,120},{... | collective-permute-start | bytes 49160 | tf_op jit(solution)/shard_map/ppermute | solution.py:460
  67.2 7.3 %collective-permute-start.14 = (f32[2,136,128]{2,1,0:T(8,128)S(1)}, f32[2,136,128]{2,1,0:T(8,128)S(1)}, u32[]{:S(2)}, u32[]{:S(2)}) collective-permute-start(f32[2,136,128]{2,1,0:T(8,128)S(1)} %pad_maximum_fusion.6), channel_id=1, source_target_pairs={{0,128},{8,136},{16,144},{24,152},{32,160},{40,168},{48,176},{56,1... | collective-permute-start | bytes 417800 | tf_op jit(solution)/shard_map/ppermute | solution.py:451
  76.7 9.9 %all-to-all-start.2 = ((f32[8,32,128]{2,1,0:T(8,128)}), f32[8,32,128]{2,1,0:T(8,128)S(1)}, u32[]{:S(2)}, u32[]{:S(2)}) async-start(f32[8,32,128]{2,1,0:T(8,128)} %carried_states.1), calls=%async_computation.2 | async-start | bytes 262144 | tf_op jit(solution)/shard_map/all_to_all | solution.py:544
  81.9 24.3 %copy-start = (bf16[4,512,512]{2,1,0:T(8,128)(2,1)S(1)}, bf16[4,512,512]{2,1,0:T(8,128)(2,1)}, u32[]{:S(2)}) copy-start(bf16[4,512,512]{2,1,0:T(8,128)(2,1)} %get-tuple-element.96.refs_8_) | copy-start | bytes 6291460
  89.2 10.8 %collective-permute-start.15 = (bf16[256,512]{1,0:T(8,128)(2,1)S(1)}, bf16[256,512]{1,0:T(8,128)(2,1)S(1)}, u32[]{:S(2)}, u32[]{:S(2)}) collective-permute-start(bf16[256,512]{1,0:T(8,128)(2,1)S(1)} %get-tuple-element.93.refs_1_), channel_id=1, source_target_pairs={{0,8},{8,16},{16,24},{24,32},{32,40},{40,48},{48,56},{56,64},{64,7... | collective-permute-start | bytes 786440 | tf_op jit(solution)/shard_map/ppermute | solution.py:460
  89.3 10.8 %collective-permute-start.16 = (bf16[256,512]{1,0:T(8,128)(2,1)S(1)}, bf16[256,512]{1,0:T(8,128)(2,1)S(1)}, u32[]{:S(2)}, u32[]{:S(2)}) collective-permute-start(bf16[256,512]{1,0:T(8,128)(2,1)S(1)} %get-tuple-element.92.refs_0_), channel_id=1, source_target_pairs={{0,248},{8,0},{16,8},{24,16},{32,24},{40,32},{48,40},{56,48},{64,5... | collective-permute-start | bytes 786440 | tf_op jit(solution)/shard_map/ppermute | solution.py:460
  94.0 12.2 %collective-permute-start.17 = (bf16[256,512]{1,0:T(8,128)(2,1)S(1)}, bf16[256,512]{1,0:T(8,128)(2,1)S(1)}, u32[]{:S(2)}, u32[]{:S(2)}) collective-permute-start(bf16[256,512]{1,0:T(8,128)(2,1)S(1)} %get-tuple-element.95.refs_3_), channel_id=1, source_target_pairs={{0,1},{1,2},{2,3},{3,4},{4,5},{5,6},{6,7},{7,0},{8,9},{9,10},{10,1... | collective-permute-start | bytes 786440 | tf_op jit(solution)/shard_map/ppermute | solution.py:460
  94.6 11.7 %collective-permute-start.18 = (bf16[256,512]{1,0:T(8,128)(2,1)S(1)}, bf16[256,512]{1,0:T(8,128)(2,1)S(1)}, u32[]{:S(2)}, u32[]{:S(2)}) collective-permute-start(bf16[256,512]{1,0:T(8,128)(2,1)S(1)} %get-tuple-element.94.refs_2_), channel_id=1, source_target_pairs={{0,7},{1,0},{2,1},{3,2},{4,3},{5,4},{6,5},{7,6},{8,15},{9,8},{10,9... | collective-permute-start | bytes 786440 | tf_op jit(solution)/shard_map/ppermute | solution.py:460

commit v6 on v5

--- a/solution.py
+++ b/solution.py
@@ -69,7 +69,7 @@
         compiler_params=params(8),
         cost_estimate=cost(2 * faces * samples * size * size, 4 * faces * samples * size),
         name="canon",
-    )(slot, in_hbm(parts), in_hbm(order))
+    )(in_hbm(slot), in_hbm(parts), in_hbm(order))
 
 
 def tables_kernel(slot, order, basis, sort, restore, restore_near, ordered, ordered_columns):

time: 110 us -> 110 us (level)
  no operation moved by 1% of the time
where the time goes in v6:
time: 110 us; the launch traced here: 109 us
  starting transfers between devices  45.5 us (41%)
  Pallas kernels  36.1 us (33%)
  waiting for transfers between devices  25 us (23%)
  other arithmetic  2.16 us (2%)
    ppermute x11, starting transfers between devices, shifted(): lax.ppermute(value, axis, [(i, (i + step) % count) for i in range(count)])  22.3 us
    ppermute x11, waiting for transfers between devices, shifted(): lax.ppermute(value, axis, [(i, (i + step) % count) for i in range(count)])  12.2 us
    pallas_call x2, Pallas kernels, dual(): pl.pallas_call(functools.partial(dual_kernel, first), out_shape=pltpu.HBM...  11.3 us
    ppermute x8, starting transfers between devices, exchange(): lax.ppermute(value, axis, [(i, i ^ bit) for i in range(lax.axis_size(axis...  11.1 us
    pallas_call x1, Pallas kernels, tables(): pl.pallas_call(tables_kernel, out_shape=[pltpu.HBM((faces, size, size), B...  5.25 us
    all_to_all x1, starting transfers between devices, per_device(): lax.all_to_all(heat.reshape(members, share, channels), 'coarse', 0, 0)  4.79 us
    all_to_all x1, waiting for transfers between devices, per_device(): carried = lax.all_to_all(carried, 'coarse', 0, 0).reshape(samples, channels)  4.72 us
    all_to_all x1, starting transfers between devices, per_device(): inflow = lax.all_to_all(inflow, 'sub', 0, 0, axis_index_groups=inside)  3.97 us
  transfers between devices with their start and end apart: 22, of which 7 were waited for; matrix products, arithmetic and copies ran while one was open for 2% of the time, Pallas kernels for 28%

profile of v6, /device:TPU:2, one launch (start us, length us, event | category | flops | bytes accessed | tf_op | source)
XLA Modules:
  0.0 109.0 jit_solution(11003404455976809087)
XLA Ops:
  0.0 7.2 %collective-permute-start = (f32[1,128,128]{2,1,0:T(8,128)}, f32[1,128,128]{2,1,0:T(8,128)S(1)}, u32[]{:S(2)}, u32[]{:S(2)}) collective-permute-start(f32[1,128,128]{2,1,0:T(8,128)} %param.20), channel_id=1, source_target_pairs={{0,32},{8,40},{16,48},{24,56},{32,0},{40,8},{48,16},{56,24},{64,96... | collective-permute-start | bytes 196616 | tf_op jit(solution)/shard_map/ppermute | solution.py:451
  7.2 2.6 %canon.1 = (bf16[256,512]{1,0:T(8,128)(2,1)S(1)}, bf16[256,512]{1,0:T(8,128)(2,1)S(1)}, bf16[256,512]{1,0:T(8,128)(2,1)S(1)}, bf16[256,512]{1,0:T(8,128)(2,1)S(1)}) custom-call(s32[4]{0:T(128)} %bitcast.27, bf16[4,256,512]{2,1,0:T(8,128)(2,1)} %bitcast.38, s32[4,512]{1,0:T(4,128)} %bitcast.40), custom_call_target="tpu_custom_call" | custom-call | flops 536870912 | bytes 2097152 | tf_op jit(solution)/shard_map/canon/pallas_call | solution.py:60
  9.9 4.7 %collective-permute-start.2 = (bf16[256,512]{1,0:T(8,128)(2,1)S(1)}, bf16[256,512]{1,0:T(8,128)(2,1)S(1)}, u32[]{:S(2)}, u32[]{:S(2)}) collective-permute-start(bf16[256,512]{1,0:T(8,128)(2,1)S(1)} %get-tuple-element.55.refs_0_), channel_id=1, source_target_pairs={{0,248},{8,0},{16,8},{24,16},{32,24},{40,32},{48,40},{56,48},{64,5... | collective-permute-start | bytes 786440 | tf_op jit(solution)/shard_map/ppermute | solution.py:460
  14.6 1.6 %collective-permute-start.3 = (bf16[256,512]{1,0:T(8,128)(2,1)S(1)}, bf16[256,512]{1,0:T(8,128)(2,1)S(1)}, u32[]{:S(2)}, u32[]{:S(2)}) collective-permute-start(bf16[256,512]{1,0:T(8,128)(2,1)S(1)} %get-tuple-element.58.refs_3_), channel_id=1, source_target_pairs={{0,1},{1,2},{2,3},{3,4},{4,5},{5,6},{6,7},{7,0},{8,9},{9,10},{10,1... | collective-permute-start | bytes 786440 | tf_op jit(solution)/shard_map/ppermute | solution.py:460
  16.2 2.6 %collective-permute-start.4 = (bf16[256,512]{1,0:T(8,128)(2,1)S(1)}, bf16[256,512]{1,0:T(8,128)(2,1)S(1)}, u32[]{:S(2)}, u32[]{:S(2)}) collective-permute-start(bf16[256,512]{1,0:T(8,128)(2,1)S(1)} %get-tuple-element.57.refs_2_), channel_id=1, source_target_pairs={{0,7},{1,0},{2,1},{3,2},{4,3},{5,4},{6,5},{7,6},{8,15},{9,8},{10,9... | collective-permute-start | bytes 786440 | tf_op jit(solution)/shard_map/ppermute | solution.py:460
  18.8 1.0 convert_reduce_fusion
  20.8 5.3 %tables.1 = (bf16[4,512,512]{2,1,0:T(8,128)(2,1)}, bf16[4,512,512]{2,1,0:T(8,128)(2,1)}, bf16[4,512,512]{2,1,0:T(8,128)(2,1)S(1)}, bf16[4,512,256]{2,1,0:T(8,128)(2,1)S(1)}, bf16[4,256,512]{2,1,0:T(8,128)(2,1)}) custom-call(s32[4]{0:T(128)S(1)} %bitcast.28, s32[4,512]{1,0:T(4,128)} %bitcast.41, bf16[4,512,256]{2,1,0:T(8,128)(2,1)} %bitcast.39), custom_call_target="tpu_custom_call" | custom-call | flops 1073741824 | bytes 7340032 | tf_op jit(solution)/shard_map/tables/pallas_call | solution.py:91
  26.1 4.1 %collective-permute-done.3.refs_6_ = bf16[256,512]{1,0:T(8,128)(2,1)S(1)} collective-permute-done((bf16[256,512]{1,0:T(8,128)(2,1)S(1)}, bf16[256,512]{1,0:T(8,128)(2,1)S(1)}, u32[]{:S(2)}, u32[]{:S(2)}) %collective-permute-start.3) | collective-permute-done | bytes 262176 | tf_op jit(solution)/shard_map/ppermute | solution.py:460
  30.2 3.2 %residuals.1 = (bf16[4,256,512]{2,1,0:T(8,128)(2,1)}, bf16[256,256]{1,0:T(8,128)(2,1)S(1)}, f32[256,128]{1,0:T(8,128)}) custom-call(s32[4]{0:T(128)S(1)} %bitcast.29, f32[4]{0:T(128)S(1)} %bitcast.23, bf16[256,512]{1,0:T(8,128)(2,1)S(1)} %get-tuple-element.55.refs_0_, bf16[256,512]{1,0:T(8,128)(2,1)S(1)} %get-tuple-element.56.refs_1_, ...), custom_call_target="tpu_custom_call" | custom-call | flops 805306368 | bytes 6291456 | tf_op jit(solution)/shard_map/residuals/pallas_call | solution.py:156
  33.7 4.8 %all-to-all-start = ((f32[8,32,128]{2,1,0:T(8,128)}), f32[8,32,128]{2,1,0:T(8,128)S(1)}, u32[]{:S(2)}, u32[]{:S(2)}) async-start(f32[8,32,128]{2,1,0:T(8,128)} %bitcast.8), calls=%async_computation | async-start | bytes 262144 | tf_op jit(solution)/shard_map/all_to_all | solution.py:517
  38.5 2.5 %collective-permute-done.8 = bf16[1,256,256]{2,1,0:T(8,128)(2,1)S(1)} collective-permute-done((bf16[1,256,256]{2,1,0:T(8,128)(2,1)S(1)}, bf16[1,256,256]{2,1,0:T(8,128)(2,1)S(1)}, u32[]{:S(2)}, u32[]{:S(2)}) %collective-permute-start.8) | collective-permute-done | bytes 131104 | tf_op jit(solution)/shard_map/ppermute | solution.py:451
  41.2 1.6 %group_maps.1 = (bf16[16,128,128]{2,1,0:T(8,128)(2,1)}, f32[1,136,128]{2,1,0:T(8,128)S(1)}) custom-call(f32[8,128,128]{2,1,0:T(8,128)S(1)} %pad_maximum_fusion.1.transfer), custom_call_target="tpu_custom_call" | custom-call | flops 100663296 | bytes 1048576 | tf_op jit(solution)/shard_map/group_maps/pallas_call | solution.py:264
  42.8 2.2 %all-to-all-done.inflow = f32[8,32,128]{2,1,0:T(8,128)S(1)} async-done(((f32[8,32,128]{2,1,0:T(8,128)}), f32[8,32,128]{2,1,0:T(8,128)S(1)}, u32[]{:S(2)}, u32[]{:S(2)}) %all-to-all-start) | async-done | bytes 131104 | tf_op jit(solution)/shard_map/all_to_all | solution.py:517
  45.7 4.0 %all-to-all-start.1 = ((f32[8,32,128]{2,1,0:T(8,128)}), f32[8,32,128]{2,1,0:T(8,128)S(1)}, u32[]{:S(2)}, u32[]{:S(2)}) async-start(f32[8,32,128]{2,1,0:T(8,128)} %shared_sum.1), calls=%async_computation.1 | async-start | bytes 262144 | tf_op jit(solution)/shard_map/all_to_all | solution.py:523
  50.2 5.7 %dual0.1 = f32[2,256,512]{2,1,0:T(8,128)} custom-call(s32[4]{0:T(128)S(1)} %bitcast.30, f32[4]{0:T(128)S(1)} %bitcast.24, bf16[4,256,512]{2,1,0:T(8,128)(2,1)} %get-tuple-element.84.masked, bf16[4,512,512]{2,1,0:T(8,128)(2,1)} %get-tuple-element.74.sort, f32[4,1,512]{2,1,0:T(1,128)S(1)} %bitcast.21, bf16[2048,2048]{1,0:T(8,128)(2,1)} %bitcast.33), custom_call_target="tpu_custom_call" | custom-call | flops 1610612736 | bytes 8388608 | tf_op jit(solution)/shard_map/dual0/pallas_call | solution.py:209
  56.0 3.3 %all-to-all-done.1.inflow = f32[8,32,128]{2,1,0:T(8,128)S(1)} async-done(((f32[8,32,128]{2,1,0:T(8,128)}), f32[8,32,128]{2,1,0:T(8,128)S(1)}, u32[]{:S(2)}, u32[]{:S(2)}) %all-to-all-start.1) | async-done | bytes 131104 | tf_op jit(solution)/shard_map/all_to_all | solution.py:523
  59.3 2.1 %group_outflow.1 = f32[32,128]{1,0:T(8,128)S(1)} custom-call(f32[8,32,128]{2,1,0:T(8,128)S(1)} %all-to-all-done.1.inflow, bf16[16,128,128]{2,1,0:T(8,128)(2,1)} %get-tuple-element.78.maps), custom_call_target="tpu_custom_call" | custom-call | flops 25165824 | bytes 655360 | tf_op jit(solution)/shard_map/group_outflow/pallas_call | solution.py:299
  61.4 1.0 collective-permute-start.10
  63.0 2.4 %collective-permute-start.12 = (f32[32,128]{1,0:T(8,128)S(1)}, f32[32,128]{1,0:T(8,128)S(1)}, u32[]{:S(2)}, u32[]{:S(2)}) collective-permute-start(f32[32,128]{1,0:T(8,128)S(1)} %group_outflow.1), channel_id=1, source_target_pairs={{0,128},{8,136},{16,144},{24,152},{32,160},{40,168},{48,176},{56,1... | collective-permute-start | bytes 49160 | tf_op jit(solution)/shard_map/ppermute | solution.py:460
  65.4 1.4 %collective-permute-start.13 = (f32[32,128]{1,0:T(8,128)S(1)}, f32[32,128]{1,0:T(8,128)S(1)}, u32[]{:S(2)}, u32[]{:S(2)}) collective-permute-start(f32[32,128]{1,0:T(8,128)S(1)} %group_outflow.1), channel_id=1, source_target_pairs={{0,64},{8,72},{16,80},{24,88},{32,96},{40,104},{48,112},{56,120},{... | collective-permute-start | bytes 49160 | tf_op jit(solution)/shard_map/ppermute | solution.py:460
  66.8 1.9 %collective-permute-start.14 = (f32[2,136,128]{2,1,0:T(8,128)S(1)}, f32[2,136,128]{2,1,0:T(8,128)S(1)}, u32[]{:S(2)}, u32[]{:S(2)}) collective-permute-start(f32[2,136,128]{2,1,0:T(8,128)S(1)} %pad_maximum_fusion.6), channel_id=1, source_target_pairs={{0,128},{8,136},{16,144},{24,152},{32,160},{40,168},{48,176},{56,1... | collective-permute-start | bytes 417800 | tf_op jit(solution)/shard_map/ppermute | solution.py:451
  68.7 5.6 %dual2.1.dual1 = f32[2,256,512]{2,1,0:T(8,128)} custom-call(s32[4]{0:T(128)S(1)} %bitcast.31, f32[4]{0:T(128)S(1)} %bitcast.25, bf16[4,256,512]{2,1,0:T(8,128)(2,1)} %get-tuple-element.84.masked, bf16[4,512,512]{2,1,0:T(8,128)(2,1)} %get-tuple-element.74.sort, f32[4,1,512]{2,1,0:T(1,128)S(1)} %bitcast.22, bf16[2048,2048]{1,0:T(8,128)(2,1)} %bitcast.34), custom_call_target="tpu_custom_call" | custom-call | flops 1610612736 | bytes 8388608 | tf_op jit(solution)/shard_map/dual2/pallas_call | solution.py:209
  74.4 2.2 %carried_states.1 = f32[8,32,128]{2,1,0:T(8,128)} custom-call(f32[4,136,128]{2,1,0:T(8,128)S(1)} %pad_maximum_fusion.3.products, f32[8,32,128]{2,1,0:T(8,128)S(1)} %all-to-all-done.1.inflow, bf16[16,128,128]{2,1,0:T(8,128)(2,1)} %get-tuple-element.78.maps, f32[32,128]{1,0:T(8,128)S(1)} %collective-permute-done.11.refs_0_, ...), custom_call_target="tpu_custom_call" | custom-call | flops 25165824 | bytes 1310720 | tf_op jit(solution)/shard_map/carried_states/pallas_call | solution.py:331
  76.6 3.4 %all-to-all-start.2 = ((f32[8,32,128]{2,1,0:T(8,128)}), f32[8,32,128]{2,1,0:T(8,128)S(1)}, u32[]{:S(2)}, u32[]{:S(2)}) async-start(f32[8,32,128]{2,1,0:T(8,128)} %carried_states.1), calls=%async_computation.2 | async-start | bytes 262144 | tf_op jit(solution)/shard_map/all_to_all | solution.py:544
  80.0 1.7 %line_base.1.base = f32[256,256]{1,0:T(8,128)S(1)} custom-call(bf16[8,256,256]{2,1,0:T(8,128)(2,1)S(1)} %pad_maximum_fusion.gathered, bf16[2048,256]{1,0:T(8,128)(2,1)} %bitcast.35), custom_call_target="tpu_custom_call" | custom-call | flops 268435456 | bytes 2097152 | tf_op jit(solution)/shard_map/line_base/pallas_call | solution.py:363
  81.7 4.7 %all-to-all-done.2 = f32[8,32,128]{2,1,0:T(8,128)S(1)} async-done(((f32[8,32,128]{2,1,0:T(8,128)}), f32[8,32,128]{2,1,0:T(8,128)S(1)}, u32[]{:S(2)}, u32[]{:S(2)}) %all-to-all-start.2) | async-done | bytes 131104 | tf_op jit(solution)/shard_map/all_to_all | solution.py:544
  86.5 2.6 %extend.1 = (bf16[256,512]{1,0:T(8,128)(2,1)S(1)}, bf16[256,512]{1,0:T(8,128)(2,1)S(1)}, bf16[256,512]{1,0:T(8,128)(2,1)S(1)}, bf16[256,512]{1,0:T(8,128)(2,1)S(1)}) custom-call(f32[4]{0:T(128)S(1)} %bitcast.26, f32[256,256]{1,0:T(8,128)S(1)} %line_base.1.base, f32[256,128]{1,0:T(8,128)S(1)} %bitcast.19, bf16[128,256]{1,0:T(8,128)(2,1)} %bitcast.36, ...), custom_call_target="tpu_custom_call" | custom-call | flops 268435456 | bytes 4194304 | tf_op jit(solution)/shard_map/extend/pallas_call | solution.py:391
  89.1 4.7 %collective-permute-start.16 = (bf16[256,512]{1,0:T(8,128)(2,1)S(1)}, bf16[256,512]{1,0:T(8,128)(2,1)S(1)}, u32[]{:S(2)}, u32[]{:S(2)}) collective-permute-start(bf16[256,512]{1,0:T(8,128)(2,1)S(1)} %get-tuple-element.92.refs_0_), channel_id=1, source_target_pairs={{0,248},{8,0},{16,8},{24,16},{32,24},{40,32},{48,40},{56,48},{64,5... | collective-permute-start | bytes 786440 | tf_op jit(solution)/shard_map/ppermute | solution.py:460
  94.4 3.6 %collective-permute-start.18 = (bf16[256,512]{1,0:T(8,128)(2,1)S(1)}, bf16[256,512]{1,0:T(8,128)(2,1)S(1)}, u32[]{:S(2)}, u32[]{:S(2)}) collective-permute-start(bf16[256,512]{1,0:T(8,128)(2,1)S(1)} %get-tuple-element.94.refs_2_), channel_id=1, source_target_pairs={{0,7},{1,0},{2,1},{3,2},{4,3},{5,4},{6,5},{7,6},{8,15},{9,8},{10,9... | collective-permute-start | bytes 786440 | tf_op jit(solution)/shard_map/ppermute | solution.py:460
  98.0 1.9 %collective-permute-done.15.refs_4_ = bf16[256,512]{1,0:T(8,128)(2,1)S(1)} collective-permute-done((bf16[256,512]{1,0:T(8,128)(2,1)S(1)}, bf16[256,512]{1,0:T(8,128)(2,1)S(1)}, u32[]{:S(2)}, u32[]{:S(2)}) %collective-permute-start.15) | collective-permute-done | bytes 262176 | tf_op jit(solution)/shard_map/ppermute | solution.py:460
  99.9 6.1 %collective-permute-done.17.refs_6_ = bf16[256,512]{1,0:T(8,128)(2,1)S(1)} collective-permute-done((bf16[256,512]{1,0:T(8,128)(2,1)S(1)}, bf16[256,512]{1,0:T(8,128)(2,1)S(1)}, u32[]{:S(2)}, u32[]{:S(2)}) %collective-permute-start.17) | collective-permute-done | bytes 262176 | tf_op jit(solution)/shard_map/ppermute | solution.py:460
  106.0 3.0 %finish.1 = bf16[4,256,512]{2,1,0:T(8,128)(2,1)} custom-call(s32[4]{0:T(128)S(1)} %bitcast.32, bf16[256,512]{1,0:T(8,128)(2,1)S(1)} %get-tuple-element.92.refs_0_, bf16[256,512]{1,0:T(8,128)(2,1)S(1)} %get-tuple-element.93.refs_1_, bf16[256,512]{1,0:T(8,128)(2,1)S(1)} %get-tuple-element.94.refs_2_, bf16[256,512]{1,0:T(8,128)(2,1)S(1)} %get-tuple-element.95.refs_3_, ...), custom_call_target="tpu_custom_call" | custom-call | flops 536870912 | bytes 5242880 | tf_op jit(solution)/shard_map/finish/pallas_call | solution.py:428
  (44 shorter events, 4.0 us)
Async XLA Ops:
  0.0 20.8 %copy-start.3 = (s32[1,1,4]{2,1,0:T(1,128)S(1)}, s32[1,1,4]{2,1,0:T(1,128)}, u32[]{:S(2)}) copy-start(s32[1,1,4]{2,1,0:T(1,128)} %param.12) | copy-start | bytes 52
  0.0 19.8 %collective-permute-start = (f32[1,128,128]{2,1,0:T(8,128)}, f32[1,128,128]{2,1,0:T(8,128)S(1)}, u32[]{:S(2)}, u32[]{:S(2)}) collective-permute-start(f32[1,128,128]{2,1,0:T(8,128)} %param.20), channel_id=1, source_target_pairs={{0,32},{8,40},{16,48},{24,56},{32,0},{40,8},{48,16},{56,24},{64,96... | collective-permute-start | bytes 196616 | tf_op jit(solution)/shard_map/ppermute | solution.py:451
  9.8 16.3 %collective-permute-start.1 = (bf16[256,512]{1,0:T(8,128)(2,1)S(1)}, bf16[256,512]{1,0:T(8,128)(2,1)S(1)}, u32[]{:S(2)}, u32[]{:S(2)}) collective-permute-start(bf16[256,512]{1,0:T(8,128)(2,1)S(1)} %get-tuple-element.56.refs_1_), channel_id=1, source_target_pairs={{0,8},{8,16},{16,24},{24,32},{32,40},{40,48},{48,56},{56,64},{64,7... | collective-permute-start | bytes 786440 | tf_op jit(solution)/shard_map/ppermute | solution.py:460
  9.9 16.2 %collective-permute-start.2 = (bf16[256,512]{1,0:T(8,128)(2,1)S(1)}, bf16[256,512]{1,0:T(8,128)(2,1)S(1)}, u32[]{:S(2)}, u32[]{:S(2)}) collective-permute-start(bf16[256,512]{1,0:T(8,128)(2,1)S(1)} %get-tuple-element.55.refs_0_), channel_id=1, source_target_pairs={{0,248},{8,0},{16,8},{24,16},{32,24},{40,32},{48,40},{56,48},{64,5... | collective-permute-start | bytes 786440 | tf_op jit(solution)/shard_map/ppermute | solution.py:460
  14.6 15.6 %collective-permute-start.3 = (bf16[256,512]{1,0:T(8,128)(2,1)S(1)}, bf16[256,512]{1,0:T(8,128)(2,1)S(1)}, u32[]{:S(2)}, u32[]{:S(2)}) collective-permute-start(bf16[256,512]{1,0:T(8,128)(2,1)S(1)} %get-tuple-element.58.refs_3_), channel_id=1, source_target_pairs={{0,1},{1,2},{2,3},{3,4},{4,5},{5,6},{6,7},{7,0},{8,9},{9,10},{10,1... | collective-permute-start | bytes 786440 | tf_op jit(solution)/shard_map/ppermute | solution.py:460
  16.2 14.0 %collective-permute-start.4 = (bf16[256,512]{1,0:T(8,128)(2,1)S(1)}, bf16[256,512]{1,0:T(8,128)(2,1)S(1)}, u32[]{:S(2)}, u32[]{:S(2)}) collective-permute-start(bf16[256,512]{1,0:T(8,128)(2,1)S(1)} %get-tuple-element.57.refs_2_), channel_id=1, source_target_pairs={{0,7},{1,0},{2,1},{3,2},{4,3},{5,4},{6,5},{7,6},{8,15},{9,8},{10,9... | collective-permute-start | bytes 786440 | tf_op jit(solution)/shard_map/ppermute | solution.py:460
  19.8 10.4 %copy-start.1 = (bf16[1,2048,128]{2,1,0:T(8,128)(2,1)S(1)}, bf16[1,2048,128]{2,1,0:T(8,128)(2,1)}, u32[]{:S(2)}) copy-start(bf16[1,2048,128]{2,1,0:T(8,128)(2,1)} %param.19) | copy-start | bytes 1572868
  19.8 10.4 %copy-start.2 = (f32[1,1,4]{2,1,0:T(1,128)S(1)}, f32[1,1,4]{2,1,0:T(1,128)}, u32[]{:S(2)}) copy-start(f32[1,1,4]{2,1,0:T(1,128)} %param.14) | copy-start | bytes 52
  20.7 12.7 %collective-permute-start.5 = (f32[2,128,128]{2,1,0:T(8,128)S(1)}, f32[2,128,128]{2,1,0:T(8,128)S(1)}, u32[]{:S(2)}, u32[]{:S(2)}) collective-permute-start(f32[2,128,128]{2,1,0:T(8,128)S(1)} %pad_maximum_fusion.7), channel_id=1, source_target_pairs={{0,16},{8,24},{16,0},{24,8},{32,48},{40,56},{48,32},{56,40},{64,80... | collective-permute-start | bytes 393224 | tf_op jit(solution)/shard_map/ppermute | solution.py:451
  30.2 3.2 %copy-start.4 = (f32[1,128,128]{2,1,0:T(8,128)S(1)}, f32[1,128,128]{2,1,0:T(8,128)}, u32[]{:S(2)}) copy-start(f32[1,128,128]{2,1,0:T(8,128)} %param.20) | copy-start | bytes 196612
  33.5 7.7 %collective-permute-start.6 = (f32[4,128,128]{2,1,0:T(8,128)S(1)}, f32[4,128,128]{2,1,0:T(8,128)S(1)}, u32[]{:S(2)}, u32[]{:S(2)}) collective-permute-start(f32[4,128,128]{2,1,0:T(8,128)S(1)} %pad_maximum_fusion.4), channel_id=1, source_target_pairs={{0,8},{8,0},{16,24},{24,16},{32,40},{40,32},{48,56},{56,48},{64,72... | collective-permute-start | bytes 786440 | tf_op jit(solution)/shard_map/ppermute | solution.py:451
  33.6 7.4 %collective-permute-start.8 = (bf16[1,256,256]{2,1,0:T(8,128)(2,1)S(1)}, bf16[1,256,256]{2,1,0:T(8,128)(2,1)S(1)}, u32[]{:S(2)}, u32[]{:S(2)}) collective-permute-start(bf16[1,256,256]{2,1,0:T(8,128)(2,1)S(1)} %bitcast.16), channel_id=1, source_target_pairs={{0,2},{1,3},{2,0},{3,1},{4,6},{5,7},{6,4},{7,5},{8,10},{9,11},{10,... | collective-permute-start | bytes 393224 | tf_op jit(solution)/shard_map/ppermute | solution.py:451
  33.7 11.4 %all-to-all-start = ((f32[8,32,128]{2,1,0:T(8,128)}), f32[8,32,128]{2,1,0:T(8,128)S(1)}, u32[]{:S(2)}, u32[]{:S(2)}) async-start(f32[8,32,128]{2,1,0:T(8,128)} %bitcast.8), calls=%async_computation | async-start | bytes 262144 | tf_op jit(solution)/shard_map/all_to_all | solution.py:517
  41.0 20.3 %collective-permute-start.9 = (bf16[2,256,256]{2,1,0:T(8,128)(2,1)S(1)}, bf16[2,256,256]{2,1,0:T(8,128)(2,1)S(1)}, u32[]{:S(2)}, u32[]{:S(2)}) collective-permute-start(bf16[2,256,256]{2,1,0:T(8,128)(2,1)S(1)} %pad_maximum_fusion.5), channel_id=1, source_target_pairs={{0,1},{1,0},{2,3},{3,2},{4,5},{5,4},{6,7},{7,6},{8,9},{9,8},{10,11... | collective-permute-start | bytes 786440 | tf_op jit(solution)/shard_map/ppermute | solution.py:451
  45.7 13.5 %all-to-all-start.1 = ((f32[8,32,128]{2,1,0:T(8,128)}), f32[8,32,128]{2,1,0:T(8,128)S(1)}, u32[]{:S(2)}, u32[]{:S(2)}) async-start(f32[8,32,128]{2,1,0:T(8,128)} %shared_sum.1), calls=%async_computation.1 | async-start | bytes 262144 | tf_op jit(solution)/shard_map/all_to_all | solution.py:523
  49.7 6.3 %collective-permute-start.7 = (f32[1,136,128]{2,1,0:T(8,128)S(1)}, f32[1,136,128]{2,1,0:T(8,128)S(1)}, u32[]{:S(2)}, u32[]{:S(2)}) collective-permute-start(f32[1,136,128]{2,1,0:T(8,128)S(1)} %get-tuple-element.72), channel_id=1, source_target_pairs={{0,64},{8,72},{16,80},{24,88},{32,96},{40,104},{48,112},{56,120},{... | collective-permute-start | bytes 208904 | tf_op jit(solution)/shard_map/ppermute | solution.py:451
  61.4 18.5 %collective-permute-start.10 = (bf16[4,256,256]{2,1,0:T(8,128)(2,1)S(1)}, bf16[4,256,256]{2,1,0:T(8,128)(2,1)S(1)}, u32[]{:S(2)}, u32[]{:S(2)}) collective-permute-start(bf16[4,256,256]{2,1,0:T(8,128)(2,1)S(1)} %pad_maximum_fusion.2), channel_id=1, source_target_pairs={{0,4},{1,5},{2,6},{3,7},{4,0},{5,1},{6,2},{7,3},{8,12},{9,13},{10,... | collective-permute-start | bytes 1572872 | tf_op jit(solution)/shard_map/ppermute | solution.py:451
  62.5 11.9 %collective-permute-start.11 = (f32[32,128]{1,0:T(8,128)S(1)}, f32[32,128]{1,0:T(8,128)S(1)}, u32[]{:S(2)}, u32[]{:S(2)}) collective-permute-start(f32[32,128]{1,0:T(8,128)S(1)} %group_outflow.1), channel_id=1, source_target_pairs={{0,192},{8,200},{16,208},{24,216},{32,224},{40,232},{48,240},{56,2... | collective-permute-start | bytes 49160 | tf_op jit(solution)/shard_map/ppermute | solution.py:460
  63.0 11.3 %collective-permute-start.12 = (f32[32,128]{1,0:T(8,128)S(1)}, f32[32,128]{1,0:T(8,128)S(1)}, u32[]{:S(2)}, u32[]{:S(2)}) collective-permute-start(f32[32,128]{1,0:T(8,128)S(1)} %group_outflow.1), channel_id=1, source_target_pairs={{0,128},{8,136},{16,144},{24,152},{32,160},{40,168},{48,176},{56,1... | collective-permute-start | bytes 49160 | tf_op jit(solution)/shard_map/ppermute | solution.py:460
  65.4 8.9 %collective-permute-start.13 = (f32[32,128]{1,0:T(8,128)S(1)}, f32[32,128]{1,0:T(8,128)S(1)}, u32[]{:S(2)}, u32[]{:S(2)}) collective-permute-start(f32[32,128]{1,0:T(8,128)S(1)} %group_outflow.1), channel_id=1, source_target_pairs={{0,64},{8,72},{16,80},{24,88},{32,96},{40,104},{48,112},{56,120},{... | collective-permute-start | bytes 49160 | tf_op jit(solution)/shard_map/ppermute | solution.py:460
  66.8 7.5 %collective-permute-start.14 = (f32[2,136,128]{2,1,0:T(8,128)S(1)}, f32[2,136,128]{2,1,0:T(8,128)S(1)}, u32[]{:S(2)}, u32[]{:S(2)}) collective-permute-start(f32[2,136,128]{2,1,0:T(8,128)S(1)} %pad_maximum_fusion.6), channel_id=1, source_target_pairs={{0,128},{8,136},{16,144},{24,152},{32,160},{40,168},{48,176},{56,1... | collective-permute-start | bytes 417800 | tf_op jit(solution)/shard_map/ppermute | solution.py:451
  76.6 9.9 %all-to-all-start.2 = ((f32[8,32,128]{2,1,0:T(8,128)}), f32[8,32,128]{2,1,0:T(8,128)S(1)}, u32[]{:S(2)}, u32[]{:S(2)}) async-start(f32[8,32,128]{2,1,0:T(8,128)} %carried_states.1), calls=%async_computation.2 | async-start | bytes 262144 | tf_op jit(solution)/shard_map/all_to_all | solution.py:544
  81.7 24.3 %copy-start = (bf16[4,512,512]{2,1,0:T(8,128)(2,1)S(1)}, bf16[4,512,512]{2,1,0:T(8,128)(2,1)}, u32[]{:S(2)}) copy-start(bf16[4,512,512]{2,1,0:T(8,128)(2,1)} %get-tuple-element.96.refs_8_) | copy-start | bytes 6291460
  89.0 10.9 %collective-permute-start.15 = (bf16[256,512]{1,0:T(8,128)(2,1)S(1)}, bf16[256,512]{1,0:T(8,128)(2,1)S(1)}, u32[]{:S(2)}, u32[]{:S(2)}) collective-permute-start(bf16[256,512]{1,0:T(8,128)(2,1)S(1)} %get-tuple-element.93.refs_1_), channel_id=1, source_target_pairs={{0,8},{8,16},{16,24},{24,32},{32,40},{40,48},{48,56},{56,64},{64,7... | collective-permute-start | bytes 786440 | tf_op jit(solution)/shard_map/ppermute | solution.py:460
  89.1 10.8 %collective-permute-start.16 = (bf16[256,512]{1,0:T(8,128)(2,1)S(1)}, bf16[256,512]{1,0:T(8,128)(2,1)S(1)}, u32[]{:S(2)}, u32[]{:S(2)}) collective-permute-start(bf16[256,512]{1,0:T(8,128)(2,1)S(1)} %get-tuple-element.92.refs_0_), channel_id=1, source_target_pairs={{0,248},{8,0},{16,8},{24,16},{32,24},{40,32},{48,40},{56,48},{64,5... | collective-permute-start | bytes 786440 | tf_op jit(solution)/shard_map/ppermute | solution.py:460
  93.9 12.1 %collective-permute-start.17 = (bf16[256,512]{1,0:T(8,128)(2,1)S(1)}, bf16[256,512]{1,0:T(8,128)(2,1)S(1)}, u32[]{:S(2)}, u32[]{:S(2)}) collective-permute-start(bf16[256,512]{1,0:T(8,128)(2,1)S(1)} %get-tuple-element.95.refs_3_), channel_id=1, source_target_pairs={{0,1},{1,2},{2,3},{3,4},{4,5},{5,6},{6,7},{7,0},{8,9},{9,10},{10,1... | collective-permute-start | bytes 786440 | tf_op jit(solution)/shard_map/ppermute | solution.py:460
  94.4 11.6 %collective-permute-start.18 = (bf16[256,512]{1,0:T(8,128)(2,1)S(1)}, bf16[256,512]{1,0:T(8,128)(2,1)S(1)}, u32[]{:S(2)}, u32[]{:S(2)}) collective-permute-start(bf16[256,512]{1,0:T(8,128)(2,1)S(1)} %get-tuple-element.94.refs_2_), channel_id=1, source_target_pairs={{0,7},{1,0},{2,1},{3,2},{4,3},{5,4},{6,5},{7,6},{8,15},{9,8},{10,9... | collective-permute-start | bytes 786440 | tf_op jit(solution)/shard_map/ppermute | solution.py:460
